TPU v7x, 1024 devices: a whole 8x8x8 slice. The times are simulated.
1024 devices in a mesh: dp: 64 (over z, y), tensor: 16 (over x, core).
Axes of the slice: x: 8, y: 8, z: 8, core: 2. Of those that a mesh axis runs over, the one named last changes fastest.
Arguments:
- hidden: bfloat16 [8192, 12288], P('dp', 'tensor'), may hold values from -6 to 6
- cotangent: bfloat16 [8192, 4096], P('dp', 'tensor'), may hold values from -6 to 6
- blocks: bfloat16 [1024, 128, 128], P('tensor'), may hold values from -0.09375 to 0.09375
- block_pos: int32 [16, 64], P('tensor'), may hold values from 0 to 191, as said below
- owner_rank: int32 [16, 64], P('tensor'), may hold values from 0 to 63, each once within a row
- moment: float32 [16, 64, 128, 128], P('tensor', 'dp'), may hold values from -0.009943689 to 0.009943689
- second: float32 [16, 64, 128, 128], P('tensor', 'dp'), may hold values from 3.0517577e-07 to 4.8828124e-06
Outputs:
- mixed: bfloat16 [8192, 4096], P('dp', 'tensor')
- hidden_grad: bfloat16 [8192, 12288], P('dp', 'tensor')
- new_moment: float32 [16, 64, 128, 128], P('tensor', 'dp')
- new_second: float32 [16, 64, 128, 128], P('tensor', 'dp')
- direction: float32 [16, 64, 128, 128], P('tensor', 'dp')
- new_blocks: bfloat16 [1024, 128, 128], P('tensor')
Inputs may be any that keep to these rules, and one draw needn't show every extreme that they name: `block_pos`: each row holds 64 different positions of the 6 x 32 blocks of one slab, in no order. `owner_rank`: the block of rank k has its optimizer state at dp index k.
All inputs are finite; a program needn't handle non-finite values.
Results may differ from a plain program's by a relative error of at most 0.017.
Values may be sent and summed in bfloat16 or wider, within the bound.
No kernel may reach another device: no remote copies, remote signals or barrier semaphores. Data moves between devices by JAX's collectives and lax.ppermute only.
A program may use at most 64 MiB of HBM per device.

v0:
```python
import jax
import jax.numpy as jnp
from jax import lax
from jax.sharding import Mesh
from jax.sharding import PartitionSpec as P

DP = ("dp_0", "dp_1")


def cut_along(value, dim, size):
    before, after = (value.shape[:dim], value.shape[dim + 1 :])
    return jnp.moveaxis(value.reshape(*before, size, -1, *after), dim, 0)


def sent_and_summed(value, axis, dim):
    pieces = cut_along(value, dim, lax.axis_size(axis))
    arrived = lax.all_to_all(pieces, axis, split_axis=0, concat_axis=0, tiled=True)
    return arrived.astype(jnp.float32).sum(axis=0)


def summed_rows(value, axes, dim):
    for axis in axes:
        value = lax.psum_scatter(value, axis, scatter_dimension=dim, tiled=True)
    return value


def joined_along(pieces, dim):
    dims = list(pieces.shape[1:])
    dims[dim] *= pieces.shape[0]
    return jnp.moveaxis(pieces, 0, dim).reshape(dims)


def gather_in_order(value, axes, order):
    pieces = value
    for k in order:
        pieces = lax.all_gather(pieces, axes[k])
    done = order[::-1]
    back = [done.index(k) for k in range(len(axes))]
    pieces = pieces.transpose(*back, *range(len(axes), pieces.ndim))
    return pieces.reshape(-1, *value.shape)


def whole_of(value, axes, order, dim):
    return joined_along(gather_in_order(value, axes, order), dim)


def shards(hidden, cotangent, blocks, block_pos, owner_rank, moment, second):
    token_count = hidden.shape[0]
    slot_count = blocks.shape[0]
    block_size = blocks.shape[1]
    row_blocks = hidden.shape[1] // block_size
    width = cotangent.shape[1] * lax.axis_size("tensor")
    col_blocks = width // block_size
    total_tokens = token_count * lax.axis_size(DP)
    owned = slot_count // lax.axis_size(DP)
    highest = lax.Precision.HIGHEST
    positions = block_pos[0]
    ranks = owner_rank[0]
    block_rows = positions // col_blocks
    block_cols = positions % col_blocks
    chosen_hid = jnp.take(hidden.reshape(token_count, row_blocks, block_size), block_rows, axis=1)
    col_hot = (block_cols[:, None] == jnp.arange(col_blocks)[None, :]).astype(jnp.float32)
    row_hot = (block_rows[:, None] == jnp.arange(row_blocks)[None, :]).astype(jnp.float32)
    contrib = jnp.einsum("nsa,sab->nsb", chosen_hid, blocks, preferred_element_type=jnp.float32)
    partial_value = jnp.einsum("nsb,sc->ncb", contrib, col_hot, precision=highest).reshape(
        token_count, width
    )
    mixed = sent_and_summed(partial_value.astype(jnp.bfloat16), "tensor", 1).astype(jnp.bfloat16)
    full_grad = lax.all_gather(cotangent, "tensor", axis=1, tiled=True)
    chosen_grad = jnp.take(
        full_grad.reshape(token_count, col_blocks, block_size), block_cols, axis=1
    )
    back = jnp.einsum("nsb,sab->nsa", chosen_grad, blocks, preferred_element_type=jnp.float32)
    hidden_grad = (
        jnp.einsum("nsa,sr->nra", back, row_hot, precision=highest)
        .reshape(token_count, row_blocks * block_size)
        .astype(jnp.bfloat16)
    )
    order = jnp.argsort(ranks)
    factor = 1.0 / total_tokens
    grads = (
        jnp.einsum("nsa,nsb->sab", chosen_hid, chosen_grad, preferred_element_type=jnp.float32)
        * factor
    )
    grads = jnp.take(grads, order, axis=0)
    mine = summed_rows(grads, DP, 0)
    owner_index = lax.axis_index(DP)
    mine_slots = lax.dynamic_slice_in_dim(order, owner_index * owned, owned)
    weights_own = jnp.take(blocks, mine_slots, axis=0).astype(jnp.float32)
    mom_next = 0.9 * moment[0] + 0.1 * mine
    sec_next = 0.999 * second[0] + 0.001 * mine * mine
    step_dir = mom_next / (jnp.sqrt(sec_next) + 1e-08)
    updated = (weights_own - 0.002 * (step_dir + 0.1 * weights_own)).astype(jnp.bfloat16)
    returned = whole_of(updated, DP, (0, 1), 0)
    new_blocks = jnp.take(returned, ranks, axis=0)
    return (mixed, hidden_grad, mom_next[None], sec_next[None], step_dir[None], new_blocks)


def solution(mesh):
    torus = Mesh(mesh.devices.reshape(8, 8, mesh.shape["tensor"]), ("dp_0", "dp_1", "tensor"))
    placed = (
        P(DP, "tensor"),
        P(DP, "tensor"),
        P("tensor", None, None),
        P("tensor", None),
        P("tensor", None),
        P("tensor", DP, None, None),
        P("tensor", DP, None, None),
    )
    return jax.shard_map(
        shards,
        mesh=torus,
        in_specs=placed,
        out_specs=(
            P(DP, "tensor"),
            P(DP, "tensor"),
            P("tensor", DP, None, None),
            P("tensor", DP, None, None),
            P("tensor", DP, None, None),
            P("tensor", None, None),
        ),
        check_vma=False,
    )
```

profile of v0, /device:TPU:1, one launch (start us, length us, event | category | flops | bytes accessed | tf_op | source)
XLA Modules:
  0.0 280.8 jit_solution(7368413724525849154)
XLA Ops:
  7.2 0.0 all-gather.5.cloned.1.call-start
  7.2 1.6 copy.44
  8.8 0.0 all-gather.5.cloned.1.call-update
  8.8 0.0 reduce-scatter.3.cloned.1.call-start
  8.9 1.1 copy.40
  9.9 0.2 copy.41
  10.1 0.7 fusion.33
  10.8 0.0 copy-start.4
  10.8 0.0 copy-start.3
  10.8 1.0 gather_fusion
  11.8 0.0 copy-done.4
  11.8 2.0 sort.17
  13.9 0.0 copy-done.3
  13.9 53.1 %all-gather.5.cloned.1.call-done = bf16[128,4096]{0,1:T(8,128)(2,1)} async-done(((bf16[128,256]{0,1:T(8,128)(2,1)}), bf16[128,4096]{0,1:T(8,128)(2,1)}) %all-gather.5.cloned.1.call-update) | async-done | bytes 1048592 | tf_op jit(solution)/shard_map/all_gather | solution.py:69
  67.0 1.6 copy.45
  68.7 2.1 gather_fusion.1
  70.8 4.5 %convolution_multiply_fusion = f32[64,128,128]{2,1,0:T(8,128)} fusion(bf16[64,128,128]{2,1,0:T(8,128)(2,1)S(1)} %gather_fusion, pred[64]{0:T(512)(128)(4,1)S(1)} %get-tuple-element.53, bf16[64,128,128]{2,1,0:T(8,128)(2,1)} %gather_fusion.1, pred[64]{0:T(512)(128)(4,1)S(1)} %get-tuple-element.45), kind=kOutput, calls=%fused_computation.8 | convolution fusion | flops 271581184 | bytes 8388736 | tf_op jit(solution)/shard_map/nsa,nsb->sab/dot_general | solution.py:82
  75.3 5.0 %gather_fusion.2 = f32[64,128,128]{2,1,0:T(8,128)} fusion(f32[64,128,128]{2,1,0:T(8,128)} %convolution_multiply_fusion, s32[1024]{0:T(1024)S(1)} %pad_clamp_fusion.1), kind=kCustom, calls=%fused_computation.2 | custom fusion | bytes 8388864 | tf_op jit(solution)/shard_map/jit(_take)/gather | solution.py:85
  80.3 4.5 %broadcast_select_fusion = f32[64,128,128]{2,1,0:T(8,128)} fusion(f32[64,128,128]{2,1,0:T(8,128)} %gather_fusion.2, pred[64]{0:T(512)(128)(4,1)S(1)} %compare_and_fusion.1), kind=kLoop, calls=%fused_computation.15 | loop fusion | flops 1048576 | bytes 8388672 | tf_op jit(solution)/shard_map/jit(_take)/select_n | solution.py:85
  84.8 0.0 copy-start.1
  84.8 0.0 reduce-scatter.3.cloned.1.call-update
  84.8 0.0 reduce-scatter.5.cloned.1.call-start
  84.9 62.2 %reduce-scatter.3.cloned.1.call-done = f32[8,128,128]{2,1,0:T(8,128)} async-done(((f32[64,128,128]{2,1,0:T(8,128)}), f32[8,128,128]{2,1,0:T(8,128)}) %reduce-scatter.3.cloned.1.call-update) | async-done | bytes 524304 | tf_op jit(solution)/shard_map/reduce_scatter | solution.py:23
  147.1 0.0 reduce-scatter.5.cloned.1.call-update
  147.1 0.0 all-gather.7.cloned.1.call-start
  147.2 0.6 dynamic_slice.3
  149.7 36.1 %reduce-scatter.5.cloned.1.call-done = f32[1,128,128]{2,1,0:T(8,128)} async-done(((f32[8,128,128]{2,1,0:T(8,128)}), f32[1,128,128]{2,1,0:T(8,128)}) %reduce-scatter.5.cloned.1.call-update) | async-done | bytes 65552 | tf_op jit(solution)/shard_map/reduce_scatter | solution.py:23
  185.8 0.0 copy-done.1
  185.8 0.0 copy-done.2
  185.8 1.6 fusion.22
  187.4 24.0 %all-gather = bf16[8,128,128]{2,1,0:T(8,128)(2,1)} all-gather(bf16[1,128,128]{2,1,0:T(8,128)(2,1)S(1)} %get-tuple-element.43), channel_id=2, replica_groups=mesh['dp_0'=8,'dp_1'=8,'tensor'=16] {'dp_0'}, dimensions={0}, use_global_device_ids=true | all-gather | bytes 294912 | tf_op jit(solution)/shard_map/all_gather | solution.py:36
  211.4 0.0 all-gather.7.cloned.1.call-update
  211.4 2.3 convolution_bitcast_fusion.1
  213.8 4.1 %fusion.11 = bf16[128,32,128]{2,1,0:T(8,128)(2,1)S(1)} fusion(f32[128,64,128]{2,0,1:T(8,128)S(1)} %convolution_bitcast_fusion.1, s32[64]{0:T(128)S(1)} %get-tuple-element.46), kind=kOutput, calls=%fused_computation.20 | convolution fusion | flops 403179520 | bytes 5243136 | tf_op jit(solution)/shard_map/nsb,sc->ncb/dot_general | solution.py:65
  217.8 0.4 convert_element_type.43
  218.2 0.0 copy-start
  218.2 1.3 copy.65
  219.6 18.6 %all-to-all-start = ((bf16[16,128,256]{2,1,0:T(8,128)(2,1)}), bf16[16,128,256]{2,1,0:T(8,128)(2,1)S(1)}, u32[]{:S(2)}, u32[]{:S(2)}) async-start(bf16[16,128,256]{2,1,0:T(8,128)(2,1)} %bitcast.102), calls=%async_computation | async-start | bytes 2097152 | tf_op jit(solution)/shard_map/all_to_all | solution.py:17
  238.2 0.0 copy-done
  238.3 3.2 %convolution_bitcast_fusion = f32[128,64,128]{2,0,1:T(8,128)S(1)} fusion(bf16[64,128,128]{2,1,0:T(8,128)(2,1)} %param.9, bf16[64,128,128]{2,1,0:T(8,128)(2,1)S(1)} %copy-done, pred[64]{0:T(512)(128)(4,1)S(1)} %get-tuple-element.45), kind=kOutput, calls=%fused_computation.9 | convolution fusion | flops 269484032 | bytes 8388672 | tf_op jit(solution)/shard_map/nsb,sab->nsa/dot_general | solution.py:73
  241.5 3.8 %fusion.17 = bf16[128,6,128]{2,1,0:T(8,128)(2,1)S(1)} fusion(f32[128,64,128]{2,0,1:T(8,128)S(1)} %convolution_bitcast_fusion, s32[64]{0:T(128)S(1)} %get-tuple-element.54), kind=kOutput, calls=%fused_computation.22 | convolution fusion | flops 75596160 | bytes 4391168 | tf_op jit(solution)/shard_map/nsa,sr->nra/dot_general | solution.py:75
  245.3 0.2 copy.47
  245.5 0.8 copy.50
  246.3 19.9 %all-to-all-done = bf16[16,128,256]{2,1,0:T(8,128)(2,1)S(1)} async-done(((bf16[16,128,256]{2,1,0:T(8,128)(2,1)}), bf16[16,128,256]{2,1,0:T(8,128)(2,1)S(1)}, u32[]{:S(2)}, u32[]{:S(2)}) %all-to-all-start) | async-done | bytes 1048608 | tf_op jit(solution)/shard_map/all_to_all | solution.py:17
  266.2 0.8 reduce_sum.12
  267.0 3.2 %copy.49 = bf16[8,8,1,128,128]{4,3,1,0,2:T(8,128)(2,1)} copy(bf16[8,8,1,128,128]{4,3,0,1,2:T(8,128)(2,1)} %bitcast.103) | data formatting | bytes 4194304 | tf_op jit(solution)/shard_map/transpose | solution.py:39
  270.1 2.5 gather_fusion.3
  272.7 1.6 broadcast_select_fusion.3
  (11 shorter events, 0.1 us)
Async XLA Ops:
  7.2 59.9 %all-gather.5.cloned.1.call-start = ((), (), s32[]{:S(2)}) async-start(), calls=%async_computation.3 | async-start | bytes 1114112 | tf_op jit(solution)/shard_map/all_gather | solution.py:69
  8.8 138.3 %reduce-scatter.3.cloned.1.call-start = ((), (), s32[]{:S(2)}) async-start(), calls=%async_computation.4 | async-start | bytes 4718592 | tf_op jit(solution)/shard_map/reduce_scatter | solution.py:23
  10.8 1.0 copy-start.4
  10.8 3.1 %copy-start.3 = (s32[1,64]{1,0:T(1,128)S(1)}, s32[1,64]{1,0:T(1,128)}, u32[]{:S(2)}) copy-start(s32[1,64]{1,0:T(1,128)} %param.10) | copy-start | bytes 772
  84.8 101.0 %copy-start.1 = (f32[1,1,128,128]{3,2,1,0:T(8,128)S(1)}, f32[1,1,128,128]{3,2,1,0:T(8,128)}, u32[]{:S(2)}) copy-start(f32[1,1,128,128]{3,2,1,0:T(8,128)} %param.13) | copy-start | bytes 196612
  84.8 101.0 %copy-start.2 = (f32[1,1,128,128]{3,2,1,0:T(8,128)S(1)}, f32[1,1,128,128]{3,2,1,0:T(8,128)}, u32[]{:S(2)}) copy-start(f32[1,1,128,128]{3,2,1,0:T(8,128)} %param.12) | copy-start | bytes 196612
  84.8 101.0 %reduce-scatter.5.cloned.1.call-start = ((), (), s32[]{:S(2)}) async-start(), calls=%async_computation.5 | async-start | bytes 589824 | tf_op jit(solution)/shard_map/reduce_scatter | solution.py:23
  147.1 119.8 %all-gather.7.cloned.1.call-start = ((), (), s32[]{:S(2)}) async-start(), calls=%async_computation.6 | async-start | bytes 2359296 | tf_op jit(solution)/shard_map/all_gather | solution.py:36
  218.2 20.0 %copy-start = (bf16[64,128,128]{2,1,0:T(8,128)(2,1)S(1)}, bf16[64,128,128]{2,1,0:T(8,128)(2,1)}, u32[]{:S(2)}) copy-start(bf16[64,128,128]{2,1,0:T(8,128)(2,1)} %gather_fusion.1) | copy-start | bytes 6291460
  219.6 46.6 %all-to-all-start = ((bf16[16,128,256]{2,1,0:T(8,128)(2,1)}), bf16[16,128,256]{2,1,0:T(8,128)(2,1)S(1)}, u32[]{:S(2)}, u32[]{:S(2)}) async-start(bf16[16,128,256]{2,1,0:T(8,128)(2,1)} %bitcast.102), calls=%async_computation | async-start | bytes 2097152 | tf_op jit(solution)/shard_map/all_to_all | solution.py:17
Sparse Core Ops, SparseCore 0:
  11.2 55.7 all-gather.4
  85.0 62.1 reduce-scatter.2
  150.5 35.2 reduce-scatter.4
  211.5 49.4 all-gather.6
where the time goes:
time: 281 us
  waiting for transfers between devices  171 us (61%)
  blocking collectives  24 us (9%)
  local copies, waits for them, and re-layouts  21.6 us (8%)
  starting transfers between devices  18.8 us (7%)
  matrix products  18 us (6%)
  between operations  15.9 us (6%)
  other arithmetic  11.2 us (4%)
    reduce_scatter x2, waiting for transfers between devices, summed_rows(): value = lax.psum_scatter(value, axis, scatter_dimension=dim, tiled=True)  98.3 us
    all_gather x1, waiting for transfers between devices, shards(): full_grad = lax.all_gather(cotangent, 'tensor', axis=1, tiled=True)  53.1 us
    all_gather x1, blocking collectives, gather_in_order(): pieces = lax.all_gather(pieces, axes[k])  24 us
    all_to_all x1, waiting for transfers between devices, sent_and_summed(): lax.all_to_all(pieces, axis, split_axis=0, concat_axis=0, tiled=True)  19.9 us
    all_to_all x1, starting transfers between devices, sent_and_summed(): lax.all_to_all(pieces, axis, split_axis=0, concat_axis=0, tiled=True)  18.6 us
  transfers between devices with their start and end apart: 5, of which 4 were waited for; matrix products, arithmetic and copies ran while one was open for 8% of the time, Pallas kernels for 0%

commit v1 on v0

v1 whole, which is shorter than its diff:
```python
import functools

import jax
import jax.numpy as jnp
from jax import lax
from jax.experimental import pallas as pl
from jax.experimental.pallas import tpu as pltpu
from jax.sharding import Mesh
from jax.sharding import PartitionSpec as P

DP = ("dp_0", "dp_1")
TENSOR = ("x", "core")
VMEM = pl.BlockSpec(memory_space=pltpu.VMEM)
SMEM = pl.BlockSpec(memory_space=pltpu.SMEM)
BF = jnp.bfloat16
F32 = jnp.float32


def call(kernel, out_shape, n_smem, n_vmem, scratch=(), flops=0, nbytes=0):
    n_out = len(jax.tree.leaves(out_shape))
    return pl.pallas_call(
        kernel,
        out_shape=out_shape,
        in_specs=[SMEM] * n_smem + [VMEM] * n_vmem,
        out_specs=VMEM if n_out == 1 else [VMEM] * n_out,
        scratch_shapes=list(scratch),
        cost_estimate=pl.CostEstimate(flops=flops, bytes_accessed=nbytes, transcendentals=0),
    )


def aligned(index, size):
    return pl.ds(pl.multiple_of(index * size, size), size)


def fill_slab(pos_ref, blocks_ref, slab):
    slots, bs, _ = blocks_ref.shape
    rows, width = slab.shape
    col_blocks = width // bs

    def clear(i, carry):
        slab[aligned(i, 16), :] = jnp.zeros((16, width), BF)
        return carry

    lax.fori_loop(0, rows // 16, clear, 0, unroll=2)

    def place(s, carry):
        p = pos_ref[0, s]
        slab[aligned(p // col_blocks, bs), aligned(p % col_blocks, bs)] = blocks_ref[s]
        return carry

    lax.fori_loop(0, slots, place, 0, unroll=4)


def partial_kernel(core_ref, pos_ref, hid_ref, blocks_ref, out_ref, slab):
    feats = out_ref.shape[-1]
    fill_slab(pos_ref, blocks_ref, slab)
    hid = hid_ref[...]

    def step(t, carry):
        value = jnp.dot(hid, slab[:, aligned(t, feats)], preferred_element_type=F32)
        out_ref[(t % 2) ^ core_ref[0], t // 2] = value.astype(BF)
        return carry

    lax.fori_loop(0, slab.shape[1] // feats, step, 0, unroll=2)


def join_features(core_ref, own_ref, other_ref, full):
    pieces, _, feats = own_ref.shape
    core = core_ref[0]
    for j in range(pieces):
        full[:, aligned(2 * j + core, feats)] = own_ref[j]
        full[:, aligned(2 * j + 1 - core, feats)] = other_ref[j]


def place_of(rank, core, side):
    return jnp.where(core == 0, rank, (rank % side) * side + rank // side)


def grads_kernel(side, factor, core_ref, pos_ref, rank_ref, hid_ref, own_ref, other_ref, out_ref, full, hid_t):
    slots, bs, _ = out_ref.shape
    col_blocks = full.shape[1] // bs
    core = core_ref[0]
    join_features(core_ref, own_ref, other_ref, full)
    hid_t[...] = hid_ref[...].T

    def step(s, carry):
        p = pos_ref[0, s]
        value = jnp.dot(
            hid_t[aligned(p // col_blocks, bs), :],
            full[:, aligned(p % col_blocks, bs)],
            preferred_element_type=F32,
        )
        out_ref[place_of(rank_ref[0, s], core, side)] = (value * factor).astype(BF)
        return carry

    lax.fori_loop(0, slots, step, 0, unroll=8)


def back_kernel(core_ref, owner_ref, pos_ref, rank_ref, own_ref, other_ref, blocks_ref, out_ref, mine_ref, full, slab):
    slots, bs, _ = blocks_ref.shape
    join_features(core_ref, own_ref, other_ref, full)
    fill_slab(pos_ref, blocks_ref, slab)

    def find(s, found):
        return jnp.where(rank_ref[0, s] == owner_ref[0], s, found)

    mine_ref[...] = blocks_ref[lax.fori_loop(0, slots, find, 0)]
    value = full[...]
    step = 2 * bs
    for n in range(slab.shape[0] // step):
        rows = slab[n * step : (n + 1) * step, :]
        out_ref[:, n * step : (n + 1) * step] = lax.dot_general(
            value, rows, (((1,), (1,)), ((), ())), preferred_element_type=F32
        ).astype(BF)


def list_kernel(side, core_ref, rank_ref, in_ref, out_ref):
    core = core_ref[0]

    def step(s, carry):
        out_ref[s] = in_ref[place_of(rank_ref[0, s], core, side)]
        return carry

    lax.fori_loop(0, out_ref.shape[0], step, 0, unroll=4)


def chip_groups(sizes):
    n0, n1, nx, nc = sizes

    def at(z, y, x, c):
        return ((z * n1 + y) * nx + x) * nc + c

    along_0 = lambda c: [[at(z, y, x, c) for z in range(n0)] for y in range(n1) for x in range(nx)]
    along_1 = lambda c: [[at(z, y, x, c) for y in range(n1)] for z in range(n0) for x in range(nx)]
    return along_0(0) + along_1(1), along_1(0) + along_0(1)


def shards(sizes, hidden, cotangent, blocks, block_pos, owner_rank, moment, second):
    tokens, feats = cotangent.shape
    rows = hidden.shape[1]
    slots, bs, _ = blocks.shape
    n0, n1, nx, nc = sizes
    width = feats * nx * nc
    axes = (*DP, *TENSOR)
    first, then = chip_groups(sizes)
    core = lax.axis_index("core").reshape(1)
    owner = lax.axis_index(DP).reshape(1)
    swap = [(0, 1), (1, 0)]
    factor = 1.0 / (tokens * n0 * n1)

    def exchange(value, groups):
        return lax.all_to_all(value, axes, 0, 0, axis_index_groups=groups, tiled=True)

    partials = call(
        partial_kernel,
        jax.ShapeDtypeStruct((nc, nx, tokens, feats), BF),
        2,
        2,
        [pltpu.VMEM((rows, width), BF)],
        flops=2 * tokens * rows * width,
        nbytes=4 * 2**20,
    )(core, block_pos, hidden, blocks)
    theirs = lax.ppermute(partials[1], "core", swap)
    pair = (partials[0].astype(F32) + theirs.astype(F32)).astype(BF)
    sent = jnp.concatenate([jnp.broadcast_to(cotangent, pair.shape), pair], axis=1)
    came = lax.all_to_all(sent, "x", 0, 0, tiled=True)
    mixed = came[:, tokens:].astype(F32).sum(axis=0).astype(BF)
    own = came[:, :tokens]
    other = lax.ppermute(own, "core", swap)

    grads = call(
        functools.partial(grads_kernel, n0, factor),
        jax.ShapeDtypeStruct((slots, bs, bs), BF),
        3,
        3,
        [pltpu.VMEM((tokens, width), BF), pltpu.VMEM((rows, tokens), BF)],
        flops=2 * tokens * bs * bs * slots,
        nbytes=4 * 2**20,
    )(core, block_pos, owner_rank, hidden, own, other)
    hidden_grad, mine = call(
        back_kernel,
        (jax.ShapeDtypeStruct((tokens, rows), BF), jax.ShapeDtypeStruct((bs, bs), BF)),
        4,
        3,
        [pltpu.VMEM((tokens, width), BF), pltpu.VMEM((rows, width), BF)],
        flops=2 * tokens * rows * width,
        nbytes=4 * 2**20,
    )(core, owner, block_pos, owner_rank, own, other, blocks)

    got = exchange(grads.reshape(n0, slots // n0, bs, bs), first)
    part = got.astype(F32).sum(axis=0).astype(BF)
    grad = exchange(part, then).astype(F32).sum(axis=0)
    weight = mine.astype(F32)
    mom_next = 0.9 * moment[0, 0] + 0.1 * grad
    sec_next = 0.999 * second[0, 0] + 0.001 * grad * grad
    step_dir = mom_next / (jnp.sqrt(sec_next) + 1e-08)
    updated = (weight - 0.002 * (step_dir + 0.1 * weight)).astype(BF)
    row = exchange(jnp.broadcast_to(updated, (n1, bs, bs)), then)
    every = exchange(jnp.broadcast_to(row, (n0, n1, bs, bs)), first)
    new_blocks = call(
        functools.partial(list_kernel, n0),
        jax.ShapeDtypeStruct((slots, bs, bs), BF),
        2,
        1,
        nbytes=4 * 2**20,
    )(core, owner_rank, every.reshape(slots, bs, bs))
    return (mixed, hidden_grad, mom_next[None, None], sec_next[None, None], step_dir[None, None], new_blocks)


def make(sizes, torus):
    placed = (
        P(DP, TENSOR),
        P(DP, TENSOR),
        P(TENSOR, None, None),
        P(TENSOR, None),
        P(TENSOR, None),
        P(TENSOR, DP, None, None),
        P(TENSOR, DP, None, None),
    )
    return jax.shard_map(
        functools.partial(shards, sizes),
        mesh=torus,
        in_specs=placed,
        out_specs=(
            P(DP, TENSOR),
            P(DP, TENSOR),
            P(TENSOR, DP, None, None),
            P(TENSOR, DP, None, None),
            P(TENSOR, DP, None, None),
            P(TENSOR, None, None),
        ),
        check_vma=False,
    )


def solution(mesh):
    sizes = (8, mesh.shape["dp"] // 8, mesh.shape["tensor"] // 2, 2)
    return make(sizes, Mesh(mesh.devices.reshape(sizes), (*DP, *TENSOR)))
```

time: 281 us -> 180 us (0.64)
  the two profiles are of different devices: /device:TPU:1 before, /device:TPU:2 now
where the time goes in v1:
time: 180 us; the launch traced here: 179 us
  blocking collectives  95.3 us (53%)
  waiting for transfers between devices  36.9 us (20%)
  Pallas kernels  21.2 us (12%)
  starting transfers between devices  15.1 us (8%)
  local copies, waits for them, and re-layouts  5.17 us (3%)
  other arithmetic  4.59 us (3%)
    all_to_all x2, blocking collectives, exchange(): lax.all_to_all(value, axes, 0, 0, axis_index_groups=groups, tiled=True)  51.9 us
    all_to_all x1, blocking collectives, shards(): came = lax.all_to_all(sent, 'x', 0, 0, tiled=True)  43.4 us
    all_to_all x2, waiting for transfers between devices, exchange(): lax.all_to_all(value, axes, 0, 0, axis_index_groups=groups, tiled=True)  33.2 us
    all_to_all x2, starting transfers between devices, exchange(): lax.all_to_all(value, axes, 0, 0, axis_index_groups=groups, tiled=True)  11.3 us
    pallas_call x1, Pallas kernels, shards(): call(back_kernel, (jax.ShapeDtypeStruct((tokens, rows), BF), jax.ShapeDty...  6.81 us
    pallas_call x1, Pallas kernels, shards(): call(partial_kernel, jax.ShapeDtypeStruct((nc, nx, tokens, feats), BF), 2...  6.2 us
    pallas_call x1, Pallas kernels, shards(): call(functools.partial(grads_kernel, n0, factor), jax.ShapeDtypeStruct((s...  4.67 us
  transfers between devices with their start and end apart: 4, of which 4 were waited for; matrix products, arithmetic and copies ran while one was open for 0% of the time, Pallas kernels for 4%

profile of v1, /device:TPU:2, one launch (start us, length us, event | category | flops | bytes accessed | tf_op | source)
XLA Modules:
  0.0 179.0 jit_solution(835817053545898067)
XLA Ops:
  0.6 6.2 %shard_map.118 = bf16[2,8,128,256]{3,2,1,0:T(8,128)(2,1)} custom-call(s32[1]{0:T(128)} %bitcast.core_ref, s32[1,64]{1,0:T(1,128)} %pos_ref.5, bf16[128,768]{1,0:T(8,128)(2,1)} %hid_ref.3, bf16[64,128,128]{2,1,0:T(8,128)(2,1)} %blocks_ref.3), custom_call_target="tpu_custom_call" | custom-call | flops 805306368 | bytes 4194304 | tf_op jit(solution)/shard_map/pallas_call | solution.py:154
  6.8 0.0 copy-start.5
  6.8 1.1 slice_bitcast_fusion
  8.0 1.9 %collective-permute-start = (bf16[8,128,256]{2,1,0:T(8,128)(2,1)S(1)}, bf16[8,128,256]{2,1,0:T(8,128)(2,1)S(1)}, u32[]{:S(2)}, u32[]{:S(2)}) collective-permute-start(bf16[8,128,256]{2,1,0:T(8,128)(2,1)S(1)} %slice_bitcast_fusion), channel_id=1, source_target_pairs={{0,1},{1,0},{2,3},{3,2},{4,5},{5,4},{6,7},{7,6},{8,9},{9,8},{10,11... | collective-permute-start | bytes 1572872 | tf_op jit(solution)/shard_map/ppermute | solution.py:163
  9.9 1.9 %collective-permute-done = bf16[8,128,256]{2,1,0:T(8,128)(2,1)S(1)} collective-permute-done((bf16[8,128,256]{2,1,0:T(8,128)(2,1)S(1)}, bf16[8,128,256]{2,1,0:T(8,128)(2,1)S(1)}, u32[]{:S(2)}, u32[]{:S(2)}) %collective-permute-start) | collective-permute-done | bytes 524320 | tf_op jit(solution)/shard_map/ppermute | solution.py:163
  11.8 1.2 fusion
  12.9 0.0 copy-done.5
  13.0 0.1 pad_maximum_fusion
  13.1 43.4 %all_to_all.25 = bf16[8,256,256]{2,1,0:T(8,128)(2,1)S(1)} all-to-all(bf16[8,256,256]{2,1,0:T(8,128)(2,1)S(1)} %pad_maximum_fusion), channel_id=1, replica_groups=mesh['dp_0'=8,'dp_1'=8,'x'=8,'core'=2] {'x'}, dimensions={0} | all-to-all | bytes 2097152 | tf_op jit(solution)/shard_map/all_to_all | solution.py:166
  56.5 0.7 fusion.12
  57.2 0.0 copy-start.1
  57.2 1.9 %collective-permute-start.1 = (bf16[8,128,256]{2,1,0:T(8,128)(2,1)S(1)}, bf16[8,128,256]{2,1,0:T(8,128)(2,1)S(1)}, u32[]{:S(2)}, u32[]{:S(2)}) collective-permute-start(bf16[8,128,256]{2,1,0:T(8,128)(2,1)S(1)} %get-tuple-element.13.own_ref), channel_id=1, source_target_pairs={{0,1},{1,0},{2,3},{3,2},{4,5},{5,4},{6,7},{7,6},{8,9},{9,8},{10,11... | collective-permute-start | bytes 1572872 | tf_op jit(solution)/shard_map/ppermute | solution.py:169
  59.1 1.9 %collective-permute-done.1.other_ref = bf16[8,128,256]{2,1,0:T(8,128)(2,1)S(1)} collective-permute-done((bf16[8,128,256]{2,1,0:T(8,128)(2,1)S(1)}, bf16[8,128,256]{2,1,0:T(8,128)(2,1)S(1)}, u32[]{:S(2)}, u32[]{:S(2)}) %collective-permute-start.1) | collective-permute-done | bytes 524320 | tf_op jit(solution)/shard_map/ppermute | solution.py:169
  61.0 0.0 copy-done.1
  61.0 0.0 copy-start.2
  61.0 0.8 copy-done.2
  61.8 4.7 %shard_map.120 = bf16[64,128,128]{2,1,0:T(8,128)(2,1)} custom-call(s32[1]{0:T(128)} %bitcast.core_ref, s32[1,64]{1,0:T(1,128)} %pos_ref.5, s32[1,64]{1,0:T(1,128)} %rank_ref.5, bf16[128,768]{1,0:T(8,128)(2,1)} %hid_ref.3, bf16[8,128,256]{2,1,0:T(8,128)(2,1)} %copy-done.1, bf16[8,128,256]{2,1,0:T(8,128)(2,1)} %copy-done.2), custom_call_target="tpu_custom_call" | custom-call | flops 268435456 | bytes 4194304 | tf_op jit(solution)/shard_map/pallas_call | solution.py:171
  66.4 38.1 %all_to_all.26 = bf16[8,8,128,128]{3,2,1,0:T(8,128)(2,1)S(1)} all-to-all(bf16[8,8,128,128]{3,2,1,0:T(8,128)(2,1)} %bitcast.25), channel_id=1, replica_groups={{0,128,256,384,512,640,768,896},{2,130,258,386,514,642,770,898},{4,132,..., dimensions={0} | all-to-all | bytes 4194304 | tf_op jit(solution)/shard_map/all_to_all | solution.py:152
  104.5 1.1 reduce_sum.36
  105.6 0.0 copy-start.3
  105.6 0.0 copy-start.4
  105.6 7.7 %all-to-all-start.2 = ((bf16[8,128,128]{2,1,0:T(8,128)(2,1)}), bf16[8,128,128]{2,1,0:T(8,128)(2,1)S(1)}, u32[]{:S(2)}, u32[]{:S(2)}) async-start(bf16[8,128,128]{2,1,0:T(8,128)(2,1)} %reduce_sum.36), calls=%async_computation.2 | async-start | bytes 524288 | tf_op jit(solution)/shard_map/all_to_all | solution.py:152
  113.3 6.8 %shard_map.119 = (bf16[128,768]{1,0:T(8,128)(2,1)}, bf16[128,128]{1,0:T(8,128)(2,1)}) custom-call(s32[1]{0:T(128)} %bitcast.core_ref, s32[1]{0:T(128)} %bitcast.3.owner_ref, s32[1,64]{1,0:T(1,128)} %pos_ref.5, s32[1,64]{1,0:T(1,128)} %rank_ref.5, bf16[8,128,256]{2,1,0:T(8,128)(2,1)} %copy-done.1, bf16[8,128,256]{2,1,0:T(8,128)(2,1)} %copy-done.2, ...), custom_call_target="tpu_custom_call" | custom-call | flops 805306368 | bytes 4194304 | tf_op jit(solution)/shard_map/pallas_call | solution.py:180
  120.1 3.7 %all-to-all-done.2 = bf16[8,128,128]{2,1,0:T(8,128)(2,1)S(1)} async-done(((bf16[8,128,128]{2,1,0:T(8,128)(2,1)}), bf16[8,128,128]{2,1,0:T(8,128)(2,1)S(1)}, u32[]{:S(2)}, u32[]{:S(2)}) %all-to-all-start.2) | async-done | bytes 262176 | tf_op jit(solution)/shard_map/all_to_all | solution.py:152
  123.8 0.0 copy-done.3
  123.8 0.0 copy-done.4
  123.8 0.8 fusion.3
  124.7 13.8 %all_to_all.27 = bf16[8,128,128]{2,1,0:T(8,128)(2,1)S(1)} all-to-all(bf16[8,128,128]{2,1,0:T(8,128)(2,1)S(1)} %broadcast_in_dim.13), channel_id=1, replica_groups={{0,16,32,48,64,80,96,112},{2,18,34,50,66,82,98,114},{4,20,36,52,68,84,1..., dimensions={0} | all-to-all | bytes 524288 | tf_op jit(solution)/shard_map/all_to_all | solution.py:152
  138.5 1.8 %broadcast_in_dim.14 = bf16[8,8,128,128]{3,2,1,0:T(8,128)(2,1)} broadcast(bf16[8,128,128]{2,1,0:T(8,128)(2,1)S(1)} %all_to_all.27), dimensions={1,2,3} | broadcast | bytes 2359296 | tf_op jit(solution)/shard_map/broadcast_in_dim | solution.py:199
  140.4 3.6 %all-to-all-start.4 = ((bf16[8,8,128,128]{3,2,1,0:T(8,128)(2,1)}), bf16[8,8,128,128]{3,2,1,0:T(8,128)(2,1)S(1)}, u32[]{:S(2)}, u32[]{:S(2)}) async-start(bf16[8,8,128,128]{3,2,1,0:T(8,128)(2,1)} %broadcast_in_dim.14), calls=%async_computation.4 | async-start | bytes 4194304 | tf_op jit(solution)/shard_map/all_to_all | solution.py:152
  144.0 0.7 add_divide_fusion
  144.7 29.5 %all-to-all-done.4 = bf16[8,8,128,128]{3,2,1,0:T(8,128)(2,1)S(1)} async-done(((bf16[8,8,128,128]{3,2,1,0:T(8,128)(2,1)}), bf16[8,8,128,128]{3,2,1,0:T(8,128)(2,1)S(1)}, u32[]{:S(2)}, u32[]{:S(2)}) %all-to-all-start.4) | async-done | bytes 2097184 | tf_op jit(solution)/shard_map/all_to_all | solution.py:152
  174.2 0.0 copy-start
  174.2 1.4 copy-done
  175.5 3.5 %shard_map.121 = bf16[64,128,128]{2,1,0:T(8,128)(2,1)} custom-call(s32[1]{0:T(128)} %bitcast.core_ref, s32[1,64]{1,0:T(1,128)} %rank_ref.5, bf16[64,128,128]{2,1,0:T(8,128)(2,1)} %bitcast.24), custom_call_target="tpu_custom_call" | custom-call | bytes 4194304 | tf_op jit(solution)/shard_map/pallas_call | solution.py:200
  (3 shorter events, 0.1 us)
Async XLA Ops:
  6.8 6.1 %copy-start.5 = (bf16[128,256]{1,0:T(8,128)(2,1)S(1)}, bf16[128,256]{1,0:T(8,128)(2,1)}, u32[]{:S(2)}) copy-start(bf16[128,256]{1,0:T(8,128)(2,1)} %param.8) | copy-start | bytes 196612
  8.0 3.8 %collective-permute-start = (bf16[8,128,256]{2,1,0:T(8,128)(2,1)S(1)}, bf16[8,128,256]{2,1,0:T(8,128)(2,1)S(1)}, u32[]{:S(2)}, u32[]{:S(2)}) collective-permute-start(bf16[8,128,256]{2,1,0:T(8,128)(2,1)S(1)} %slice_bitcast_fusion), channel_id=1, source_target_pairs={{0,1},{1,0},{2,3},{3,2},{4,5},{5,4},{6,7},{7,6},{8,9},{9,8},{10,11... | collective-permute-start | bytes 1572872 | tf_op jit(solution)/shard_map/ppermute | solution.py:163
  57.2 3.8 %copy-start.1 = (bf16[8,128,256]{2,1,0:T(8,128)(2,1)}, bf16[8,128,256]{2,1,0:T(8,128)(2,1)S(1)}, u32[]{:S(2)}) copy-start(bf16[8,128,256]{2,1,0:T(8,128)(2,1)S(1)} %get-tuple-element.13.own_ref) | copy-start | bytes 1572868
  57.2 3.8 %collective-permute-start.1 = (bf16[8,128,256]{2,1,0:T(8,128)(2,1)S(1)}, bf16[8,128,256]{2,1,0:T(8,128)(2,1)S(1)}, u32[]{:S(2)}, u32[]{:S(2)}) collective-permute-start(bf16[8,128,256]{2,1,0:T(8,128)(2,1)S(1)} %get-tuple-element.13.own_ref), channel_id=1, source_target_pairs={{0,1},{1,0},{2,3},{3,2},{4,5},{5,4},{6,7},{7,6},{8,9},{9,8},{10,11... | collective-permute-start | bytes 1572872 | tf_op jit(solution)/shard_map/ppermute | solution.py:169
  61.0 0.8 copy-start.2
  105.6 18.2 %copy-start.3 = (f32[1,1,128,128]{3,2,1,0:T(8,128)S(1)}, f32[1,1,128,128]{3,2,1,0:T(8,128)}, u32[]{:S(2)}) copy-start(f32[1,1,128,128]{3,2,1,0:T(8,128)} %param.13) | copy-start | bytes 196612
  105.6 18.2 %copy-start.4 = (f32[1,1,128,128]{3,2,1,0:T(8,128)S(1)}, f32[1,1,128,128]{3,2,1,0:T(8,128)}, u32[]{:S(2)}) copy-start(f32[1,1,128,128]{3,2,1,0:T(8,128)} %param.12) | copy-start | bytes 196612
  105.6 18.2 %all-to-all-start.2 = ((bf16[8,128,128]{2,1,0:T(8,128)(2,1)}), bf16[8,128,128]{2,1,0:T(8,128)(2,1)S(1)}, u32[]{:S(2)}, u32[]{:S(2)}) async-start(bf16[8,128,128]{2,1,0:T(8,128)(2,1)} %reduce_sum.36), calls=%async_computation.2 | async-start | bytes 524288 | tf_op jit(solution)/shard_map/all_to_all | solution.py:152
  140.4 33.8 %all-to-all-start.4 = ((bf16[8,8,128,128]{3,2,1,0:T(8,128)(2,1)}), bf16[8,8,128,128]{3,2,1,0:T(8,128)(2,1)S(1)}, u32[]{:S(2)}, u32[]{:S(2)}) async-start(bf16[8,8,128,128]{3,2,1,0:T(8,128)(2,1)} %broadcast_in_dim.14), calls=%async_computation.4 | async-start | bytes 4194304 | tf_op jit(solution)/shard_map/all_to_all | solution.py:152
  174.2 1.4 copy-start

commit v2 on v1

v2 whole, which is shorter than its diff:
```python
import functools

import jax
import jax.numpy as jnp
from jax import lax
from jax.experimental import pallas as pl
from jax.experimental.pallas import tpu as pltpu
from jax.sharding import Mesh
from jax.sharding import PartitionSpec as P

DP = ("dp_0", "dp_1")
TENSOR = ("x", "core")
VMEM = pl.BlockSpec(memory_space=pltpu.VMEM)
SMEM = pl.BlockSpec(memory_space=pltpu.SMEM)
ANY = pl.BlockSpec(memory_space=pl.ANY)
BF = jnp.bfloat16
F32 = jnp.float32


def call(kernel, out_shape, ins, outs, scratch=(), flops=0, nbytes=0, limit=24):
    return pl.pallas_call(
        kernel,
        out_shape=out_shape,
        in_specs=ins,
        out_specs=outs,
        scratch_shapes=list(scratch),
        cost_estimate=pl.CostEstimate(flops=flops, bytes_accessed=nbytes, transcendentals=0),
        compiler_params=pltpu.CompilerParams(vmem_limit_bytes=limit * 2**20),
    )


def aligned(index, size):
    return pl.ds(pl.multiple_of(index * size, size), size)


def fill_slab(pos_ref, blocks_ref, slab):
    slots, bs, _ = blocks_ref.shape
    rows, width = slab.shape
    col_blocks = width // bs

    def clear(i, carry):
        slab[aligned(i, 16), :] = jnp.zeros((16, width), BF)
        return carry

    lax.fori_loop(0, rows // 16, clear, 0, unroll=2)

    def place(s, carry):
        p = pos_ref[0, s]
        slab[aligned(p // col_blocks, bs), aligned(p % col_blocks, bs)] = blocks_ref[s]
        return carry

    lax.fori_loop(0, slots, place, 0, unroll=4)


def partial_kernel(place_ref, pos_ref, hid_ref, blocks_ref, keep_ref, send_ref, slab):
    chips, _, feats = keep_ref.shape
    bits = chips.bit_length() - 1
    x, core = place_ref[0], place_ref[1]
    fill_slab(pos_ref, blocks_ref, slab)
    hid = hid_ref[...]
    for i in range(chips):
        r = sum(((i >> b) & 1) << (bits - 1 - b) for b in range(bits))
        chip = x ^ r
        for ref, c in ((keep_ref, core), (send_ref, 1 - core)):
            value = jnp.dot(hid, slab[:, aligned(2 * chip + c, feats)], preferred_element_type=F32)
            ref[i] = value.astype(BF)


def join_features(core, own_ref, other_ref, full, sems):
    pieces, _, feats = own_ref.shape
    copies = []
    for j in range(pieces):
        for k, (ref, c) in enumerate(((own_ref, core), (other_ref, 1 - core))):
            copies.append(pltpu.make_async_copy(ref.at[j], full.at[:, aligned(2 * j + c, feats)], sems.at[k, j]))
    for copy in copies:
        copy.start()
    return copies


def place_of(rank, core, side):
    return jnp.where(core == 0, rank, (rank % side) * side + rank // side)


def grads_kernel(side, factor, place_ref, pos_ref, rank_ref, hid_ref, own_ref, other_ref, out_ref, full, hid_t, sems):
    slots, bs, _ = out_ref.shape
    col_blocks = full.shape[1] // bs
    core = place_ref[1]
    copies = join_features(core, own_ref, other_ref, full, sems)
    hid_t[...] = hid_ref[...].T
    for copy in copies:
        copy.wait()

    def step(s, carry):
        p = pos_ref[0, s]
        value = jnp.dot(
            hid_t[aligned(p // col_blocks, bs), :],
            full[:, aligned(p % col_blocks, bs)],
            preferred_element_type=F32,
        )
        out_ref[place_of(rank_ref[0, s], core, side)] = (value * factor).astype(BF)
        return carry

    lax.fori_loop(0, slots, step, 0, unroll=8)


def back_kernel(place_ref, pos_ref, rank_ref, blocks_ref, own_ref, other_ref, out_ref, mine_ref, full, slab, sems):
    slots, bs, _ = blocks_ref.shape
    copies = join_features(place_ref[1], own_ref, other_ref, full, sems)
    fill_slab(pos_ref, blocks_ref, slab)

    def find(s, found):
        return jnp.where(rank_ref[0, s] == place_ref[2], s, found)

    mine_ref[...] = blocks_ref[lax.fori_loop(0, slots, find, 0)]
    for copy in copies:
        copy.wait()
    value = full[...]
    step = 2 * bs
    for n in range(slab.shape[0] // step):
        rows = slab[n * step : (n + 1) * step, :]
        out_ref[:, n * step : (n + 1) * step] = lax.dot_general(
            value, rows, (((1,), (1,)), ((), ())), preferred_element_type=F32
        ).astype(BF)


def list_kernel(side, place_ref, rank_ref, in_ref, out_ref, sems):
    core = place_ref[1]
    slots = out_ref.shape[0]

    def copy(s):
        return pltpu.make_async_copy(in_ref.at[place_of(rank_ref[0, s], core, side)], out_ref.at[s], sems.at[s])

    def start(s, carry):
        copy(s).start()
        return carry

    def wait(s, carry):
        copy(s).wait()
        return carry

    lax.fori_loop(0, slots, start, 0, unroll=4)
    lax.fori_loop(0, slots, wait, 0, unroll=4)


def chip_groups(sizes):
    n0, n1, nx, nc = sizes

    def at(z, y, x, c):
        return ((z * n1 + y) * nx + x) * nc + c

    along_0 = lambda c: [[at(z, y, x, c) for z in range(n0)] for y in range(n1) for x in range(nx)]
    along_1 = lambda c: [[at(z, y, x, c) for y in range(n1)] for z in range(n0) for x in range(nx)]
    return along_0(0) + along_1(1), along_1(0) + along_0(1)


def shards(sizes, hidden, cotangent, blocks, block_pos, owner_rank, moment, second):
    tokens, feats = cotangent.shape
    rows = hidden.shape[1]
    slots, bs, _ = blocks.shape
    n0, n1, nx, nc = sizes
    width = feats * nx * nc
    axes = (*DP, *TENSOR)
    first, then = chip_groups(sizes)
    place = jnp.stack([lax.axis_index("x"), lax.axis_index("core"), lax.axis_index(DP)])
    swap = [(0, 1), (1, 0)]
    factor = 1.0 / (tokens * n0 * n1)
    block_list = jax.ShapeDtypeStruct((slots, bs, bs), BF)

    def exchange(value, groups):
        return lax.all_to_all(value, axes, 0, 0, axis_index_groups=groups, tiled=True)

    own = lax.all_to_all(jnp.broadcast_to(cotangent, (nx, tokens, feats)), "x", 0, 0, tiled=True)
    keep, send = call(
        partial_kernel,
        (jax.ShapeDtypeStruct((nx, tokens, feats), BF),) * 2,
        [SMEM, SMEM, VMEM, VMEM],
        [VMEM, VMEM],
        [pltpu.VMEM((rows, width), BF)],
        flops=2 * tokens * rows * width,
        nbytes=4 * 2**20,
    )(place, block_pos, hidden, blocks)
    total = keep.astype(F32) + lax.ppermute(send, "core", swap).astype(F32)
    total = total.astype(BF)
    own, total = lax.optimization_barrier((own, total))
    other = lax.ppermute(own, "core", swap)

    def halved(value, step):
        half = value.shape[0] // 2
        theirs = lax.ppermute(value[half:], "x", [(i, i ^ step) for i in range(nx)])
        return (value[:half].astype(F32) + theirs.astype(F32)).astype(BF)

    total = halved(total, 1)

    grads = call(
        functools.partial(grads_kernel, n0, factor),
        block_list,
        [SMEM, SMEM, SMEM, VMEM, ANY, ANY],
        VMEM,
        [pltpu.VMEM((tokens, width), BF), pltpu.VMEM((rows, tokens), BF), pltpu.SemaphoreType.DMA((2, nx))],
        flops=2 * tokens * bs * bs * slots,
        nbytes=4 * 2**20,
    )(place, block_pos, owner_rank, hidden, own, other)
    hidden_grad, mine = call(
        back_kernel,
        (jax.ShapeDtypeStruct((tokens, rows), BF), jax.ShapeDtypeStruct((bs, bs), BF)),
        [SMEM, SMEM, SMEM, VMEM, ANY, ANY],
        [VMEM, VMEM],
        [pltpu.VMEM((tokens, width), BF), pltpu.VMEM((rows, width), BF), pltpu.SemaphoreType.DMA((2, nx))],
        flops=2 * tokens * rows * width,
        nbytes=4 * 2**20,
    )(place, block_pos, owner_rank, blocks, own, other)

    got = exchange(grads.reshape(n0, slots // n0, bs, bs), first)
    got, mine, total = lax.optimization_barrier((got, mine, total))
    step = 2
    while total.shape[0] > 1:
        total = halved(total, step)
        step *= 2
    mixed = total[0]
    part = got.astype(F32).sum(axis=0).astype(BF)
    grad = exchange(part, then).astype(F32).sum(axis=0)
    weight = mine.astype(F32)
    mom_next = 0.9 * moment[0, 0] + 0.1 * grad
    sec_next = 0.999 * second[0, 0] + 0.001 * grad * grad
    step_dir = mom_next / (jnp.sqrt(sec_next) + 1e-08)
    updated = (weight - 0.002 * (step_dir + 0.1 * weight)).astype(BF)
    row = exchange(jnp.broadcast_to(updated, (n1, bs, bs)), then)
    every = exchange(jnp.broadcast_to(row, (n0, n1, bs, bs)), first)
    new_blocks = call(
        functools.partial(list_kernel, n0),
        block_list,
        [SMEM, SMEM, ANY],
        ANY,
        [pltpu.SemaphoreType.DMA((slots,))],
        nbytes=4 * 2**20,
        limit=4,
    )(place, owner_rank, every.reshape(slots, bs, bs))
    return (mixed, hidden_grad, mom_next[None, None], sec_next[None, None], step_dir[None, None], new_blocks)


def make(sizes, torus):
    placed = (
        P(DP, TENSOR),
        P(DP, TENSOR),
        P(TENSOR, None, None),
        P(TENSOR, None),
        P(TENSOR, None),
        P(TENSOR, DP, None, None),
        P(TENSOR, DP, None, None),
    )
    return jax.shard_map(
        functools.partial(shards, sizes),
        mesh=torus,
        in_specs=placed,
        out_specs=(
            P(DP, TENSOR),
            P(DP, TENSOR),
            P(TENSOR, DP, None, None),
            P(TENSOR, DP, None, None),
            P(TENSOR, DP, None, None),
            P(TENSOR, None, None),
        ),
        check_vma=False,
    )


def solution(mesh):
    sizes = (8, mesh.shape["dp"] // 8, mesh.shape["tensor"] // 2, 2)
    return make(sizes, Mesh(mesh.devices.reshape(sizes), (*DP, *TENSOR)))
```

time: 180 us -> 154 us (0.86)
  blocking collectives: 95.3 us -> 31.6 us
  starting transfers between devices: 15.1 us -> 43.9 us
  waiting for transfers between devices: 36.9 us -> 48.1 us
  Pallas kernels: 21.2 us -> 15.1 us
  local copies, waits for them, and re-layouts: 5.17 us -> 7.71 us
    all_to_all x1 -> x0, blocking collectives: 43.4 us -> none  [shards(): came = lax.all_to_all(sent, 'x', 0, 0, tiled=True)]
    all_to_all x2, blocking collectives: 51.9 us -> 31.6 us  [exchange(): lax.all_to_all(value, axes, 0, 0, axis_index_groups=groups, tiled=True)]
    ppermute x1 -> x4, waiting for transfers between devices: 1.88 us -> 20.7 us  [the longest x3 18.9 us: halved(): theirs = lax.ppermute(value[half:], 'x', [(i, i ^ step) for i in range(nx)])]
    all_to_all x0 -> x1, starting transfers between devices: none -> 17.6 us  [shards(): lax.all_to_all(jnp.broadcast_to(cotangent, (nx, tokens, feats)), 'x', 0,...]
    all_to_all x2, waiting for transfers between devices: 33.2 us -> 24.5 us  [exchange(): lax.all_to_all(value, axes, 0, 0, axis_index_groups=groups, tiled=True)]
    ppermute x1 -> x4, starting transfers between devices: 1.92 us -> 10.1 us  [the longest x3 8.13 us: halved(): theirs = lax.ppermute(value[half:], 'x', [(i, i ^ step) for i in range(nx)])]
    pallas_call x3, Pallas kernels: 14.3 us -> 9.45 us  [the longest x1 4.2 us: shards(): call(functools.partial(grads_kernel, n0, factor), block_list, [SMEM, SMEM...]
    all_to_all x2, starting transfers between devices: 11.3 us -> 14.3 us  [exchange(): lax.all_to_all(value, axes, 0, 0, axis_index_groups=groups, tiled=True)]
  transfers between devices with their start and end apart: 4 -> 8, of which waited for: 4 -> 8; matrix products, arithmetic and copies ran while one was open for 0% -> 3% of each run, Pallas kernels for 4% -> 6%
where the time goes in v2:
time: 154 us; the launch traced here: 153 us
  waiting for transfers between devices  48.1 us (31%)
  starting transfers between devices  43.9 us (29%)
  blocking collectives  31.6 us (21%)
  Pallas kernels  15.1 us (10%)
  local copies, waits for them, and re-layouts  7.71 us (5%)
  other arithmetic  5.51 us (4%)
    all_to_all x2, blocking collectives, exchange(): lax.all_to_all(value, axes, 0, 0, axis_index_groups=groups, tiled=True)  31.6 us
    all_to_all x2, waiting for transfers between devices, exchange(): lax.all_to_all(value, axes, 0, 0, axis_index_groups=groups, tiled=True)  24.5 us
    ppermute x3, waiting for transfers between devices, halved(): theirs = lax.ppermute(value[half:], 'x', [(i, i ^ step) for i in range(nx)])  18.9 us
    all_to_all x1, starting transfers between devices, shards(): lax.all_to_all(jnp.broadcast_to(cotangent, (nx, tokens, feats)), 'x', 0,...  17.6 us
    all_to_all x2, starting transfers between devices, exchange(): lax.all_to_all(value, axes, 0, 0, axis_index_groups=groups, tiled=True)  14.3 us
    ppermute x3, starting transfers between devices, halved(): theirs = lax.ppermute(value[half:], 'x', [(i, i ^ step) for i in range(nx)])  8.13 us
    pallas_call x1, Pallas kernels, shards(): call(back_kernel, (jax.ShapeDtypeStruct((tokens, rows), BF), jax.ShapeDty...  5.62 us
    pallas_call x1, Pallas kernels, shards(): call(functools.partial(grads_kernel, n0, factor), block_list, [SMEM, SMEM...  4.2 us
  transfers between devices with their start and end apart: 8, of which 8 were waited for; matrix products, arithmetic and copies ran while one was open for 3% of the time, Pallas kernels for 6%

profile of v2, /device:TPU:2, one launch (start us, length us, event | category | flops | bytes accessed | tf_op | source)
XLA Modules:
  0.0 152.8 jit_solution(4295656353260104029)
XLA Ops:
  0.6 1.7 %broadcast_in_dim.12 = bf16[8,128,256]{2,1,0:T(8,128)(2,1)} broadcast(bf16[128,256]{1,0:T(8,128)(2,1)} %param.8), dimensions={1,2} | broadcast | bytes 589824 | tf_op jit(solution)/shard_map/broadcast_in_dim | solution.py:172
  2.3 17.6 %all-to-all-start = ((bf16[8,128,256]{2,1,0:T(8,128)(2,1)}), bf16[8,128,256]{2,1,0:T(8,128)(2,1)S(1)}, u32[]{:S(2)}, u32[]{:S(2)}) async-start(bf16[8,128,256]{2,1,0:T(8,128)(2,1)} %broadcast_in_dim.12), calls=%async_computation | async-start | bytes 1048576 | tf_op jit(solution)/shard_map/all_to_all | solution.py:172
  19.9 0.1 pad_add_fusion.place_ref
  20.0 0.0 copy-start
  20.0 1.6 %copy-done = bf16[64,128,128]{2,1,0:T(8,128)(2,1)S(1)} copy-done((bf16[64,128,128]{2,1,0:T(8,128)(2,1)S(1)}, bf16[64,128,128]{2,1,0:T(8,128)(2,1)}, u32[]{:S(2)}) %copy-start) | copy-done | bytes 2097176
  21.6 0.0 copy-start.2
  21.6 0.9 copy-done.2
  22.5 0.0 copy-start.5
  22.5 0.7 copy-done.5
  23.2 0.0 copy-start.3
  23.2 2.9 %shard_map.118 = (bf16[8,128,256]{2,1,0:T(8,128)(2,1)S(1)}, bf16[8,128,256]{2,1,0:T(8,128)(2,1)S(1)}) custom-call(s32[3]{0:T(128)S(1)} %pad_add_fusion.place_ref, s32[1,64]{1,0:T(1,128)S(1)} %copy-done.5, bf16[128,768]{1,0:T(8,128)(2,1)S(1)} %copy-done.2, bf16[64,128,128]{2,1,0:T(8,128)(2,1)S(1)} %copy-done), custom_call_target="tpu_custom_call" | custom-call | flops 805306368 | bytes 4194304 | tf_op jit(solution)/shard_map/pallas_call | solution.py:173
  26.0 1.9 %collective-permute-start = (bf16[8,128,256]{2,1,0:T(8,128)(2,1)S(1)}, bf16[8,128,256]{2,1,0:T(8,128)(2,1)S(1)}, u32[]{:S(2)}, u32[]{:S(2)}) collective-permute-start(bf16[8,128,256]{2,1,0:T(8,128)(2,1)S(1)} %get-tuple-element.16), channel_id=1, source_target_pairs={{0,1},{1,0},{2,3},{3,2},{4,5},{5,4},{6,7},{7,6},{8,9},{9,8},{10,11... | collective-permute-start | bytes 1572872 | tf_op jit(solution)/shard_map/ppermute | solution.py:182
  28.0 1.9 %collective-permute-done = bf16[8,128,256]{2,1,0:T(8,128)(2,1)S(1)} collective-permute-done((bf16[8,128,256]{2,1,0:T(8,128)(2,1)S(1)}, bf16[8,128,256]{2,1,0:T(8,128)(2,1)S(1)}, u32[]{:S(2)}, u32[]{:S(2)}) %collective-permute-start) | collective-permute-done | bytes 524320 | tf_op jit(solution)/shard_map/ppermute | solution.py:182
  29.9 1.0 add_convert_fusion
  30.8 1.0 all-to-all-done.own_ref
  31.8 1.9 %collective-permute-start.1 = (bf16[8,128,256]{2,1,0:T(8,128)(2,1)S(1)}, bf16[8,128,256]{2,1,0:T(8,128)(2,1)S(1)}, u32[]{:S(2)}, u32[]{:S(2)}) collective-permute-start(bf16[8,128,256]{2,1,0:T(8,128)(2,1)S(1)} %all-to-all-done.own_ref), channel_id=1, source_target_pairs={{0,1},{1,0},{2,3},{3,2},{4,5},{5,4},{6,7},{7,6},{8,9},{9,8},{10,11... | collective-permute-start | bytes 1572872 | tf_op jit(solution)/shard_map/ppermute | solution.py:185
  33.7 1.9 %collective-permute-done.1.other_ref = bf16[8,128,256]{2,1,0:T(8,128)(2,1)S(1)} collective-permute-done((bf16[8,128,256]{2,1,0:T(8,128)(2,1)S(1)}, bf16[8,128,256]{2,1,0:T(8,128)(2,1)S(1)}, u32[]{:S(2)}, u32[]{:S(2)}) %collective-permute-start.1) | collective-permute-done | bytes 524320 | tf_op jit(solution)/shard_map/ppermute | solution.py:185
  35.6 0.0 copy-done.3
  35.6 0.0 copy-done.4
  35.6 0.0 copy-done.6
  35.6 4.2 %shard_map.119 = bf16[64,128,128]{2,1,0:T(8,128)(2,1)} custom-call(s32[3]{0:T(128)S(1)} %pad_add_fusion.place_ref, s32[1,64]{1,0:T(1,128)S(1)} %copy-done.6, s32[1,64]{1,0:T(1,128)S(1)} %copy-done.4, bf16[128,768]{1,0:T(8,128)(2,1)S(1)} %copy-done.3, bf16[8,128,256]{2,1,0:T(8,128)(2,1)S(1)} %all-to-all-done.own_ref, ...), custom_call_target="tpu_custom_call" | custom-call | flops 268435456 | bytes 4194304 | tf_op jit(solution)/shard_map/pallas_call | solution.py:194
  39.8 0.0 copy-start.1
  39.8 10.7 %all-to-all-start.1 = ((bf16[8,8,128,128]{3,2,1,0:T(8,128)(2,1)}), bf16[8,8,128,128]{3,2,1,0:T(8,128)(2,1)}, u32[]{:S(2)}, u32[]{:S(2)}) async-start(bf16[8,8,128,128]{3,2,1,0:T(8,128)(2,1)} %bitcast.3), calls=%async_computation.1 | async-start | bytes 4194304 | tf_op jit(solution)/shard_map/all_to_all | solution.py:170
  50.5 1.0 slice.19
  51.5 3.4 %collective-permute-start.2 = (bf16[4,128,256]{2,1,0:T(8,128)(2,1)S(1)}, bf16[4,128,256]{2,1,0:T(8,128)(2,1)S(1)}, u32[]{:S(2)}, u32[]{:S(2)}) collective-permute-start(bf16[4,128,256]{2,1,0:T(8,128)(2,1)S(1)} %slice.19), channel_id=1, source_target_pairs={{0,2},{2,0},{4,6},{6,4},{8,10},{10,8},{12,14},{14,12},{1,3},{3,1},... | collective-permute-start | bytes 786440 | tf_op jit(solution)/shard_map/ppermute | solution.py:189
  54.9 4.9 %collective-permute-done.2 = bf16[4,128,256]{2,1,0:T(8,128)(2,1)S(1)} collective-permute-done((bf16[4,128,256]{2,1,0:T(8,128)(2,1)S(1)}, bf16[4,128,256]{2,1,0:T(8,128)(2,1)S(1)}, u32[]{:S(2)}, u32[]{:S(2)}) %collective-permute-start.2) | collective-permute-done | bytes 262176 | tf_op jit(solution)/shard_map/ppermute | solution.py:189
  59.8 1.0 add_convert_fusion.1
  60.8 0.0 copy-done.1
  60.8 5.6 %shard_map.120 = (bf16[128,768]{1,0:T(8,128)(2,1)}, bf16[128,128]{1,0:T(8,128)(2,1)S(1)}) custom-call(s32[3]{0:T(128)S(1)} %pad_add_fusion.place_ref, s32[1,64]{1,0:T(1,128)S(1)} %copy-done.6, s32[1,64]{1,0:T(1,128)S(1)} %copy-done.4, bf16[64,128,128]{2,1,0:T(8,128)(2,1)S(1)} %copy-done.1, bf16[8,128,256]{2,1,0:T(8,128)(2,1)S(1)} %all-to-all-done.own_ref, ...), custom_call_target="tpu_custom_call" | custom-call | flops 805306368 | bytes 4194304 | tf_op jit(solution)/shard_map/pallas_call | solution.py:203
  66.4 0.0 copy-start.7
  66.5 0.0 copy-start.8
  66.5 14.4 %all-to-all-done.1 = bf16[8,8,128,128]{3,2,1,0:T(8,128)(2,1)} async-done(((bf16[8,8,128,128]{3,2,1,0:T(8,128)(2,1)}), bf16[8,8,128,128]{3,2,1,0:T(8,128)(2,1)}, u32[]{:S(2)}, u32[]{:S(2)}) %all-to-all-start.1) | async-done | bytes 2097184 | tf_op jit(solution)/shard_map/all_to_all | solution.py:170
  80.9 2.0 %reduce_sum.23 = bf16[8,128,128]{2,1,0:T(8,128)(2,1)S(1)} reduce(bf16[8,8,128,128]{3,2,1,0:T(8,128)(2,1)} %all-to-all-done.1, bf16[]{:T(256)} %constant.26.clone.1), dimensions={0}, to_apply=%region_0.0 | reduce | flops 917504 | bytes 2359298 | tf_op jit(solution)/shard_map/reduce_sum | solution.py:220
  82.9 18.8 %all_to_all.25 = bf16[8,128,128]{2,1,0:T(8,128)(2,1)S(1)} all-to-all(bf16[8,128,128]{2,1,0:T(8,128)(2,1)S(1)} %reduce_sum.23), channel_id=1, replica_groups={{0,16,32,48,64,80,96,112},{2,18,34,50,66,82,98,114},{4,20,36,52,68,84,1..., dimensions={0} | all-to-all | bytes 524288 | tf_op jit(solution)/shard_map/all_to_all | solution.py:170
  101.7 0.0 copy-done.7
  101.7 0.0 copy-done.8
  101.7 0.1 fusion.2
  101.8 12.9 %all_to_all.26 = bf16[8,128,128]{2,1,0:T(8,128)(2,1)S(1)} all-to-all(bf16[8,128,128]{2,1,0:T(8,128)(2,1)S(1)} %broadcast_in_dim.13), channel_id=1, replica_groups={{0,16,32,48,64,80,96,112},{2,18,34,50,66,82,98,114},{4,20,36,52,68,84,1..., dimensions={0} | all-to-all | bytes 524288 | tf_op jit(solution)/shard_map/all_to_all | solution.py:170
  114.7 1.8 %broadcast_in_dim.14 = bf16[8,8,128,128]{3,2,1,0:T(8,128)(2,1)} broadcast(bf16[8,128,128]{2,1,0:T(8,128)(2,1)S(1)} %all_to_all.26), dimensions={1,2,3} | broadcast | bytes 2359296 | tf_op jit(solution)/shard_map/broadcast_in_dim | solution.py:228
  116.5 3.6 %all-to-all-start.4 = ((bf16[8,8,128,128]{3,2,1,0:T(8,128)(2,1)}), bf16[8,8,128,128]{3,2,1,0:T(8,128)(2,1)S(1)}, u32[]{:S(2)}, u32[]{:S(2)}) async-start(bf16[8,8,128,128]{3,2,1,0:T(8,128)(2,1)} %broadcast_in_dim.14), calls=%async_computation.4 | async-start | bytes 4194304 | tf_op jit(solution)/shard_map/all_to_all | solution.py:170
  120.2 1.9 %collective-permute-start.3 = (bf16[2,128,256]{2,1,0:T(8,128)(2,1)S(1)}, bf16[2,128,256]{2,1,0:T(8,128)(2,1)S(1)}, u32[]{:S(2)}, u32[]{:S(2)}) collective-permute-start(bf16[2,128,256]{2,1,0:T(8,128)(2,1)S(1)} %slice.21), channel_id=1, source_target_pairs={{0,4},{2,6},{4,0},{6,2},{8,12},{10,14},{12,8},{14,10},{1,5},{3,7},... | collective-permute-start | bytes 393224 | tf_op jit(solution)/shard_map/ppermute | solution.py:189
  122.1 6.5 %collective-permute-done.3 = bf16[2,128,256]{2,1,0:T(8,128)(2,1)S(1)} collective-permute-done((bf16[2,128,256]{2,1,0:T(8,128)(2,1)S(1)}, bf16[2,128,256]{2,1,0:T(8,128)(2,1)S(1)}, u32[]{:S(2)}, u32[]{:S(2)}) %collective-permute-start.3) | collective-permute-done | bytes 131104 | tf_op jit(solution)/shard_map/ppermute | solution.py:189
  128.6 2.8 %collective-permute-start.4 = (bf16[1,128,256]{2,1,0:T(8,128)(2,1)S(1)}, bf16[1,128,256]{2,1,0:T(8,128)(2,1)S(1)}, u32[]{:S(2)}, u32[]{:S(2)}) collective-permute-start(bf16[1,128,256]{2,1,0:T(8,128)(2,1)S(1)} %slice.25), channel_id=1, source_target_pairs={{0,8},{2,10},{4,12},{6,14},{8,0},{10,2},{12,4},{14,6},{1,9},{3,11}... | collective-permute-start | bytes 196616 | tf_op jit(solution)/shard_map/ppermute | solution.py:189
  131.5 7.5 %collective-permute-done.4 = bf16[1,128,256]{2,1,0:T(8,128)(2,1)S(1)} collective-permute-done((bf16[1,128,256]{2,1,0:T(8,128)(2,1)S(1)}, bf16[1,128,256]{2,1,0:T(8,128)(2,1)S(1)}, u32[]{:S(2)}, u32[]{:S(2)}) %collective-permute-start.4) | collective-permute-done | bytes 65568 | tf_op jit(solution)/shard_map/ppermute | solution.py:189
  139.0 0.6 fusion.8
  139.6 0.7 add_divide_fusion
  140.3 10.0 %all-to-all-done.4 = bf16[8,8,128,128]{3,2,1,0:T(8,128)(2,1)S(1)} async-done(((bf16[8,8,128,128]{3,2,1,0:T(8,128)(2,1)}), bf16[8,8,128,128]{3,2,1,0:T(8,128)(2,1)S(1)}, u32[]{:S(2)}, u32[]{:S(2)}) %all-to-all-start.4) | async-done | bytes 2097184 | tf_op jit(solution)/shard_map/all_to_all | solution.py:170
  150.3 2.4 %shard_map.121 = bf16[64,128,128]{2,1,0:T(8,128)(2,1)} custom-call(s32[3]{0:T(128)S(1)} %pad_add_fusion.place_ref, s32[1,64]{1,0:T(1,128)S(1)} %copy-done.4, bf16[64,128,128]{2,1,0:T(8,128)(2,1)S(1)} %bitcast.20), custom_call_target="tpu_custom_call" | custom-call | bytes 4194304 | tf_op jit(solution)/shard_map/pallas_call | solution.py:229
  (7 shorter events, 0.1 us)
Async XLA Ops:
  2.3 29.5 %all-to-all-start = ((bf16[8,128,256]{2,1,0:T(8,128)(2,1)}), bf16[8,128,256]{2,1,0:T(8,128)(2,1)S(1)}, u32[]{:S(2)}, u32[]{:S(2)}) async-start(bf16[8,128,256]{2,1,0:T(8,128)(2,1)} %broadcast_in_dim.12), calls=%async_computation | async-start | bytes 1048576 | tf_op jit(solution)/shard_map/all_to_all | solution.py:172
  20.0 1.6 %copy-start = (bf16[64,128,128]{2,1,0:T(8,128)(2,1)S(1)}, bf16[64,128,128]{2,1,0:T(8,128)(2,1)}, u32[]{:S(2)}) copy-start(bf16[64,128,128]{2,1,0:T(8,128)(2,1)} %blocks_ref.3) | copy-start | bytes 6291460
  21.6 0.9 copy-start.2
  22.5 0.7 copy-start.5
  23.2 12.4 %copy-start.3 = (bf16[128,768]{1,0:T(8,128)(2,1)S(1)}, bf16[128,768]{1,0:T(8,128)(2,1)}, u32[]{:S(2)}) copy-start(bf16[128,768]{1,0:T(8,128)(2,1)} %hid_ref.3) | copy-start | bytes 589828
  23.2 12.4 %copy-start.4 = (s32[1,64]{1,0:T(1,128)S(1)}, s32[1,64]{1,0:T(1,128)}, u32[]{:S(2)}) copy-start(s32[1,64]{1,0:T(1,128)} %rank_ref.5) | copy-start | bytes 772
  23.2 12.4 %copy-start.6 = (s32[1,64]{1,0:T(1,128)S(1)}, s32[1,64]{1,0:T(1,128)}, u32[]{:S(2)}) copy-start(s32[1,64]{1,0:T(1,128)} %pos_ref.5) | copy-start | bytes 772
  26.0 3.8 %collective-permute-start = (bf16[8,128,256]{2,1,0:T(8,128)(2,1)S(1)}, bf16[8,128,256]{2,1,0:T(8,128)(2,1)S(1)}, u32[]{:S(2)}, u32[]{:S(2)}) collective-permute-start(bf16[8,128,256]{2,1,0:T(8,128)(2,1)S(1)} %get-tuple-element.16), channel_id=1, source_target_pairs={{0,1},{1,0},{2,3},{3,2},{4,5},{5,4},{6,7},{7,6},{8,9},{9,8},{10,11... | collective-permute-start | bytes 1572872 | tf_op jit(solution)/shard_map/ppermute | solution.py:182
  31.8 3.8 %collective-permute-start.1 = (bf16[8,128,256]{2,1,0:T(8,128)(2,1)S(1)}, bf16[8,128,256]{2,1,0:T(8,128)(2,1)S(1)}, u32[]{:S(2)}, u32[]{:S(2)}) collective-permute-start(bf16[8,128,256]{2,1,0:T(8,128)(2,1)S(1)} %all-to-all-done.own_ref), channel_id=1, source_target_pairs={{0,1},{1,0},{2,3},{3,2},{4,5},{5,4},{6,7},{7,6},{8,9},{9,8},{10,11... | collective-permute-start | bytes 1572872 | tf_op jit(solution)/shard_map/ppermute | solution.py:185
  39.8 21.0 %copy-start.1 = (bf16[64,128,128]{2,1,0:T(8,128)(2,1)S(1)}, bf16[64,128,128]{2,1,0:T(8,128)(2,1)}, u32[]{:S(2)}) copy-start(bf16[64,128,128]{2,1,0:T(8,128)(2,1)} %blocks_ref.3) | copy-start | bytes 6291460
  39.8 41.1 %all-to-all-start.1 = ((bf16[8,8,128,128]{3,2,1,0:T(8,128)(2,1)}), bf16[8,8,128,128]{3,2,1,0:T(8,128)(2,1)}, u32[]{:S(2)}, u32[]{:S(2)}) async-start(bf16[8,8,128,128]{3,2,1,0:T(8,128)(2,1)} %bitcast.3), calls=%async_computation.1 | async-start | bytes 4194304 | tf_op jit(solution)/shard_map/all_to_all | solution.py:170
  51.5 8.3 %collective-permute-start.2 = (bf16[4,128,256]{2,1,0:T(8,128)(2,1)S(1)}, bf16[4,128,256]{2,1,0:T(8,128)(2,1)S(1)}, u32[]{:S(2)}, u32[]{:S(2)}) collective-permute-start(bf16[4,128,256]{2,1,0:T(8,128)(2,1)S(1)} %slice.19), channel_id=1, source_target_pairs={{0,2},{2,0},{4,6},{6,4},{8,10},{10,8},{12,14},{14,12},{1,3},{3,1},... | collective-permute-start | bytes 786440 | tf_op jit(solution)/shard_map/ppermute | solution.py:189
  66.4 35.2 %copy-start.7 = (f32[1,1,128,128]{3,2,1,0:T(8,128)S(1)}, f32[1,1,128,128]{3,2,1,0:T(8,128)}, u32[]{:S(2)}) copy-start(f32[1,1,128,128]{3,2,1,0:T(8,128)} %param.13) | copy-start | bytes 196612
  66.5 35.2 %copy-start.8 = (f32[1,1,128,128]{3,2,1,0:T(8,128)S(1)}, f32[1,1,128,128]{3,2,1,0:T(8,128)}, u32[]{:S(2)}) copy-start(f32[1,1,128,128]{3,2,1,0:T(8,128)} %param.12) | copy-start | bytes 196612
  116.5 33.8 %all-to-all-start.4 = ((bf16[8,8,128,128]{3,2,1,0:T(8,128)(2,1)}), bf16[8,8,128,128]{3,2,1,0:T(8,128)(2,1)S(1)}, u32[]{:S(2)}, u32[]{:S(2)}) async-start(bf16[8,8,128,128]{3,2,1,0:T(8,128)(2,1)} %broadcast_in_dim.14), calls=%async_computation.4 | async-start | bytes 4194304 | tf_op jit(solution)/shard_map/all_to_all | solution.py:170
  120.2 8.4 %collective-permute-start.3 = (bf16[2,128,256]{2,1,0:T(8,128)(2,1)S(1)}, bf16[2,128,256]{2,1,0:T(8,128)(2,1)S(1)}, u32[]{:S(2)}, u32[]{:S(2)}) collective-permute-start(bf16[2,128,256]{2,1,0:T(8,128)(2,1)S(1)} %slice.21), channel_id=1, source_target_pairs={{0,4},{2,6},{4,0},{6,2},{8,12},{10,14},{12,8},{14,10},{1,5},{3,7},... | collective-permute-start | bytes 393224 | tf_op jit(solution)/shard_map/ppermute | solution.py:189
  128.6 10.4 %collective-permute-start.4 = (bf16[1,128,256]{2,1,0:T(8,128)(2,1)S(1)}, bf16[1,128,256]{2,1,0:T(8,128)(2,1)S(1)}, u32[]{:S(2)}, u32[]{:S(2)}) collective-permute-start(bf16[1,128,256]{2,1,0:T(8,128)(2,1)S(1)} %slice.25), channel_id=1, source_target_pairs={{0,8},{2,10},{4,12},{6,14},{8,0},{10,2},{12,4},{14,6},{1,9},{3,11}... | collective-permute-start | bytes 196616 | tf_op jit(solution)/shard_map/ppermute | solution.py:189

commit v3 on v2

--- a/solution.py
+++ b/solution.py
@@ -52,11 +52,16 @@
     lax.fori_loop(0, slots, place, 0, unroll=4)
 
 
-def partial_kernel(place_ref, pos_ref, hid_ref, blocks_ref, keep_ref, send_ref, slab):
+def partial_kernel(place_ref, pos_ref, rank_ref, hid_ref, blocks_ref, keep_ref, send_ref, mine_ref, slab):
     chips, _, feats = keep_ref.shape
     bits = chips.bit_length() - 1
     x, core = place_ref[0], place_ref[1]
     fill_slab(pos_ref, blocks_ref, slab)
+
+    def find(s, found):
+        return jnp.where(rank_ref[0, s] == place_ref[2], s, found)
+
+    mine_ref[...] = blocks_ref[lax.fori_loop(0, blocks_ref.shape[0], find, 0)]
     hid = hid_ref[...]
     for i in range(chips):
         r = sum(((i >> b) & 1) << (bits - 1 - b) for b in range(bits))
@@ -81,7 +86,7 @@
     return jnp.where(core == 0, rank, (rank % side) * side + rank // side)
 
 
-def grads_kernel(side, factor, place_ref, pos_ref, rank_ref, hid_ref, own_ref, other_ref, out_ref, full, hid_t, sems):
+def grads_kernel(side, factor, place_ref, pos_ref, rank_ref, hid_ref, own_ref, other_ref, out_ref, full, hid_t, made, sems, out_sems):
     slots, bs, _ = out_ref.shape
     col_blocks = full.shape[1] // bs
     core = place_ref[1]
@@ -90,28 +95,39 @@
     for copy in copies:
         copy.wait()
 
-    def step(s, carry):
-        p = pos_ref[0, s]
-        value = jnp.dot(
-            hid_t[aligned(p // col_blocks, bs), :],
-            full[:, aligned(p % col_blocks, bs)],
-            preferred_element_type=F32,
-        )
-        out_ref[place_of(rank_ref[0, s], core, side)] = (value * factor).astype(BF)
-        return carry
-
-    lax.fori_loop(0, slots, step, 0, unroll=8)
-
-
-def back_kernel(place_ref, pos_ref, rank_ref, blocks_ref, own_ref, other_ref, out_ref, mine_ref, full, slab, sems):
-    slots, bs, _ = blocks_ref.shape
+    def out_copy(s):
+        return pltpu.make_async_copy(made.at[s], out_ref.at[place_of(rank_ref[0, s], core, side)], out_sems.at[s])
+
+    group = min(8, slots)
+
+    def step(g, carry):
+        for i in range(group):
+            s = g * group + i
+            p = pos_ref[0, s]
+            value = jnp.dot(
+                hid_t[aligned(p // col_blocks, bs), :],
+                full[:, aligned(p % col_blocks, bs)],
+                preferred_element_type=F32,
+            )
+            made[s] = (value * factor).astype(BF)
+        for i in range(group):
+            out_copy(g * group + i).start()
+        return carry
+
+    lax.fori_loop(0, slots // group, step, 0)
+
+    def wait(s, carry):
+        out_copy(s).wait()
+        return carry
+
+    lax.fori_loop(0, slots, wait, 0, unroll=4)
+
+
+def back_kernel(place_ref, pos_ref, blocks_ref, own_ref, other_ref, out_ref, full, slab, sems):
+    bs = blocks_ref.shape[1]
     copies = join_features(place_ref[1], own_ref, other_ref, full, sems)
     fill_slab(pos_ref, blocks_ref, slab)
 
-    def find(s, found):
-        return jnp.where(rank_ref[0, s] == place_ref[2], s, found)
-
-    mine_ref[...] = blocks_ref[lax.fori_loop(0, slots, find, 0)]
     for copy in copies:
         copy.wait()
     value = full[...]
@@ -170,51 +186,58 @@
         return lax.all_to_all(value, axes, 0, 0, axis_index_groups=groups, tiled=True)
 
     own = lax.all_to_all(jnp.broadcast_to(cotangent, (nx, tokens, feats)), "x", 0, 0, tiled=True)
-    keep, send = call(
+    keep, send, mine = call(
         partial_kernel,
-        (jax.ShapeDtypeStruct((nx, tokens, feats), BF),) * 2,
-        [SMEM, SMEM, VMEM, VMEM],
-        [VMEM, VMEM],
+        (*(jax.ShapeDtypeStruct((nx, tokens, feats), BF),) * 2, jax.ShapeDtypeStruct((bs, bs), BF)),
+        [SMEM, SMEM, SMEM, VMEM, VMEM],
+        [VMEM] * 3,
         [pltpu.VMEM((rows, width), BF)],
         flops=2 * tokens * rows * width,
         nbytes=4 * 2**20,
-    )(place, block_pos, hidden, blocks)
-    total = keep.astype(F32) + lax.ppermute(send, "core", swap).astype(F32)
-    total = total.astype(BF)
-    own, total = lax.optimization_barrier((own, total))
+    )(place, block_pos, owner_rank, hidden, blocks)
+    own, keep, send = lax.optimization_barrier((own, keep, send))
     other = lax.ppermute(own, "core", swap)
-
-    def halved(value, step):
-        half = value.shape[0] // 2
-        theirs = lax.ppermute(value[half:], "x", [(i, i ^ step) for i in range(nx)])
-        return (value[:half].astype(F32) + theirs.astype(F32)).astype(BF)
-
-    total = halved(total, 1)
-
     grads = call(
         functools.partial(grads_kernel, n0, factor),
         block_list,
         [SMEM, SMEM, SMEM, VMEM, ANY, ANY],
+        ANY,
+        [
+            pltpu.VMEM((tokens, width), BF),
+            pltpu.VMEM((rows, tokens), BF),
+            pltpu.VMEM((slots, bs, bs), BF),
+            pltpu.SemaphoreType.DMA((2, nx)),
+            pltpu.SemaphoreType.DMA((slots,)),
+        ],
+        flops=2 * tokens * bs * bs * slots,
+        nbytes=4 * 2**20,
+        limit=12,
+    )(place, block_pos, owner_rank, hidden, own, other)
+    grads, keep, send = lax.optimization_barrier((grads, keep, send))
+    hidden_grad = call(
+        back_kernel,
+        jax.ShapeDtypeStruct((tokens, rows), BF),
+        [SMEM, SMEM, VMEM, ANY, ANY],
         VMEM,
-        [pltpu.VMEM((tokens, width), BF), pltpu.VMEM((rows, tokens), BF), pltpu.SemaphoreType.DMA((2, nx))],
-        flops=2 * tokens * bs * bs * slots,
-        nbytes=4 * 2**20,
-    )(place, block_pos, owner_rank, hidden, own, other)
-    hidden_grad, mine = call(
-        back_kernel,
-        (jax.ShapeDtypeStruct((tokens, rows), BF), jax.ShapeDtypeStruct((bs, bs), BF)),
-        [SMEM, SMEM, SMEM, VMEM, ANY, ANY],
-        [VMEM, VMEM],
         [pltpu.VMEM((tokens, width), BF), pltpu.VMEM((rows, width), BF), pltpu.SemaphoreType.DMA((2, nx))],
         flops=2 * tokens * rows * width,
         nbytes=4 * 2**20,
-    )(place, block_pos, owner_rank, blocks, own, other)
+        limit=16,
+    )(place, block_pos, blocks, own, other)
+
+    def halved(value, step, beside=None):
+        half = value.shape[0] // 2
+        theirs = lax.ppermute(value[half:], "x", [(i, i ^ step) for i in range(nx)])
+        theirs, beside = lax.optimization_barrier((theirs, beside))
+        return (value[:half].astype(F32) + theirs.astype(F32)).astype(BF), beside
 
     got = exchange(grads.reshape(n0, slots // n0, bs, bs), first)
-    got, mine, total = lax.optimization_barrier((got, mine, total))
+    total = (keep.astype(F32) + lax.ppermute(send, "core", swap).astype(F32)).astype(BF)
+    total, hidden_grad = halved(total, 1, hidden_grad)
+    got, total = lax.optimization_barrier((got, total))
     step = 2
     while total.shape[0] > 1:
-        total = halved(total, step)
+        total, _ = halved(total, step)
         step *= 2
     mixed = total[0]
     part = got.astype(F32).sum(axis=0).astype(BF)

time: 154 us -> 153 us (level)
    ppermute x3, waiting for transfers between devices: 18.9 us -> 15.9 us  [halved(): theirs = lax.ppermute(value[half:], 'x', [(i, i ^ step) for i in range(nx)])]
    unnamed x18 -> x24, local copies, waits for them, and re-layouts: 3.2 us -> 5.44 us
    all_to_all x1, waiting for transfers between devices: 0.97 us -> 2.81 us  [shards(): lax.all_to_all(jnp.broadcast_to(cotangent, (nx, tokens, feats)), 'x', 0,...]
  transfers between devices with their start and end apart: 8 -> 8, of which waited for: 8 -> 8; matrix products, arithmetic and copies ran while one was open for 3% -> 2% of each run, Pallas kernels for 6% -> 6%
where the time goes in v3:
time: 153 us; the launch traced here: 152 us
  waiting for transfers between devices  47.6 us (31%)
  starting transfers between devices  44.1 us (29%)
  blocking collectives  30.9 us (20%)
  Pallas kernels  15.1 us (10%)
  local copies, waits for them, and re-layouts  9 us (6%)
  other arithmetic  4.75 us (3%)
    all_to_all x2, blocking collectives, exchange(): lax.all_to_all(value, axes, 0, 0, axis_index_groups=groups, tiled=True)  30.9 us
    all_to_all x2, waiting for transfers between devices, exchange(): lax.all_to_all(value, axes, 0, 0, axis_index_groups=groups, tiled=True)  24.9 us
    all_to_all x1, starting transfers between devices, shards(): lax.all_to_all(jnp.broadcast_to(cotangent, (nx, tokens, feats)), 'x', 0,...  17.9 us
    ppermute x3, waiting for transfers between devices, halved(): theirs = lax.ppermute(value[half:], 'x', [(i, i ^ step) for i in range(nx)])  15.9 us
    all_to_all x2, starting transfers between devices, exchange(): lax.all_to_all(value, axes, 0, 0, axis_index_groups=groups, tiled=True)  14.2 us
    ppermute x3, starting transfers between devices, halved(): theirs = lax.ppermute(value[half:], 'x', [(i, i ^ step) for i in range(nx)])  8.15 us
    unnamed x24, local copies, waits for them, and re-layouts  5.44 us
    pallas_call x1, Pallas kernels, shards(): call(back_kernel, jax.ShapeDtypeStruct((tokens, rows), BF), [SMEM, SMEM,...  4.9 us
  transfers between devices with their start and end apart: 8, of which 8 were waited for; matrix products, arithmetic and copies ran while one was open for 2% of the time, Pallas kernels for 6%

profile of v3, /device:TPU:2, one launch (start us, length us, event | category | flops | bytes accessed | tf_op | source)
XLA Modules:
  0.0 152.2 jit_solution(18075751418083705193)
XLA Ops:
  0.6 1.7 %broadcast_in_dim.12 = bf16[8,128,256]{2,1,0:T(8,128)(2,1)} broadcast(bf16[128,256]{1,0:T(8,128)(2,1)} %param.8), dimensions={1,2} | broadcast | bytes 589824 | tf_op jit(solution)/shard_map/broadcast_in_dim | solution.py:188
  2.3 0.0 copy-start.4
  2.3 17.9 %all-to-all-start = ((bf16[8,128,256]{2,1,0:T(8,128)(2,1)}), bf16[8,128,256]{2,1,0:T(8,128)(2,1)S(1)}, u32[]{:S(2)}, u32[]{:S(2)}) async-start(bf16[8,128,256]{2,1,0:T(8,128)(2,1)} %broadcast_in_dim.12), calls=%async_computation | async-start | bytes 1048576 | tf_op jit(solution)/shard_map/all_to_all | solution.py:188
  20.2 0.1 pad_add_fusion.place_ref
  20.2 1.6 %copy-done = bf16[64,128,128]{2,1,0:T(8,128)(2,1)S(1)} copy-done((bf16[64,128,128]{2,1,0:T(8,128)(2,1)S(1)}, bf16[64,128,128]{2,1,0:T(8,128)(2,1)}, u32[]{:S(2)}) %copy-start) | copy-done | bytes 2097176
  21.8 0.9 copy-done.3
  22.8 0.7 copy-done.5
  23.4 0.7 copy-done.7
  24.1 3.5 %shard_map.118 = (bf16[8,128,256]{2,1,0:T(8,128)(2,1)S(1)}, bf16[8,128,256]{2,1,0:T(8,128)(2,1)S(1)}, bf16[128,128]{1,0:T(8,128)(2,1)S(1)}) custom-call(s32[3]{0:T(128)S(1)} %pad_add_fusion.place_ref, s32[1,64]{1,0:T(1,128)S(1)} %copy-done.5, s32[1,64]{1,0:T(1,128)S(1)} %copy-done.7, bf16[128,768]{1,0:T(8,128)(2,1)S(1)} %copy-done.3, ...), custom_call_target="tpu_custom_call" | custom-call | flops 805306368 | bytes 4194304 | tf_op jit(solution)/shard_map/pallas_call | solution.py:189
  27.6 0.0 copy-start.2
  27.6 0.8 copy-done.2
  28.4 0.8 copy-done.9
  29.2 2.8 %all-to-all-done.own_ref = bf16[8,128,256]{2,1,0:T(8,128)(2,1)S(1)} async-done(((bf16[8,128,256]{2,1,0:T(8,128)(2,1)}), bf16[8,128,256]{2,1,0:T(8,128)(2,1)S(1)}, u32[]{:S(2)}, u32[]{:S(2)}) %all-to-all-start) | async-done | bytes 524320 | tf_op jit(solution)/shard_map/all_to_all | solution.py:188
  32.0 1.9 %collective-permute-start = (bf16[8,128,256]{2,1,0:T(8,128)(2,1)S(1)}, bf16[8,128,256]{2,1,0:T(8,128)(2,1)S(1)}, u32[]{:S(2)}, u32[]{:S(2)}) collective-permute-start(bf16[8,128,256]{2,1,0:T(8,128)(2,1)S(1)} %all-to-all-done.own_ref), channel_id=1, source_target_pairs={{0,1},{1,0},{2,3},{3,2},{4,5},{5,4},{6,7},{7,6},{8,9},{9,8},{10,11... | collective-permute-start | bytes 1572872 | tf_op jit(solution)/shard_map/ppermute | solution.py:199
  33.9 1.9 %collective-permute-done.other_ref = bf16[8,128,256]{2,1,0:T(8,128)(2,1)S(1)} collective-permute-done((bf16[8,128,256]{2,1,0:T(8,128)(2,1)S(1)}, bf16[8,128,256]{2,1,0:T(8,128)(2,1)S(1)}, u32[]{:S(2)}, u32[]{:S(2)}) %collective-permute-start) | collective-permute-done | bytes 524320 | tf_op jit(solution)/shard_map/ppermute | solution.py:199
  35.8 0.0 copy-done.4
  35.8 0.0 copy-done.6
  35.8 0.0 copy-done.8
  35.8 4.3 %shard_map.119 = bf16[64,128,128]{2,1,0:T(8,128)(2,1)} custom-call(s32[3]{0:T(128)S(1)} %pad_add_fusion.place_ref, s32[1,64]{1,0:T(1,128)S(1)} %copy-done.6, s32[1,64]{1,0:T(1,128)S(1)} %copy-done.8, bf16[128,768]{1,0:T(8,128)(2,1)S(1)} %copy-done.4, bf16[8,128,256]{2,1,0:T(8,128)(2,1)S(1)} %all-to-all-done.own_ref, ...), custom_call_target="tpu_custom_call" | custom-call | flops 268435456 | bytes 4194304 | tf_op jit(solution)/shard_map/pallas_call | solution.py:200
  40.1 0.0 copy-start.1
  40.1 10.6 %all-to-all-start.1 = ((bf16[8,8,128,128]{3,2,1,0:T(8,128)(2,1)}), bf16[8,8,128,128]{3,2,1,0:T(8,128)(2,1)}, u32[]{:S(2)}, u32[]{:S(2)}) async-start(bf16[8,8,128,128]{3,2,1,0:T(8,128)(2,1)} %bitcast.3), calls=%async_computation.1 | async-start | bytes 4194304 | tf_op jit(solution)/shard_map/all_to_all | solution.py:186
  50.7 1.9 %collective-permute-start.1 = (bf16[8,128,256]{2,1,0:T(8,128)(2,1)}, bf16[8,128,256]{2,1,0:T(8,128)(2,1)S(1)}, u32[]{:S(2)}, u32[]{:S(2)}) collective-permute-start(bf16[8,128,256]{2,1,0:T(8,128)(2,1)} %copy-done.9), channel_id=1, source_target_pairs={{0,1},{1,0},{2,3},{3,2},{4,5},{5,4},{6,7},{7,6},{8,9},{9,8},{10,11... | collective-permute-start | bytes 1572872 | tf_op jit(solution)/shard_map/ppermute | solution.py:235
  52.6 2.1 %collective-permute-done.1 = bf16[8,128,256]{2,1,0:T(8,128)(2,1)S(1)} collective-permute-done((bf16[8,128,256]{2,1,0:T(8,128)(2,1)}, bf16[8,128,256]{2,1,0:T(8,128)(2,1)S(1)}, u32[]{:S(2)}, u32[]{:S(2)}) %collective-permute-start.1) | collective-permute-done | bytes 524320 | tf_op jit(solution)/shard_map/ppermute | solution.py:235
  54.7 1.2 add_convert_fusion
  55.9 3.4 %collective-permute-start.2 = (bf16[4,128,256]{2,1,0:T(8,128)(2,1)S(1)}, bf16[4,128,256]{2,1,0:T(8,128)(2,1)S(1)}, u32[]{:S(2)}, u32[]{:S(2)}) collective-permute-start(bf16[4,128,256]{2,1,0:T(8,128)(2,1)S(1)} %slice.25), channel_id=1, source_target_pairs={{0,2},{2,0},{4,6},{6,4},{8,10},{10,8},{12,14},{14,12},{1,3},{3,1},... | collective-permute-start | bytes 786440 | tf_op jit(solution)/shard_map/ppermute | solution.py:230
  59.3 0.0 copy-done.1
  59.3 4.9 %shard_map.120 = bf16[128,768]{1,0:T(8,128)(2,1)} custom-call(s32[3]{0:T(128)S(1)} %pad_add_fusion.place_ref, s32[1,64]{1,0:T(1,128)S(1)} %copy-done.6, bf16[64,128,128]{2,1,0:T(8,128)(2,1)S(1)} %copy-done.1, bf16[8,128,256]{2,1,0:T(8,128)(2,1)S(1)} %all-to-all-done.own_ref, bf16[8,128,256]{2,1,0:T(8,128)(2,1)S(1)} %collective-permute-done.other_ref), custom_call_target="tpu_custom_call" | custom-call | flops 805306368 | bytes 4194304 | tf_op jit(solution)/shard_map/pallas_call | solution.py:217
  64.2 0.0 copy-start.10
  64.2 0.0 copy-start.11
  64.2 1.9 %collective-permute-done.2 = bf16[4,128,256]{2,1,0:T(8,128)(2,1)S(1)} collective-permute-done((bf16[4,128,256]{2,1,0:T(8,128)(2,1)S(1)}, bf16[4,128,256]{2,1,0:T(8,128)(2,1)S(1)}, u32[]{:S(2)}, u32[]{:S(2)}) %collective-permute-start.2) | collective-permute-done | bytes 262176 | tf_op jit(solution)/shard_map/ppermute | solution.py:230
  66.2 0.1 add_convert_fusion.1
  66.2 14.9 %all-to-all-done.1 = bf16[8,8,128,128]{3,2,1,0:T(8,128)(2,1)} async-done(((bf16[8,8,128,128]{3,2,1,0:T(8,128)(2,1)}), bf16[8,8,128,128]{3,2,1,0:T(8,128)(2,1)}, u32[]{:S(2)}, u32[]{:S(2)}) %all-to-all-start.1) | async-done | bytes 2097184 | tf_op jit(solution)/shard_map/all_to_all | solution.py:186
  81.1 2.0 %reduce_sum.23 = bf16[8,128,128]{2,1,0:T(8,128)(2,1)S(1)} reduce(bf16[8,8,128,128]{3,2,1,0:T(8,128)(2,1)} %all-to-all-done.1, bf16[]{:T(256)} %constant.26.clone.1), dimensions={0}, to_apply=%region_0.0 | reduce | flops 917504 | bytes 2359298 | tf_op jit(solution)/shard_map/reduce_sum | solution.py:243
  83.1 18.0 %all_to_all.25 = bf16[8,128,128]{2,1,0:T(8,128)(2,1)S(1)} all-to-all(bf16[8,128,128]{2,1,0:T(8,128)(2,1)S(1)} %reduce_sum.23), channel_id=1, replica_groups={{0,16,32,48,64,80,96,112},{2,18,34,50,66,82,98,114},{4,20,36,52,68,84,1..., dimensions={0} | all-to-all | bytes 524288 | tf_op jit(solution)/shard_map/all_to_all | solution.py:186
  101.1 0.0 copy-done.10
  101.1 0.0 copy-done.11
  101.1 0.1 fusion.2
  101.3 12.9 %all_to_all.26 = bf16[8,128,128]{2,1,0:T(8,128)(2,1)S(1)} all-to-all(bf16[8,128,128]{2,1,0:T(8,128)(2,1)S(1)} %broadcast_in_dim.13), channel_id=1, replica_groups={{0,16,32,48,64,80,96,112},{2,18,34,50,66,82,98,114},{4,20,36,52,68,84,1..., dimensions={0} | all-to-all | bytes 524288 | tf_op jit(solution)/shard_map/all_to_all | solution.py:186
  114.1 1.8 %broadcast_in_dim.14 = bf16[8,8,128,128]{3,2,1,0:T(8,128)(2,1)} broadcast(bf16[8,128,128]{2,1,0:T(8,128)(2,1)S(1)} %all_to_all.26), dimensions={1,2,3} | broadcast | bytes 2359296 | tf_op jit(solution)/shard_map/broadcast_in_dim | solution.py:251
  116.0 3.6 %all-to-all-start.4 = ((bf16[8,8,128,128]{3,2,1,0:T(8,128)(2,1)}), bf16[8,8,128,128]{3,2,1,0:T(8,128)(2,1)S(1)}, u32[]{:S(2)}, u32[]{:S(2)}) async-start(bf16[8,8,128,128]{3,2,1,0:T(8,128)(2,1)} %broadcast_in_dim.14), calls=%async_computation.4 | async-start | bytes 4194304 | tf_op jit(solution)/shard_map/all_to_all | solution.py:186
  119.6 1.9 %collective-permute-start.3 = (bf16[2,128,256]{2,1,0:T(8,128)(2,1)S(1)}, bf16[2,128,256]{2,1,0:T(8,128)(2,1)S(1)}, u32[]{:S(2)}, u32[]{:S(2)}) collective-permute-start(bf16[2,128,256]{2,1,0:T(8,128)(2,1)S(1)} %slice.21), channel_id=1, source_target_pairs={{0,4},{2,6},{4,0},{6,2},{8,12},{10,14},{12,8},{14,10},{1,5},{3,7},... | collective-permute-start | bytes 393224 | tf_op jit(solution)/shard_map/ppermute | solution.py:230
  121.5 6.4 %collective-permute-done.3 = bf16[2,128,256]{2,1,0:T(8,128)(2,1)S(1)} collective-permute-done((bf16[2,128,256]{2,1,0:T(8,128)(2,1)S(1)}, bf16[2,128,256]{2,1,0:T(8,128)(2,1)S(1)}, u32[]{:S(2)}, u32[]{:S(2)}) %collective-permute-start.3) | collective-permute-done | bytes 131104 | tf_op jit(solution)/shard_map/ppermute | solution.py:230
  128.0 2.9 %collective-permute-start.4 = (bf16[1,128,256]{2,1,0:T(8,128)(2,1)S(1)}, bf16[1,128,256]{2,1,0:T(8,128)(2,1)S(1)}, u32[]{:S(2)}, u32[]{:S(2)}) collective-permute-start(bf16[1,128,256]{2,1,0:T(8,128)(2,1)S(1)} %slice.27), channel_id=1, source_target_pairs={{0,8},{2,10},{4,12},{6,14},{8,0},{10,2},{12,4},{14,6},{1,9},{3,11}... | collective-permute-start | bytes 196616 | tf_op jit(solution)/shard_map/ppermute | solution.py:230
  130.9 7.5 %collective-permute-done.4 = bf16[1,128,256]{2,1,0:T(8,128)(2,1)S(1)} collective-permute-done((bf16[1,128,256]{2,1,0:T(8,128)(2,1)S(1)}, bf16[1,128,256]{2,1,0:T(8,128)(2,1)S(1)}, u32[]{:S(2)}, u32[]{:S(2)}) %collective-permute-start.4) | collective-permute-done | bytes 65568 | tf_op jit(solution)/shard_map/ppermute | solution.py:230
  138.4 0.6 fusion.8
  139.0 0.7 add_divide_fusion
  139.7 10.1 %all-to-all-done.4 = bf16[8,8,128,128]{3,2,1,0:T(8,128)(2,1)S(1)} async-done(((bf16[8,8,128,128]{3,2,1,0:T(8,128)(2,1)}), bf16[8,8,128,128]{3,2,1,0:T(8,128)(2,1)S(1)}, u32[]{:S(2)}, u32[]{:S(2)}) %all-to-all-start.4) | async-done | bytes 2097184 | tf_op jit(solution)/shard_map/all_to_all | solution.py:186
  149.8 2.4 %shard_map.121 = bf16[64,128,128]{2,1,0:T(8,128)(2,1)} custom-call(s32[3]{0:T(128)S(1)} %pad_add_fusion.place_ref, s32[1,64]{1,0:T(1,128)S(1)} %copy-done.8, bf16[64,128,128]{2,1,0:T(8,128)(2,1)S(1)} %bitcast.20), custom_call_target="tpu_custom_call" | custom-call | bytes 4194304 | tf_op jit(solution)/shard_map/pallas_call | solution.py:252
  (13 shorter events, 0.2 us)
Async XLA Ops:
  2.3 33.5 %copy-start.4 = (bf16[128,768]{1,0:T(8,128)(2,1)S(1)}, bf16[128,768]{1,0:T(8,128)(2,1)}, u32[]{:S(2)}) copy-start(bf16[128,768]{1,0:T(8,128)(2,1)} %hid_ref.3) | copy-start | bytes 589828
  2.3 33.5 %copy-start.6 = (s32[1,64]{1,0:T(1,128)S(1)}, s32[1,64]{1,0:T(1,128)}, u32[]{:S(2)}) copy-start(s32[1,64]{1,0:T(1,128)} %pos_ref.5) | copy-start | bytes 772
  2.3 33.5 %copy-start.8 = (s32[1,64]{1,0:T(1,128)S(1)}, s32[1,64]{1,0:T(1,128)}, u32[]{:S(2)}) copy-start(s32[1,64]{1,0:T(1,128)} %rank_ref.5) | copy-start | bytes 772
  2.3 29.7 %all-to-all-start = ((bf16[8,128,256]{2,1,0:T(8,128)(2,1)}), bf16[8,128,256]{2,1,0:T(8,128)(2,1)S(1)}, u32[]{:S(2)}, u32[]{:S(2)}) async-start(bf16[8,128,256]{2,1,0:T(8,128)(2,1)} %broadcast_in_dim.12), calls=%async_computation | async-start | bytes 1048576 | tf_op jit(solution)/shard_map/all_to_all | solution.py:188
  20.2 1.6 %copy-start = (bf16[64,128,128]{2,1,0:T(8,128)(2,1)S(1)}, bf16[64,128,128]{2,1,0:T(8,128)(2,1)}, u32[]{:S(2)}) copy-start(bf16[64,128,128]{2,1,0:T(8,128)(2,1)} %blocks_ref.3) | copy-start | bytes 6291460
  21.8 0.9 copy-start.3
  22.8 0.7 copy-start.5
  23.4 0.7 copy-start.7
  27.6 0.8 copy-start.2
  28.4 0.8 copy-start.9
  32.0 3.8 %collective-permute-start = (bf16[8,128,256]{2,1,0:T(8,128)(2,1)S(1)}, bf16[8,128,256]{2,1,0:T(8,128)(2,1)S(1)}, u32[]{:S(2)}, u32[]{:S(2)}) collective-permute-start(bf16[8,128,256]{2,1,0:T(8,128)(2,1)S(1)} %all-to-all-done.own_ref), channel_id=1, source_target_pairs={{0,1},{1,0},{2,3},{3,2},{4,5},{5,4},{6,7},{7,6},{8,9},{9,8},{10,11... | collective-permute-start | bytes 1572872 | tf_op jit(solution)/shard_map/ppermute | solution.py:199
  40.1 19.2 %copy-start.1 = (bf16[64,128,128]{2,1,0:T(8,128)(2,1)S(1)}, bf16[64,128,128]{2,1,0:T(8,128)(2,1)}, u32[]{:S(2)}) copy-start(bf16[64,128,128]{2,1,0:T(8,128)(2,1)} %blocks_ref.3) | copy-start | bytes 6291460
  40.1 41.0 %all-to-all-start.1 = ((bf16[8,8,128,128]{3,2,1,0:T(8,128)(2,1)}), bf16[8,8,128,128]{3,2,1,0:T(8,128)(2,1)}, u32[]{:S(2)}, u32[]{:S(2)}) async-start(bf16[8,8,128,128]{3,2,1,0:T(8,128)(2,1)} %bitcast.3), calls=%async_computation.1 | async-start | bytes 4194304 | tf_op jit(solution)/shard_map/all_to_all | solution.py:186
  50.7 4.0 %collective-permute-start.1 = (bf16[8,128,256]{2,1,0:T(8,128)(2,1)}, bf16[8,128,256]{2,1,0:T(8,128)(2,1)S(1)}, u32[]{:S(2)}, u32[]{:S(2)}) collective-permute-start(bf16[8,128,256]{2,1,0:T(8,128)(2,1)} %copy-done.9), channel_id=1, source_target_pairs={{0,1},{1,0},{2,3},{3,2},{4,5},{5,4},{6,7},{7,6},{8,9},{9,8},{10,11... | collective-permute-start | bytes 1572872 | tf_op jit(solution)/shard_map/ppermute | solution.py:235
  55.9 10.2 %collective-permute-start.2 = (bf16[4,128,256]{2,1,0:T(8,128)(2,1)S(1)}, bf16[4,128,256]{2,1,0:T(8,128)(2,1)S(1)}, u32[]{:S(2)}, u32[]{:S(2)}) collective-permute-start(bf16[4,128,256]{2,1,0:T(8,128)(2,1)S(1)} %slice.25), channel_id=1, source_target_pairs={{0,2},{2,0},{4,6},{6,4},{8,10},{10,8},{12,14},{14,12},{1,3},{3,1},... | collective-permute-start | bytes 786440 | tf_op jit(solution)/shard_map/ppermute | solution.py:230
  64.2 36.9 %copy-start.10 = (f32[1,1,128,128]{3,2,1,0:T(8,128)S(1)}, f32[1,1,128,128]{3,2,1,0:T(8,128)}, u32[]{:S(2)}) copy-start(f32[1,1,128,128]{3,2,1,0:T(8,128)} %param.13) | copy-start | bytes 196612
  64.2 36.9 %copy-start.11 = (f32[1,1,128,128]{3,2,1,0:T(8,128)S(1)}, f32[1,1,128,128]{3,2,1,0:T(8,128)}, u32[]{:S(2)}) copy-start(f32[1,1,128,128]{3,2,1,0:T(8,128)} %param.12) | copy-start | bytes 196612
  116.0 33.8 %all-to-all-start.4 = ((bf16[8,8,128,128]{3,2,1,0:T(8,128)(2,1)}), bf16[8,8,128,128]{3,2,1,0:T(8,128)(2,1)S(1)}, u32[]{:S(2)}, u32[]{:S(2)}) async-start(bf16[8,8,128,128]{3,2,1,0:T(8,128)(2,1)} %broadcast_in_dim.14), calls=%async_computation.4 | async-start | bytes 4194304 | tf_op jit(solution)/shard_map/all_to_all | solution.py:186
  119.6 8.4 %collective-permute-start.3 = (bf16[2,128,256]{2,1,0:T(8,128)(2,1)S(1)}, bf16[2,128,256]{2,1,0:T(8,128)(2,1)S(1)}, u32[]{:S(2)}, u32[]{:S(2)}) collective-permute-start(bf16[2,128,256]{2,1,0:T(8,128)(2,1)S(1)} %slice.21), channel_id=1, source_target_pairs={{0,4},{2,6},{4,0},{6,2},{8,12},{10,14},{12,8},{14,10},{1,5},{3,7},... | collective-permute-start | bytes 393224 | tf_op jit(solution)/shard_map/ppermute | solution.py:230
  128.0 10.4 %collective-permute-start.4 = (bf16[1,128,256]{2,1,0:T(8,128)(2,1)S(1)}, bf16[1,128,256]{2,1,0:T(8,128)(2,1)S(1)}, u32[]{:S(2)}, u32[]{:S(2)}) collective-permute-start(bf16[1,128,256]{2,1,0:T(8,128)(2,1)S(1)} %slice.27), channel_id=1, source_target_pairs={{0,8},{2,10},{4,12},{6,14},{8,0},{10,2},{12,4},{14,6},{1,9},{3,11}... | collective-permute-start | bytes 196616 | tf_op jit(solution)/shard_map/ppermute | solution.py:230

commit v4 on v3

--- a/solution.py
+++ b/solution.py
@@ -52,7 +52,7 @@
     lax.fori_loop(0, slots, place, 0, unroll=4)
 
 
-def partial_kernel(place_ref, pos_ref, rank_ref, hid_ref, blocks_ref, keep_ref, send_ref, mine_ref, slab):
+def partial_kernel(place_ref, pos_ref, rank_ref, hid_ref, blocks_ref, keep_ref, send_ref, mine_ref, hid_t_ref, slab):
     chips, _, feats = keep_ref.shape
     bits = chips.bit_length() - 1
     x, core = place_ref[0], place_ref[1]
@@ -63,6 +63,7 @@
 
     mine_ref[...] = blocks_ref[lax.fori_loop(0, blocks_ref.shape[0], find, 0)]
     hid = hid_ref[...]
+    hid_t_ref[...] = hid.T
     for i in range(chips):
         r = sum(((i >> b) & 1) << (bits - 1 - b) for b in range(bits))
         chip = x ^ r
@@ -86,12 +87,11 @@
     return jnp.where(core == 0, rank, (rank % side) * side + rank // side)
 
 
-def grads_kernel(side, factor, place_ref, pos_ref, rank_ref, hid_ref, own_ref, other_ref, out_ref, full, hid_t, made, sems, out_sems):
+def grads_kernel(side, factor, place_ref, pos_ref, rank_ref, hid_t, own_ref, other_ref, out_ref, full, made, sems, out_sems):
     slots, bs, _ = out_ref.shape
     col_blocks = full.shape[1] // bs
     core = place_ref[1]
     copies = join_features(core, own_ref, other_ref, full, sems)
-    hid_t[...] = hid_ref[...].T
     for copy in copies:
         copy.wait()
 
@@ -146,16 +146,10 @@
     def copy(s):
         return pltpu.make_async_copy(in_ref.at[place_of(rank_ref[0, s], core, side)], out_ref.at[s], sems.at[s])
 
-    def start(s, carry):
+    for s in range(slots):
         copy(s).start()
-        return carry
-
-    def wait(s, carry):
+    for s in range(slots):
         copy(s).wait()
-        return carry
-
-    lax.fori_loop(0, slots, start, 0, unroll=4)
-    lax.fori_loop(0, slots, wait, 0, unroll=4)
 
 
 def chip_groups(sizes):
@@ -186,11 +180,11 @@
         return lax.all_to_all(value, axes, 0, 0, axis_index_groups=groups, tiled=True)
 
     own = lax.all_to_all(jnp.broadcast_to(cotangent, (nx, tokens, feats)), "x", 0, 0, tiled=True)
-    keep, send, mine = call(
+    keep, send, mine, hid_t = call(
         partial_kernel,
-        (*(jax.ShapeDtypeStruct((nx, tokens, feats), BF),) * 2, jax.ShapeDtypeStruct((bs, bs), BF)),
+        (*(jax.ShapeDtypeStruct((nx, tokens, feats), BF),) * 2, jax.ShapeDtypeStruct((bs, bs), BF), jax.ShapeDtypeStruct((rows, tokens), BF)),
         [SMEM, SMEM, SMEM, VMEM, VMEM],
-        [VMEM] * 3,
+        [VMEM] * 4,
         [pltpu.VMEM((rows, width), BF)],
         flops=2 * tokens * rows * width,
         nbytes=4 * 2**20,
@@ -204,7 +198,6 @@
         ANY,
         [
             pltpu.VMEM((tokens, width), BF),
-            pltpu.VMEM((rows, tokens), BF),
             pltpu.VMEM((slots, bs, bs), BF),
             pltpu.SemaphoreType.DMA((2, nx)),
             pltpu.SemaphoreType.DMA((slots,)),
@@ -212,7 +205,7 @@
         flops=2 * tokens * bs * bs * slots,
         nbytes=4 * 2**20,
         limit=12,
-    )(place, block_pos, owner_rank, hidden, own, other)
+    )(place, block_pos, owner_rank, hid_t, own, other)
     grads, keep, send = lax.optimization_barrier((grads, keep, send))
     hidden_grad = call(
         back_kernel,
@@ -234,13 +227,13 @@
     got = exchange(grads.reshape(n0, slots // n0, bs, bs), first)
     total = (keep.astype(F32) + lax.ppermute(send, "core", swap).astype(F32)).astype(BF)
     total, hidden_grad = halved(total, 1, hidden_grad)
-    got, total = lax.optimization_barrier((got, total))
+    part = got.astype(F32).sum(axis=0).astype(BF)
+    part, total = lax.optimization_barrier((part, total))
     step = 2
     while total.shape[0] > 1:
         total, _ = halved(total, step)
         step *= 2
     mixed = total[0]
-    part = got.astype(F32).sum(axis=0).astype(BF)
     grad = exchange(part, then).astype(F32).sum(axis=0)
     weight = mine.astype(F32)
     mom_next = 0.9 * moment[0, 0] + 0.1 * grad

time: 153 us -> 153 us (level)
    unnamed x24 -> x22, local copies, waits for them, and re-layouts: 5.44 us -> 5.45 us
where the time goes in v4:
time: 153 us; the launch traced here: 152 us
  waiting for transfers between devices  47.6 us (31%)
  starting transfers between devices  44 us (29%)
  blocking collectives  30.9 us (20%)
  Pallas kernels  15.1 us (10%)
  local copies, waits for them, and re-layouts  9.01 us (6%)
  other arithmetic  4.75 us (3%)
    all_to_all x2, blocking collectives, exchange(): lax.all_to_all(value, axes, 0, 0, axis_index_groups=groups, tiled=True)  30.9 us
    all_to_all x2, waiting for transfers between devices, exchange(): lax.all_to_all(value, axes, 0, 0, axis_index_groups=groups, tiled=True)  24.9 us
    all_to_all x1, starting transfers between devices, shards(): lax.all_to_all(jnp.broadcast_to(cotangent, (nx, tokens, feats)), 'x', 0,...  17.9 us
    ppermute x3, waiting for transfers between devices, halved(): theirs = lax.ppermute(value[half:], 'x', [(i, i ^ step) for i in range(nx)])  15.9 us
    all_to_all x2, starting transfers between devices, exchange(): lax.all_to_all(value, axes, 0, 0, axis_index_groups=groups, tiled=True)  14.2 us
    ppermute x3, starting transfers between devices, halved(): theirs = lax.ppermute(value[half:], 'x', [(i, i ^ step) for i in range(nx)])  8.13 us
    unnamed x22, local copies, waits for them, and re-layouts  5.45 us
    pallas_call x1, Pallas kernels, shards(): call(back_kernel, jax.ShapeDtypeStruct((tokens, rows), BF), [SMEM, SMEM,...  4.9 us
  transfers between devices with their start and end apart: 8, of which 8 were waited for; matrix products, arithmetic and copies ran while one was open for 2% of the time, Pallas kernels for 6%

profile of v4, /device:TPU:2, one launch (start us, length us, event | category | flops | bytes accessed | tf_op | source)
XLA Modules:
  0.0 152.1 jit_solution(14757045600666608146)
XLA Ops:
  0.6 1.7 %broadcast_in_dim.12 = bf16[8,128,256]{2,1,0:T(8,128)(2,1)} broadcast(bf16[128,256]{1,0:T(8,128)(2,1)} %param.8), dimensions={1,2} | broadcast | bytes 589824 | tf_op jit(solution)/shard_map/broadcast_in_dim | solution.py:182
  2.3 0.0 copy-start.4
  2.3 0.0 copy-start.6
  2.3 17.9 %all-to-all-start = ((bf16[8,128,256]{2,1,0:T(8,128)(2,1)}), bf16[8,128,256]{2,1,0:T(8,128)(2,1)S(1)}, u32[]{:S(2)}, u32[]{:S(2)}) async-start(bf16[8,128,256]{2,1,0:T(8,128)(2,1)} %broadcast_in_dim.12), calls=%async_computation | async-start | bytes 1048576 | tf_op jit(solution)/shard_map/all_to_all | solution.py:182
  20.2 0.1 pad_add_fusion.place_ref
  20.2 1.6 %copy-done = bf16[64,128,128]{2,1,0:T(8,128)(2,1)S(1)} copy-done((bf16[64,128,128]{2,1,0:T(8,128)(2,1)S(1)}, bf16[64,128,128]{2,1,0:T(8,128)(2,1)}, u32[]{:S(2)}) %copy-start) | copy-done | bytes 2097176
  21.8 0.7 copy-done.3
  22.5 0.7 copy-done.5
  23.1 0.9 copy-done.8
  24.1 3.6 %shard_map.118 = (bf16[8,128,256]{2,1,0:T(8,128)(2,1)S(1)}, bf16[8,128,256]{2,1,0:T(8,128)(2,1)S(1)}, bf16[128,128]{1,0:T(8,128)(2,1)S(1)}, bf16[768,128]{1,0:T(8,128)(2,1)S(1)}) custom-call(s32[3]{0:T(128)S(1)} %pad_add_fusion.place_ref, s32[1,64]{1,0:T(1,128)S(1)} %copy-done.3, s32[1,64]{1,0:T(1,128)S(1)} %copy-done.5, bf16[128,768]{1,0:T(8,128)(2,1)S(1)} %copy-done.8, ...), custom_call_target="tpu_custom_call" | custom-call | flops 805306368 | bytes 4194304 | tf_op jit(solution)/shard_map/pallas_call | solution.py:183
  27.6 0.0 copy-start.2
  27.6 0.8 copy-done.2
  28.4 0.8 copy-done.7
  29.2 2.8 %all-to-all-done.own_ref = bf16[8,128,256]{2,1,0:T(8,128)(2,1)S(1)} async-done(((bf16[8,128,256]{2,1,0:T(8,128)(2,1)}), bf16[8,128,256]{2,1,0:T(8,128)(2,1)S(1)}, u32[]{:S(2)}, u32[]{:S(2)}) %all-to-all-start) | async-done | bytes 524320 | tf_op jit(solution)/shard_map/all_to_all | solution.py:182
  32.0 1.9 %collective-permute-start = (bf16[8,128,256]{2,1,0:T(8,128)(2,1)S(1)}, bf16[8,128,256]{2,1,0:T(8,128)(2,1)S(1)}, u32[]{:S(2)}, u32[]{:S(2)}) collective-permute-start(bf16[8,128,256]{2,1,0:T(8,128)(2,1)S(1)} %all-to-all-done.own_ref), channel_id=1, source_target_pairs={{0,1},{1,0},{2,3},{3,2},{4,5},{5,4},{6,7},{7,6},{8,9},{9,8},{10,11... | collective-permute-start | bytes 1572872 | tf_op jit(solution)/shard_map/ppermute | solution.py:193
  33.9 1.9 %collective-permute-done.other_ref = bf16[8,128,256]{2,1,0:T(8,128)(2,1)S(1)} collective-permute-done((bf16[8,128,256]{2,1,0:T(8,128)(2,1)S(1)}, bf16[8,128,256]{2,1,0:T(8,128)(2,1)S(1)}, u32[]{:S(2)}, u32[]{:S(2)}) %collective-permute-start) | collective-permute-done | bytes 524320 | tf_op jit(solution)/shard_map/ppermute | solution.py:193
  35.8 0.0 copy-done.4
  35.8 0.0 copy-done.6
  35.8 4.2 %shard_map.119 = bf16[64,128,128]{2,1,0:T(8,128)(2,1)} custom-call(s32[3]{0:T(128)S(1)} %pad_add_fusion.place_ref, s32[1,64]{1,0:T(1,128)S(1)} %copy-done.4, s32[1,64]{1,0:T(1,128)S(1)} %copy-done.6, bf16[768,128]{1,0:T(8,128)(2,1)S(1)} %get-tuple-element.20.hid_t, bf16[8,128,256]{2,1,0:T(8,128)(2,1)S(1)} %all-to-all-done.own_ref, ...), custom_call_target="tpu_custom_call" | custom-call | flops 268435456 | bytes 4194304 | tf_op jit(solution)/shard_map/pallas_call | solution.py:194
  40.0 0.0 copy-start.1
  40.1 10.6 %all-to-all-start.1 = ((bf16[8,8,128,128]{3,2,1,0:T(8,128)(2,1)}), bf16[8,8,128,128]{3,2,1,0:T(8,128)(2,1)}, u32[]{:S(2)}, u32[]{:S(2)}) async-start(bf16[8,8,128,128]{3,2,1,0:T(8,128)(2,1)} %bitcast.3), calls=%async_computation.1 | async-start | bytes 4194304 | tf_op jit(solution)/shard_map/all_to_all | solution.py:180
  50.7 1.9 %collective-permute-start.1 = (bf16[8,128,256]{2,1,0:T(8,128)(2,1)}, bf16[8,128,256]{2,1,0:T(8,128)(2,1)S(1)}, u32[]{:S(2)}, u32[]{:S(2)}) collective-permute-start(bf16[8,128,256]{2,1,0:T(8,128)(2,1)} %copy-done.7), channel_id=1, source_target_pairs={{0,1},{1,0},{2,3},{3,2},{4,5},{5,4},{6,7},{7,6},{8,9},{9,8},{10,11... | collective-permute-start | bytes 1572872 | tf_op jit(solution)/shard_map/ppermute | solution.py:228
  52.6 2.1 %collective-permute-done.1 = bf16[8,128,256]{2,1,0:T(8,128)(2,1)S(1)} collective-permute-done((bf16[8,128,256]{2,1,0:T(8,128)(2,1)}, bf16[8,128,256]{2,1,0:T(8,128)(2,1)S(1)}, u32[]{:S(2)}, u32[]{:S(2)}) %collective-permute-start.1) | collective-permute-done | bytes 524320 | tf_op jit(solution)/shard_map/ppermute | solution.py:228
  54.7 1.2 add_convert_fusion
  55.9 3.4 %collective-permute-start.2 = (bf16[4,128,256]{2,1,0:T(8,128)(2,1)S(1)}, bf16[4,128,256]{2,1,0:T(8,128)(2,1)S(1)}, u32[]{:S(2)}, u32[]{:S(2)}) collective-permute-start(bf16[4,128,256]{2,1,0:T(8,128)(2,1)S(1)} %slice.25), channel_id=1, source_target_pairs={{0,2},{2,0},{4,6},{6,4},{8,10},{10,8},{12,14},{14,12},{1,3},{3,1},... | collective-permute-start | bytes 786440 | tf_op jit(solution)/shard_map/ppermute | solution.py:223
  59.2 0.0 copy-done.1
  59.3 4.9 %shard_map.120 = bf16[128,768]{1,0:T(8,128)(2,1)} custom-call(s32[3]{0:T(128)S(1)} %pad_add_fusion.place_ref, s32[1,64]{1,0:T(1,128)S(1)} %copy-done.4, bf16[64,128,128]{2,1,0:T(8,128)(2,1)S(1)} %copy-done.1, bf16[8,128,256]{2,1,0:T(8,128)(2,1)S(1)} %all-to-all-done.own_ref, bf16[8,128,256]{2,1,0:T(8,128)(2,1)S(1)} %collective-permute-done.other_ref), custom_call_target="tpu_custom_call" | custom-call | flops 805306368 | bytes 4194304 | tf_op jit(solution)/shard_map/pallas_call | solution.py:210
  64.2 0.0 copy-start.9
  64.2 0.0 copy-start.10
  64.2 1.9 %collective-permute-done.2 = bf16[4,128,256]{2,1,0:T(8,128)(2,1)S(1)} collective-permute-done((bf16[4,128,256]{2,1,0:T(8,128)(2,1)S(1)}, bf16[4,128,256]{2,1,0:T(8,128)(2,1)S(1)}, u32[]{:S(2)}, u32[]{:S(2)}) %collective-permute-start.2) | collective-permute-done | bytes 262176 | tf_op jit(solution)/shard_map/ppermute | solution.py:223
  66.1 0.1 add_convert_fusion.1
  66.2 14.9 %all-to-all-done.1 = bf16[8,8,128,128]{3,2,1,0:T(8,128)(2,1)} async-done(((bf16[8,8,128,128]{3,2,1,0:T(8,128)(2,1)}), bf16[8,8,128,128]{3,2,1,0:T(8,128)(2,1)}, u32[]{:S(2)}, u32[]{:S(2)}) %all-to-all-start.1) | async-done | bytes 2097184 | tf_op jit(solution)/shard_map/all_to_all | solution.py:180
  81.1 2.0 %reduce_sum.23 = bf16[8,128,128]{2,1,0:T(8,128)(2,1)S(1)} reduce(bf16[8,8,128,128]{3,2,1,0:T(8,128)(2,1)} %all-to-all-done.1, bf16[]{:T(256)} %constant.11.clone.1), dimensions={0}, to_apply=%region_0.0 | reduce | flops 917504 | bytes 2359298 | tf_op jit(solution)/shard_map/reduce_sum | solution.py:230
  83.0 18.0 %all_to_all.25 = bf16[8,128,128]{2,1,0:T(8,128)(2,1)S(1)} all-to-all(bf16[8,128,128]{2,1,0:T(8,128)(2,1)S(1)} %reduce_sum.23), channel_id=1, replica_groups={{0,16,32,48,64,80,96,112},{2,18,34,50,66,82,98,114},{4,20,36,52,68,84,1..., dimensions={0} | all-to-all | bytes 524288 | tf_op jit(solution)/shard_map/all_to_all | solution.py:180
  101.1 0.0 copy-done.9
  101.1 0.0 copy-done.10
  101.1 0.1 fusion.2
  101.2 12.9 %all_to_all.26 = bf16[8,128,128]{2,1,0:T(8,128)(2,1)S(1)} all-to-all(bf16[8,128,128]{2,1,0:T(8,128)(2,1)S(1)} %broadcast_in_dim.13), channel_id=1, replica_groups={{0,16,32,48,64,80,96,112},{2,18,34,50,66,82,98,114},{4,20,36,52,68,84,1..., dimensions={0} | all-to-all | bytes 524288 | tf_op jit(solution)/shard_map/all_to_all | solution.py:180
  114.1 1.8 %broadcast_in_dim.14 = bf16[8,8,128,128]{3,2,1,0:T(8,128)(2,1)} broadcast(bf16[8,128,128]{2,1,0:T(8,128)(2,1)S(1)} %all_to_all.26), dimensions={1,2,3} | broadcast | bytes 2359296 | tf_op jit(solution)/shard_map/broadcast_in_dim | solution.py:244
  115.9 3.6 %all-to-all-start.4 = ((bf16[8,8,128,128]{3,2,1,0:T(8,128)(2,1)}), bf16[8,8,128,128]{3,2,1,0:T(8,128)(2,1)S(1)}, u32[]{:S(2)}, u32[]{:S(2)}) async-start(bf16[8,8,128,128]{3,2,1,0:T(8,128)(2,1)} %broadcast_in_dim.14), calls=%async_computation.4 | async-start | bytes 4194304 | tf_op jit(solution)/shard_map/all_to_all | solution.py:180
  119.5 1.9 %collective-permute-start.3 = (bf16[2,128,256]{2,1,0:T(8,128)(2,1)S(1)}, bf16[2,128,256]{2,1,0:T(8,128)(2,1)S(1)}, u32[]{:S(2)}, u32[]{:S(2)}) collective-permute-start(bf16[2,128,256]{2,1,0:T(8,128)(2,1)S(1)} %slice.21), channel_id=1, source_target_pairs={{0,4},{2,6},{4,0},{6,2},{8,12},{10,14},{12,8},{14,10},{1,5},{3,7},... | collective-permute-start | bytes 393224 | tf_op jit(solution)/shard_map/ppermute | solution.py:223
  121.5 6.4 %collective-permute-done.3 = bf16[2,128,256]{2,1,0:T(8,128)(2,1)S(1)} collective-permute-done((bf16[2,128,256]{2,1,0:T(8,128)(2,1)S(1)}, bf16[2,128,256]{2,1,0:T(8,128)(2,1)S(1)}, u32[]{:S(2)}, u32[]{:S(2)}) %collective-permute-start.3) | collective-permute-done | bytes 131104 | tf_op jit(solution)/shard_map/ppermute | solution.py:223
  128.0 2.8 %collective-permute-start.4 = (bf16[1,128,256]{2,1,0:T(8,128)(2,1)S(1)}, bf16[1,128,256]{2,1,0:T(8,128)(2,1)S(1)}, u32[]{:S(2)}, u32[]{:S(2)}) collective-permute-start(bf16[1,128,256]{2,1,0:T(8,128)(2,1)S(1)} %slice.27), channel_id=1, source_target_pairs={{0,8},{2,10},{4,12},{6,14},{8,0},{10,2},{12,4},{14,6},{1,9},{3,11}... | collective-permute-start | bytes 196616 | tf_op jit(solution)/shard_map/ppermute | solution.py:223
  130.8 7.5 %collective-permute-done.4 = bf16[1,128,256]{2,1,0:T(8,128)(2,1)S(1)} collective-permute-done((bf16[1,128,256]{2,1,0:T(8,128)(2,1)S(1)}, bf16[1,128,256]{2,1,0:T(8,128)(2,1)S(1)}, u32[]{:S(2)}, u32[]{:S(2)}) %collective-permute-start.4) | collective-permute-done | bytes 65568 | tf_op jit(solution)/shard_map/ppermute | solution.py:223
  138.3 0.6 fusion.8
  139.0 0.7 add_divide_fusion
  139.7 10.1 %all-to-all-done.4 = bf16[8,8,128,128]{3,2,1,0:T(8,128)(2,1)S(1)} async-done(((bf16[8,8,128,128]{3,2,1,0:T(8,128)(2,1)}), bf16[8,8,128,128]{3,2,1,0:T(8,128)(2,1)S(1)}, u32[]{:S(2)}, u32[]{:S(2)}) %all-to-all-start.4) | async-done | bytes 2097184 | tf_op jit(solution)/shard_map/all_to_all | solution.py:180
  149.7 2.4 %shard_map.121 = bf16[64,128,128]{2,1,0:T(8,128)(2,1)} custom-call(s32[3]{0:T(128)S(1)} %pad_add_fusion.place_ref, s32[1,64]{1,0:T(1,128)S(1)} %copy-done.6, bf16[64,128,128]{2,1,0:T(8,128)(2,1)S(1)} %bitcast.20), custom_call_target="tpu_custom_call" | custom-call | bytes 4194304 | tf_op jit(solution)/shard_map/pallas_call | solution.py:245
  (11 shorter events, 0.2 us)
Async XLA Ops:
  2.3 33.5 %copy-start.4 = (s32[1,64]{1,0:T(1,128)S(1)}, s32[1,64]{1,0:T(1,128)}, u32[]{:S(2)}) copy-start(s32[1,64]{1,0:T(1,128)} %pos_ref.5) | copy-start | bytes 772
  2.3 33.5 %copy-start.6 = (s32[1,64]{1,0:T(1,128)S(1)}, s32[1,64]{1,0:T(1,128)}, u32[]{:S(2)}) copy-start(s32[1,64]{1,0:T(1,128)} %rank_ref.5) | copy-start | bytes 772
  2.3 29.7 %all-to-all-start = ((bf16[8,128,256]{2,1,0:T(8,128)(2,1)}), bf16[8,128,256]{2,1,0:T(8,128)(2,1)S(1)}, u32[]{:S(2)}, u32[]{:S(2)}) async-start(bf16[8,128,256]{2,1,0:T(8,128)(2,1)} %broadcast_in_dim.12), calls=%async_computation | async-start | bytes 1048576 | tf_op jit(solution)/shard_map/all_to_all | solution.py:182
  20.2 1.6 %copy-start = (bf16[64,128,128]{2,1,0:T(8,128)(2,1)S(1)}, bf16[64,128,128]{2,1,0:T(8,128)(2,1)}, u32[]{:S(2)}) copy-start(bf16[64,128,128]{2,1,0:T(8,128)(2,1)} %blocks_ref.3) | copy-start | bytes 6291460
  21.8 0.7 copy-start.3
  22.5 0.7 copy-start.5
  23.1 0.9 copy-start.8
  27.6 0.8 copy-start.2
  28.4 0.8 copy-start.7
  32.0 3.8 %collective-permute-start = (bf16[8,128,256]{2,1,0:T(8,128)(2,1)S(1)}, bf16[8,128,256]{2,1,0:T(8,128)(2,1)S(1)}, u32[]{:S(2)}, u32[]{:S(2)}) collective-permute-start(bf16[8,128,256]{2,1,0:T(8,128)(2,1)S(1)} %all-to-all-done.own_ref), channel_id=1, source_target_pairs={{0,1},{1,0},{2,3},{3,2},{4,5},{5,4},{6,7},{7,6},{8,9},{9,8},{10,11... | collective-permute-start | bytes 1572872 | tf_op jit(solution)/shard_map/ppermute | solution.py:193
  40.0 19.2 %copy-start.1 = (bf16[64,128,128]{2,1,0:T(8,128)(2,1)S(1)}, bf16[64,128,128]{2,1,0:T(8,128)(2,1)}, u32[]{:S(2)}) copy-start(bf16[64,128,128]{2,1,0:T(8,128)(2,1)} %blocks_ref.3) | copy-start | bytes 6291460
  40.1 41.0 %all-to-all-start.1 = ((bf16[8,8,128,128]{3,2,1,0:T(8,128)(2,1)}), bf16[8,8,128,128]{3,2,1,0:T(8,128)(2,1)}, u32[]{:S(2)}, u32[]{:S(2)}) async-start(bf16[8,8,128,128]{3,2,1,0:T(8,128)(2,1)} %bitcast.3), calls=%async_computation.1 | async-start | bytes 4194304 | tf_op jit(solution)/shard_map/all_to_all | solution.py:180
  50.7 4.0 %collective-permute-start.1 = (bf16[8,128,256]{2,1,0:T(8,128)(2,1)}, bf16[8,128,256]{2,1,0:T(8,128)(2,1)S(1)}, u32[]{:S(2)}, u32[]{:S(2)}) collective-permute-start(bf16[8,128,256]{2,1,0:T(8,128)(2,1)} %copy-done.7), channel_id=1, source_target_pairs={{0,1},{1,0},{2,3},{3,2},{4,5},{5,4},{6,7},{7,6},{8,9},{9,8},{10,11... | collective-permute-start | bytes 1572872 | tf_op jit(solution)/shard_map/ppermute | solution.py:228
  55.9 10.2 %collective-permute-start.2 = (bf16[4,128,256]{2,1,0:T(8,128)(2,1)S(1)}, bf16[4,128,256]{2,1,0:T(8,128)(2,1)S(1)}, u32[]{:S(2)}, u32[]{:S(2)}) collective-permute-start(bf16[4,128,256]{2,1,0:T(8,128)(2,1)S(1)} %slice.25), channel_id=1, source_target_pairs={{0,2},{2,0},{4,6},{6,4},{8,10},{10,8},{12,14},{14,12},{1,3},{3,1},... | collective-permute-start | bytes 786440 | tf_op jit(solution)/shard_map/ppermute | solution.py:223
  64.2 36.9 %copy-start.9 = (f32[1,1,128,128]{3,2,1,0:T(8,128)S(1)}, f32[1,1,128,128]{3,2,1,0:T(8,128)}, u32[]{:S(2)}) copy-start(f32[1,1,128,128]{3,2,1,0:T(8,128)} %param.13) | copy-start | bytes 196612
  64.2 36.9 %copy-start.10 = (f32[1,1,128,128]{3,2,1,0:T(8,128)S(1)}, f32[1,1,128,128]{3,2,1,0:T(8,128)}, u32[]{:S(2)}) copy-start(f32[1,1,128,128]{3,2,1,0:T(8,128)} %param.12) | copy-start | bytes 196612
  115.9 33.8 %all-to-all-start.4 = ((bf16[8,8,128,128]{3,2,1,0:T(8,128)(2,1)}), bf16[8,8,128,128]{3,2,1,0:T(8,128)(2,1)S(1)}, u32[]{:S(2)}, u32[]{:S(2)}) async-start(bf16[8,8,128,128]{3,2,1,0:T(8,128)(2,1)} %broadcast_in_dim.14), calls=%async_computation.4 | async-start | bytes 4194304 | tf_op jit(solution)/shard_map/all_to_all | solution.py:180
  119.5 8.4 %collective-permute-start.3 = (bf16[2,128,256]{2,1,0:T(8,128)(2,1)S(1)}, bf16[2,128,256]{2,1,0:T(8,128)(2,1)S(1)}, u32[]{:S(2)}, u32[]{:S(2)}) collective-permute-start(bf16[2,128,256]{2,1,0:T(8,128)(2,1)S(1)} %slice.21), channel_id=1, source_target_pairs={{0,4},{2,6},{4,0},{6,2},{8,12},{10,14},{12,8},{14,10},{1,5},{3,7},... | collective-permute-start | bytes 393224 | tf_op jit(solution)/shard_map/ppermute | solution.py:223
  128.0 10.3 %collective-permute-start.4 = (bf16[1,128,256]{2,1,0:T(8,128)(2,1)S(1)}, bf16[1,128,256]{2,1,0:T(8,128)(2,1)S(1)}, u32[]{:S(2)}, u32[]{:S(2)}) collective-permute-start(bf16[1,128,256]{2,1,0:T(8,128)(2,1)S(1)} %slice.27), channel_id=1, source_target_pairs={{0,8},{2,10},{4,12},{6,14},{8,0},{10,2},{12,4},{14,6},{1,9},{3,11}... | collective-permute-start | bytes 196616 | tf_op jit(solution)/shard_map/ppermute | solution.py:223

commit v5 on v4

--- a/solution.py
+++ b/solution.py
@@ -15,6 +15,7 @@
 ANY = pl.BlockSpec(memory_space=pl.ANY)
 BF = jnp.bfloat16
 F32 = jnp.float32
+SHIFTS = (0, 5, 2, 6, 1, 7, 4, 3)
 
 
 def call(kernel, out_shape, ins, outs, scratch=(), flops=0, nbytes=0, limit=24):
@@ -139,17 +140,21 @@
         ).astype(BF)
 
 
-def list_kernel(side, place_ref, rank_ref, in_ref, out_ref, sems):
-    core = place_ref[1]
-    slots = out_ref.shape[0]
-
-    def copy(s):
-        return pltpu.make_async_copy(in_ref.at[place_of(rank_ref[0, s], core, side)], out_ref.at[s], sems.at[s])
-
-    for s in range(slots):
-        copy(s).start()
-    for s in range(slots):
-        copy(s).wait()
+def list_kernel(side, shifts, place_ref, rank_ref, *refs):
+    rows, (out_ref, slot_of, sems) = refs[:-3], refs[-3:]
+    core, along = place_ref[1], place_ref[3]
+    for s in range(out_ref.shape[0]):
+        slot_of[rank_ref[0, s]] = s
+    copies = []
+    for k, row_ref in enumerate(rows):
+        j = (along + side - shifts[k]) % side
+        for i in range(row_ref.shape[0]):
+            rank = jnp.where(core == 0, j * side + i, i * side + j)
+            copies.append(pltpu.make_async_copy(row_ref.at[i], out_ref.at[slot_of[rank]], sems.at[k, i]))
+    for copy in copies:
+        copy.start()
+    for copy in copies:
+        copy.wait()
 
 
 def chip_groups(sizes):
@@ -161,6 +166,19 @@
     along_0 = lambda c: [[at(z, y, x, c) for z in range(n0)] for y in range(n1) for x in range(nx)]
     along_1 = lambda c: [[at(z, y, x, c) for y in range(n1)] for z in range(n0) for x in range(nx)]
     return along_0(0) + along_1(1), along_1(0) + along_0(1)
+
+
+def ring_shift(sizes, k):
+    n0, n1, nx, nc = sizes
+    pairs = []
+    for z in range(n0):
+        for y in range(n1):
+            to = ((z + k) % n0, y), (z, (y + k) % n1)
+            for x in range(nx):
+                for c in range(nc):
+                    there = (to[c][0] * n1 + to[c][1]) * nx + x
+                    pairs.append((((z * n1 + y) * nx + x) * nc + c, there * nc + c))
+    return pairs
 
 
 def shards(sizes, hidden, cotangent, blocks, block_pos, owner_rank, moment, second):
@@ -171,7 +189,8 @@
     width = feats * nx * nc
     axes = (*DP, *TENSOR)
     first, then = chip_groups(sizes)
-    place = jnp.stack([lax.axis_index("x"), lax.axis_index("core"), lax.axis_index(DP)])
+    along = jnp.where(lax.axis_index("core") == 0, lax.axis_index(DP[0]), lax.axis_index(DP[1]))
+    place = jnp.stack([lax.axis_index("x"), lax.axis_index("core"), lax.axis_index(DP), along])
     swap = [(0, 1), (1, 0)]
     factor = 1.0 / (tokens * n0 * n1)
     block_list = jax.ShapeDtypeStruct((slots, bs, bs), BF)
@@ -227,13 +246,10 @@
     got = exchange(grads.reshape(n0, slots // n0, bs, bs), first)
     total = (keep.astype(F32) + lax.ppermute(send, "core", swap).astype(F32)).astype(BF)
     total, hidden_grad = halved(total, 1, hidden_grad)
+    if total.shape[0] > 1:
+        total, _ = halved(total, 2)
     part = got.astype(F32).sum(axis=0).astype(BF)
     part, total = lax.optimization_barrier((part, total))
-    step = 2
-    while total.shape[0] > 1:
-        total, _ = halved(total, step)
-        step *= 2
-    mixed = total[0]
     grad = exchange(part, then).astype(F32).sum(axis=0)
     weight = mine.astype(F32)
     mom_next = 0.9 * moment[0, 0] + 0.1 * grad
@@ -241,16 +257,23 @@
     step_dir = mom_next / (jnp.sqrt(sec_next) + 1e-08)
     updated = (weight - 0.002 * (step_dir + 0.1 * weight)).astype(BF)
     row = exchange(jnp.broadcast_to(updated, (n1, bs, bs)), then)
-    every = exchange(jnp.broadcast_to(row, (n0, n1, bs, bs)), first)
+    row, total = lax.optimization_barrier((row, total))
+    step = 4
+    while total.shape[0] > 1:
+        total, _ = halved(total, step)
+        step *= 2
+    mixed = total[0]
+    shifts = SHIFTS if n0 == len(SHIFTS) else tuple(range(n0))
+    rows_from = [lax.ppermute(row, axes, ring_shift(sizes, k)) if k else row for k in shifts]
     new_blocks = call(
-        functools.partial(list_kernel, n0),
+        functools.partial(list_kernel, n0, shifts),
         block_list,
-        [SMEM, SMEM, ANY],
+        [SMEM, SMEM] + [ANY] * n0,
         ANY,
-        [pltpu.SemaphoreType.DMA((slots,))],
+        [pltpu.SMEM((slots,), jnp.int32), pltpu.SemaphoreType.DMA((n0, slots // n0))],
         nbytes=4 * 2**20,
         limit=4,
-    )(place, owner_rank, every.reshape(slots, bs, bs))
+    )(place, owner_rank, *rows_from)
     return (mixed, hidden_grad, mom_next[None, None], sec_next[None, None], step_dir[None, None], new_blocks)
 
 
@@ -282,4 +305,5 @@
 
 def solution(mesh):
     sizes = (8, mesh.shape["dp"] // 8, mesh.shape["tensor"] // 2, 2)
-    return make(sizes, Mesh(mesh.devices.reshape(sizes), (*DP, *TENSOR)))
+    step = make(sizes, Mesh(mesh.devices.reshape(sizes), (*DP, *TENSOR)))
+    return step

time: 153 us -> 153 us (level)
  starting transfers between devices: 44 us -> 67.3 us
  waiting for transfers between devices: 47.6 us -> 26.4 us
  local copies, waits for them, and re-layouts: 9.01 us -> 7.15 us
    ppermute x0 -> x7, starting transfers between devices: none -> 25.7 us  [shards(): lax.ppermute(row, axes, ring_shift(sizes, k))]
    all_to_all x2 -> x1, waiting for transfers between devices: 24.9 us -> 6.85 us  [exchange(): lax.all_to_all(value, axes, 0, 0, axis_index_groups=groups, tiled=True)]
    ppermute x3, waiting for transfers between devices: 15.9 us -> 7.76 us  [halved(): theirs = lax.ppermute(value[half:], 'x', [(i, i ^ step) for i in range(nx)])]
    ppermute x0 -> x7, waiting for transfers between devices: none -> 5.01 us  [shards(): lax.ppermute(row, axes, ring_shift(sizes, k))]
    all_to_all x2 -> x1, starting transfers between devices: 14.2 us -> 10.6 us  [exchange(): lax.all_to_all(value, axes, 0, 0, axis_index_groups=groups, tiled=True)]
    broadcast_in_dim x1 -> x0, local copies, waits for them, and re-layouts: 1.82 us -> none  [shards(): every = exchange(jnp.broadcast_to(row, (n0, n1, bs, bs)), first)]
  transfers between devices with their start and end apart: 8 -> 14, of which waited for: 8 -> 8; matrix products, arithmetic and copies ran while one was open for 2% -> 2% of each run, Pallas kernels for 6% -> 6%
where the time goes in v5:
time: 153 us
  starting transfers between devices  67.3 us (44%)
  blocking collectives  30.9 us (20%)
  waiting for transfers between devices  26.4 us (17%)
  Pallas kernels  15.1 us (10%)
  local copies, waits for them, and re-layouts  7.15 us (5%)
  other arithmetic  4.8 us (3%)
    all_to_all x2, blocking collectives, exchange(): lax.all_to_all(value, axes, 0, 0, axis_index_groups=groups, tiled=True)  30.9 us
    ppermute x7, starting transfers between devices, shards(): lax.ppermute(row, axes, ring_shift(sizes, k))  25.7 us
    all_to_all x1, starting transfers between devices, shards(): lax.all_to_all(jnp.broadcast_to(cotangent, (nx, tokens, feats)), 'x', 0,...  17.9 us
    all_to_all x1, starting transfers between devices, exchange(): lax.all_to_all(value, axes, 0, 0, axis_index_groups=groups, tiled=True)  10.6 us
    ppermute x3, starting transfers between devices, halved(): theirs = lax.ppermute(value[half:], 'x', [(i, i ^ step) for i in range(nx)])  9.33 us
    ppermute x3, waiting for transfers between devices, halved(): theirs = lax.ppermute(value[half:], 'x', [(i, i ^ step) for i in range(nx)])  7.76 us
    all_to_all x1, waiting for transfers between devices, exchange(): lax.all_to_all(value, axes, 0, 0, axis_index_groups=groups, tiled=True)  6.85 us
    unnamed x22, local copies, waits for them, and re-layouts  5.42 us
  transfers between devices with their start and end apart: 14, of which 8 were waited for; matrix products, arithmetic and copies ran while one was open for 2% of the time, Pallas kernels for 6%

profile of v5, /device:TPU:2, one launch (start us, length us, event | category | flops | bytes accessed | tf_op | source)
XLA Modules:
  0.0 152.5 jit_solution(13396202471214500279)
XLA Ops:
  0.6 1.7 %broadcast_in_dim.4 = bf16[8,128,256]{2,1,0:T(8,128)(2,1)} broadcast(bf16[128,256]{1,0:T(8,128)(2,1)} %param.8), dimensions={1,2} | broadcast | bytes 589824 | tf_op jit(solution)/shard_map/broadcast_in_dim | solution.py:201
  2.3 17.9 %all-to-all-start = ((bf16[8,128,256]{2,1,0:T(8,128)(2,1)}), bf16[8,128,256]{2,1,0:T(8,128)(2,1)S(1)}, u32[]{:S(2)}, u32[]{:S(2)}) async-start(bf16[8,128,256]{2,1,0:T(8,128)(2,1)} %broadcast_in_dim.4), calls=%async_computation | async-start | bytes 1048576 | tf_op jit(solution)/shard_map/all_to_all | solution.py:201
  20.2 0.1 pad_add_fusion.place_ref
  20.2 1.6 %copy-done = bf16[64,128,128]{2,1,0:T(8,128)(2,1)S(1)} copy-done((bf16[64,128,128]{2,1,0:T(8,128)(2,1)S(1)}, bf16[64,128,128]{2,1,0:T(8,128)(2,1)}, u32[]{:S(2)}) %copy-start) | copy-done | bytes 2097176
  21.8 0.7 copy-done.3
  22.5 0.7 copy-done.5
  23.1 0.9 copy-done.8
  24.1 3.6 %shard_map.118 = (bf16[8,128,256]{2,1,0:T(8,128)(2,1)S(1)}, bf16[8,128,256]{2,1,0:T(8,128)(2,1)S(1)}, bf16[128,128]{1,0:T(8,128)(2,1)S(1)}, bf16[768,128]{1,0:T(8,128)(2,1)S(1)}) custom-call(s32[4]{0:T(128)S(1)} %pad_add_fusion.place_ref, s32[1,64]{1,0:T(1,128)S(1)} %copy-done.3, s32[1,64]{1,0:T(1,128)S(1)} %copy-done.5, bf16[128,768]{1,0:T(8,128)(2,1)S(1)} %copy-done.8, ...), custom_call_target="tpu_custom_call" | custom-call | flops 805306368 | bytes 4194304 | tf_op jit(solution)/shard_map/pallas_call | solution.py:202
  27.6 0.8 copy-done.2
  28.4 0.8 copy-done.7
  29.2 2.8 %all-to-all-done.own_ref = bf16[8,128,256]{2,1,0:T(8,128)(2,1)S(1)} async-done(((bf16[8,128,256]{2,1,0:T(8,128)(2,1)}), bf16[8,128,256]{2,1,0:T(8,128)(2,1)S(1)}, u32[]{:S(2)}, u32[]{:S(2)}) %all-to-all-start) | async-done | bytes 524320 | tf_op jit(solution)/shard_map/all_to_all | solution.py:201
  32.0 1.9 %collective-permute-start = (bf16[8,128,256]{2,1,0:T(8,128)(2,1)S(1)}, bf16[8,128,256]{2,1,0:T(8,128)(2,1)S(1)}, u32[]{:S(2)}, u32[]{:S(2)}) collective-permute-start(bf16[8,128,256]{2,1,0:T(8,128)(2,1)S(1)} %all-to-all-done.own_ref), channel_id=1, source_target_pairs={{0,1},{1,0},{2,3},{3,2},{4,5},{5,4},{6,7},{7,6},{8,9},{9,8},{10,11... | collective-permute-start | bytes 1572872 | tf_op jit(solution)/shard_map/ppermute | solution.py:212
  33.9 1.9 %collective-permute-done.other_ref = bf16[8,128,256]{2,1,0:T(8,128)(2,1)S(1)} collective-permute-done((bf16[8,128,256]{2,1,0:T(8,128)(2,1)S(1)}, bf16[8,128,256]{2,1,0:T(8,128)(2,1)S(1)}, u32[]{:S(2)}, u32[]{:S(2)}) %collective-permute-start) | collective-permute-done | bytes 524320 | tf_op jit(solution)/shard_map/ppermute | solution.py:212
  35.8 4.2 %shard_map.119 = bf16[64,128,128]{2,1,0:T(8,128)(2,1)} custom-call(s32[4]{0:T(128)S(1)} %pad_add_fusion.place_ref, s32[1,64]{1,0:T(1,128)S(1)} %copy-done.4, s32[1,64]{1,0:T(1,128)S(1)} %copy-done.6, bf16[768,128]{1,0:T(8,128)(2,1)S(1)} %get-tuple-element.23.hid_t, bf16[8,128,256]{2,1,0:T(8,128)(2,1)S(1)} %all-to-all-done.own_ref, ...), custom_call_target="tpu_custom_call" | custom-call | flops 268435456 | bytes 4194304 | tf_op jit(solution)/shard_map/pallas_call | solution.py:213
  40.0 0.0 copy-start.1
  40.0 10.6 %all-to-all-start.1 = ((bf16[8,8,128,128]{3,2,1,0:T(8,128)(2,1)}), bf16[8,8,128,128]{3,2,1,0:T(8,128)(2,1)}, u32[]{:S(2)}, u32[]{:S(2)}) async-start(bf16[8,8,128,128]{3,2,1,0:T(8,128)(2,1)} %bitcast.5), calls=%async_computation.1 | async-start | bytes 4194304 | tf_op jit(solution)/shard_map/all_to_all | solution.py:199
  50.6 1.9 %collective-permute-start.1 = (bf16[8,128,256]{2,1,0:T(8,128)(2,1)}, bf16[8,128,256]{2,1,0:T(8,128)(2,1)S(1)}, u32[]{:S(2)}, u32[]{:S(2)}) collective-permute-start(bf16[8,128,256]{2,1,0:T(8,128)(2,1)} %copy-done.7), channel_id=1, source_target_pairs={{0,1},{1,0},{2,3},{3,2},{4,5},{5,4},{6,7},{7,6},{8,9},{9,8},{10,11... | collective-permute-start | bytes 1572872 | tf_op jit(solution)/shard_map/ppermute | solution.py:247
  52.6 2.1 %collective-permute-done.1 = bf16[8,128,256]{2,1,0:T(8,128)(2,1)S(1)} collective-permute-done((bf16[8,128,256]{2,1,0:T(8,128)(2,1)}, bf16[8,128,256]{2,1,0:T(8,128)(2,1)S(1)}, u32[]{:S(2)}, u32[]{:S(2)}) %collective-permute-start.1) | collective-permute-done | bytes 524320 | tf_op jit(solution)/shard_map/ppermute | solution.py:247
  54.6 1.2 add_convert_fusion
  55.9 3.4 %collective-permute-start.2 = (bf16[4,128,256]{2,1,0:T(8,128)(2,1)S(1)}, bf16[4,128,256]{2,1,0:T(8,128)(2,1)S(1)}, u32[]{:S(2)}, u32[]{:S(2)}) collective-permute-start(bf16[4,128,256]{2,1,0:T(8,128)(2,1)S(1)} %slice.25), channel_id=1, source_target_pairs={{0,2},{2,0},{4,6},{6,4},{8,10},{10,8},{12,14},{14,12},{1,3},{3,1},... | collective-permute-start | bytes 786440 | tf_op jit(solution)/shard_map/ppermute | solution.py:242
  59.3 4.9 %shard_map.120 = bf16[128,768]{1,0:T(8,128)(2,1)} custom-call(s32[4]{0:T(128)S(1)} %pad_add_fusion.place_ref, s32[1,64]{1,0:T(1,128)S(1)} %copy-done.4, bf16[64,128,128]{2,1,0:T(8,128)(2,1)S(1)} %copy-done.1, bf16[8,128,256]{2,1,0:T(8,128)(2,1)S(1)} %all-to-all-done.own_ref, bf16[8,128,256]{2,1,0:T(8,128)(2,1)S(1)} %collective-permute-done.other_ref), custom_call_target="tpu_custom_call" | custom-call | flops 805306368 | bytes 4194304 | tf_op jit(solution)/shard_map/pallas_call | solution.py:229
  64.2 1.9 %collective-permute-done.2 = bf16[4,128,256]{2,1,0:T(8,128)(2,1)S(1)} collective-permute-done((bf16[4,128,256]{2,1,0:T(8,128)(2,1)S(1)}, bf16[4,128,256]{2,1,0:T(8,128)(2,1)S(1)}, u32[]{:S(2)}, u32[]{:S(2)}) %collective-permute-start.2) | collective-permute-done | bytes 262176 | tf_op jit(solution)/shard_map/ppermute | solution.py:242
  66.1 0.1 add_convert_fusion.1
  66.2 0.0 copy-start.9
  66.2 0.0 copy-start.10
  66.2 2.1 %collective-permute-start.3 = (bf16[2,128,256]{2,1,0:T(8,128)(2,1)S(1)}, bf16[2,128,256]{2,1,0:T(8,128)(2,1)S(1)}, u32[]{:S(2)}, u32[]{:S(2)}) collective-permute-start(bf16[2,128,256]{2,1,0:T(8,128)(2,1)S(1)} %slice.27), channel_id=1, source_target_pairs={{0,4},{2,6},{4,0},{6,2},{8,12},{10,14},{12,8},{14,10},{1,5},{3,7},... | collective-permute-start | bytes 393224 | tf_op jit(solution)/shard_map/ppermute | solution.py:242
  68.3 5.8 %collective-permute-done.3 = bf16[2,128,256]{2,1,0:T(8,128)(2,1)S(1)} collective-permute-done((bf16[2,128,256]{2,1,0:T(8,128)(2,1)S(1)}, bf16[2,128,256]{2,1,0:T(8,128)(2,1)S(1)}, u32[]{:S(2)}, u32[]{:S(2)}) %collective-permute-start.3) | collective-permute-done | bytes 131104 | tf_op jit(solution)/shard_map/ppermute | solution.py:242
  74.2 6.8 %all-to-all-done.1 = bf16[8,8,128,128]{3,2,1,0:T(8,128)(2,1)} async-done(((bf16[8,8,128,128]{3,2,1,0:T(8,128)(2,1)}), bf16[8,8,128,128]{3,2,1,0:T(8,128)(2,1)}, u32[]{:S(2)}, u32[]{:S(2)}) %all-to-all-start.1) | async-done | bytes 2097184 | tf_op jit(solution)/shard_map/all_to_all | solution.py:199
  81.0 2.0 %reduce_sum.23 = bf16[8,128,128]{2,1,0:T(8,128)(2,1)S(1)} reduce(bf16[8,8,128,128]{3,2,1,0:T(8,128)(2,1)} %all-to-all-done.1, bf16[]{:T(256)} %constant.28.clone.1), dimensions={0}, to_apply=%region_0.1 | reduce | flops 917504 | bytes 2359298 | tf_op jit(solution)/shard_map/reduce_sum | solution.py:251
  83.0 18.0 %all_to_all.20 = bf16[8,128,128]{2,1,0:T(8,128)(2,1)S(1)} all-to-all(bf16[8,128,128]{2,1,0:T(8,128)(2,1)S(1)} %reduce_sum.23), channel_id=1, replica_groups={{0,16,32,48,64,80,96,112},{2,18,34,50,66,82,98,114},{4,20,36,52,68,84,1..., dimensions={0} | all-to-all | bytes 524288 | tf_op jit(solution)/shard_map/all_to_all | solution.py:199
  101.1 0.1 fusion.2
  101.2 12.9 %all_to_all.21.refs_0_ = bf16[8,128,128]{2,1,0:T(8,128)(2,1)S(1)} all-to-all(bf16[8,128,128]{2,1,0:T(8,128)(2,1)S(1)} %broadcast_in_dim.10), channel_id=1, replica_groups={{0,16,32,48,64,80,96,112},{2,18,34,50,66,82,98,114},{4,20,36,52,68,84,1..., dimensions={0} | all-to-all | bytes 524288 | tf_op jit(solution)/shard_map/all_to_all | solution.py:199
  114.1 2.3 %collective-permute-start.10 = (bf16[8,128,128]{2,1,0:T(8,128)(2,1)S(1)}, bf16[8,128,128]{2,1,0:T(8,128)(2,1)S(1)}, u32[]{:S(2)}, u32[]{:S(2)}) collective-permute-start(bf16[8,128,128]{2,1,0:T(8,128)(2,1)S(1)} %all_to_all.21.refs_0_), channel_id=1, source_target_pairs={{0,512},{1,65},{2,514},{3,67},{4,516},{5,69},{6,518},{7,71},{8,520... | collective-permute-start | bytes 786440 | tf_op jit(solution)/shard_map/ppermute | solution.py:267
  116.4 3.5 %collective-permute-start.11 = (bf16[8,128,128]{2,1,0:T(8,128)(2,1)S(1)}, bf16[8,128,128]{2,1,0:T(8,128)(2,1)S(1)}, u32[]{:S(2)}, u32[]{:S(2)}) collective-permute-start(bf16[8,128,128]{2,1,0:T(8,128)(2,1)S(1)} %all_to_all.21.refs_0_), channel_id=1, source_target_pairs={{0,384},{1,49},{2,386},{3,51},{4,388},{5,53},{6,390},{7,55},{8,392... | collective-permute-start | bytes 786440 | tf_op jit(solution)/shard_map/ppermute | solution.py:267
  119.9 3.9 %collective-permute-start.4 = (bf16[1,128,256]{2,1,0:T(8,128)(2,1)S(1)}, bf16[1,128,256]{2,1,0:T(8,128)(2,1)S(1)}, u32[]{:S(2)}, u32[]{:S(2)}) collective-permute-start(bf16[1,128,256]{2,1,0:T(8,128)(2,1)S(1)} %slice.23), channel_id=1, source_target_pairs={{0,8},{2,10},{4,12},{6,14},{8,0},{10,2},{12,4},{14,6},{1,9},{3,11}... | collective-permute-start | bytes 196616 | tf_op jit(solution)/shard_map/ppermute | solution.py:242
  123.8 4.9 %collective-permute-start.5 = (bf16[8,128,128]{2,1,0:T(8,128)(2,1)S(1)}, bf16[8,128,128]{2,1,0:T(8,128)(2,1)S(1)}, u32[]{:S(2)}, u32[]{:S(2)}) collective-permute-start(bf16[8,128,128]{2,1,0:T(8,128)(2,1)S(1)} %all_to_all.21.refs_0_), channel_id=1, source_target_pairs={{0,640},{1,81},{2,642},{3,83},{4,644},{5,85},{6,646},{7,87},{8,648... | collective-permute-start | bytes 786440 | tf_op jit(solution)/shard_map/ppermute | solution.py:267
  128.7 4.0 %collective-permute-start.6 = (bf16[8,128,128]{2,1,0:T(8,128)(2,1)S(1)}, bf16[8,128,128]{2,1,0:T(8,128)(2,1)S(1)}, u32[]{:S(2)}, u32[]{:S(2)}) collective-permute-start(bf16[8,128,128]{2,1,0:T(8,128)(2,1)S(1)} %all_to_all.21.refs_0_), channel_id=1, source_target_pairs={{0,256},{1,33},{2,258},{3,35},{4,260},{5,37},{6,262},{7,39},{8,264... | collective-permute-start | bytes 786440 | tf_op jit(solution)/shard_map/ppermute | solution.py:267
  132.7 3.9 %collective-permute-start.7 = (bf16[8,128,128]{2,1,0:T(8,128)(2,1)S(1)}, bf16[8,128,128]{2,1,0:T(8,128)(2,1)S(1)}, u32[]{:S(2)}, u32[]{:S(2)}) collective-permute-start(bf16[8,128,128]{2,1,0:T(8,128)(2,1)S(1)} %all_to_all.21.refs_0_), channel_id=1, source_target_pairs={{0,768},{1,97},{2,770},{3,99},{4,772},{5,101},{6,774},{7,103},{8,7... | collective-permute-start | bytes 786440 | tf_op jit(solution)/shard_map/ppermute | solution.py:267
  136.6 0.0 collective-permute-done.10.refs_6_
  136.7 3.4 %collective-permute-start.8 = (bf16[8,128,128]{2,1,0:T(8,128)(2,1)S(1)}, bf16[8,128,128]{2,1,0:T(8,128)(2,1)S(1)}, u32[]{:S(2)}, u32[]{:S(2)}) collective-permute-start(bf16[8,128,128]{2,1,0:T(8,128)(2,1)S(1)} %all_to_all.21.refs_0_), channel_id=1, source_target_pairs={{0,128},{1,17},{2,130},{3,19},{4,132},{5,21},{6,134},{7,23},{8,136... | collective-permute-start | bytes 786440 | tf_op jit(solution)/shard_map/ppermute | solution.py:267
  140.0 0.0 collective-permute-done.11.refs_7_
  140.0 3.7 %collective-permute-start.9 = (bf16[8,128,128]{2,1,0:T(8,128)(2,1)S(1)}, bf16[8,128,128]{2,1,0:T(8,128)(2,1)S(1)}, u32[]{:S(2)}, u32[]{:S(2)}) collective-permute-start(bf16[8,128,128]{2,1,0:T(8,128)(2,1)S(1)} %all_to_all.21.refs_0_), channel_id=1, source_target_pairs={{0,896},{1,113},{2,898},{3,115},{4,900},{5,117},{6,902},{7,119},{8... | collective-permute-start | bytes 786440 | tf_op jit(solution)/shard_map/ppermute | solution.py:267
  143.7 0.7 add_divide_fusion
  144.4 0.6 fusion.8
  145.1 0.0 collective-permute-done.5.refs_1_
  145.1 2.3 %collective-permute-done.7.refs_3_ = bf16[8,128,128]{2,1,0:T(8,128)(2,1)S(1)} collective-permute-done((bf16[8,128,128]{2,1,0:T(8,128)(2,1)S(1)}, bf16[8,128,128]{2,1,0:T(8,128)(2,1)S(1)}, u32[]{:S(2)}, u32[]{:S(2)}) %collective-permute-start.7) | collective-permute-done | bytes 262176 | tf_op jit(solution)/shard_map/ppermute | solution.py:267
  147.4 2.7 %collective-permute-done.9.refs_5_ = bf16[8,128,128]{2,1,0:T(8,128)(2,1)S(1)} collective-permute-done((bf16[8,128,128]{2,1,0:T(8,128)(2,1)S(1)}, bf16[8,128,128]{2,1,0:T(8,128)(2,1)S(1)}, u32[]{:S(2)}, u32[]{:S(2)}) %collective-permute-start.9) | collective-permute-done | bytes 262176 | tf_op jit(solution)/shard_map/ppermute | solution.py:267
  150.1 2.5 %shard_map.121 = bf16[64,128,128]{2,1,0:T(8,128)(2,1)} custom-call(s32[4]{0:T(128)S(1)} %pad_add_fusion.place_ref, s32[1,64]{1,0:T(1,128)S(1)} %copy-done.6, bf16[8,128,128]{2,1,0:T(8,128)(2,1)S(1)} %all_to_all.21.refs_0_, bf16[8,128,128]{2,1,0:T(8,128)(2,1)S(1)} %collective-permute-done.5.refs_1_, bf16[8,128,128]{2,1,0:T(8,128)(2,1)S(1)} %collective-permute-done.6.refs_2_, ...), custom_call_target="tpu_custom_call" | custom-call | bytes 4194304 | tf_op jit(solution)/shard_map/pallas_call | solution.py:268
  (22 shorter events, 0.2 us)
Async XLA Ops:
  2.3 33.5 %copy-start.4 = (s32[1,64]{1,0:T(1,128)S(1)}, s32[1,64]{1,0:T(1,128)}, u32[]{:S(2)}) copy-start(s32[1,64]{1,0:T(1,128)} %pos_ref.5) | copy-start | bytes 772
  2.3 33.5 %copy-start.6 = (s32[1,64]{1,0:T(1,128)S(1)}, s32[1,64]{1,0:T(1,128)}, u32[]{:S(2)}) copy-start(s32[1,64]{1,0:T(1,128)} %rank_ref.5) | copy-start | bytes 772
  2.3 29.7 %all-to-all-start = ((bf16[8,128,256]{2,1,0:T(8,128)(2,1)}), bf16[8,128,256]{2,1,0:T(8,128)(2,1)S(1)}, u32[]{:S(2)}, u32[]{:S(2)}) async-start(bf16[8,128,256]{2,1,0:T(8,128)(2,1)} %broadcast_in_dim.4), calls=%async_computation | async-start | bytes 1048576 | tf_op jit(solution)/shard_map/all_to_all | solution.py:201
  20.2 1.6 %copy-start = (bf16[64,128,128]{2,1,0:T(8,128)(2,1)S(1)}, bf16[64,128,128]{2,1,0:T(8,128)(2,1)}, u32[]{:S(2)}) copy-start(bf16[64,128,128]{2,1,0:T(8,128)(2,1)} %blocks_ref.3) | copy-start | bytes 6291460
  21.8 0.7 copy-start.3
  22.5 0.7 copy-start.5
  23.1 0.9 copy-start.8
  27.6 0.8 copy-start.2
  28.4 0.8 copy-start.7
  32.0 3.8 %collective-permute-start = (bf16[8,128,256]{2,1,0:T(8,128)(2,1)S(1)}, bf16[8,128,256]{2,1,0:T(8,128)(2,1)S(1)}, u32[]{:S(2)}, u32[]{:S(2)}) collective-permute-start(bf16[8,128,256]{2,1,0:T(8,128)(2,1)S(1)} %all-to-all-done.own_ref), channel_id=1, source_target_pairs={{0,1},{1,0},{2,3},{3,2},{4,5},{5,4},{6,7},{7,6},{8,9},{9,8},{10,11... | collective-permute-start | bytes 1572872 | tf_op jit(solution)/shard_map/ppermute | solution.py:212
  40.0 19.3 %copy-start.1 = (bf16[64,128,128]{2,1,0:T(8,128)(2,1)S(1)}, bf16[64,128,128]{2,1,0:T(8,128)(2,1)}, u32[]{:S(2)}) copy-start(bf16[64,128,128]{2,1,0:T(8,128)(2,1)} %blocks_ref.3) | copy-start | bytes 6291460
  40.0 41.0 %all-to-all-start.1 = ((bf16[8,8,128,128]{3,2,1,0:T(8,128)(2,1)}), bf16[8,8,128,128]{3,2,1,0:T(8,128)(2,1)}, u32[]{:S(2)}, u32[]{:S(2)}) async-start(bf16[8,8,128,128]{3,2,1,0:T(8,128)(2,1)} %bitcast.5), calls=%async_computation.1 | async-start | bytes 4194304 | tf_op jit(solution)/shard_map/all_to_all | solution.py:199
  50.6 4.0 %collective-permute-start.1 = (bf16[8,128,256]{2,1,0:T(8,128)(2,1)}, bf16[8,128,256]{2,1,0:T(8,128)(2,1)S(1)}, u32[]{:S(2)}, u32[]{:S(2)}) collective-permute-start(bf16[8,128,256]{2,1,0:T(8,128)(2,1)} %copy-done.7), channel_id=1, source_target_pairs={{0,1},{1,0},{2,3},{3,2},{4,5},{5,4},{6,7},{7,6},{8,9},{9,8},{10,11... | collective-permute-start | bytes 1572872 | tf_op jit(solution)/shard_map/ppermute | solution.py:247
  55.9 10.2 %collective-permute-start.2 = (bf16[4,128,256]{2,1,0:T(8,128)(2,1)S(1)}, bf16[4,128,256]{2,1,0:T(8,128)(2,1)S(1)}, u32[]{:S(2)}, u32[]{:S(2)}) collective-permute-start(bf16[4,128,256]{2,1,0:T(8,128)(2,1)S(1)} %slice.25), channel_id=1, source_target_pairs={{0,2},{2,0},{4,6},{6,4},{8,10},{10,8},{12,14},{14,12},{1,3},{3,1},... | collective-permute-start | bytes 786440 | tf_op jit(solution)/shard_map/ppermute | solution.py:242
  66.2 34.8 %copy-start.9 = (f32[1,1,128,128]{3,2,1,0:T(8,128)S(1)}, f32[1,1,128,128]{3,2,1,0:T(8,128)}, u32[]{:S(2)}) copy-start(f32[1,1,128,128]{3,2,1,0:T(8,128)} %param.13) | copy-start | bytes 196612
  66.2 34.8 %copy-start.10 = (f32[1,1,128,128]{3,2,1,0:T(8,128)S(1)}, f32[1,1,128,128]{3,2,1,0:T(8,128)}, u32[]{:S(2)}) copy-start(f32[1,1,128,128]{3,2,1,0:T(8,128)} %param.12) | copy-start | bytes 196612
  66.2 7.9 %collective-permute-start.3 = (bf16[2,128,256]{2,1,0:T(8,128)(2,1)S(1)}, bf16[2,128,256]{2,1,0:T(8,128)(2,1)S(1)}, u32[]{:S(2)}, u32[]{:S(2)}) collective-permute-start(bf16[2,128,256]{2,1,0:T(8,128)(2,1)S(1)} %slice.27), channel_id=1, source_target_pairs={{0,4},{2,6},{4,0},{6,2},{8,12},{10,14},{12,8},{14,10},{1,5},{3,7},... | collective-permute-start | bytes 393224 | tf_op jit(solution)/shard_map/ppermute | solution.py:242
  114.1 22.6 %collective-permute-start.10 = (bf16[8,128,128]{2,1,0:T(8,128)(2,1)S(1)}, bf16[8,128,128]{2,1,0:T(8,128)(2,1)S(1)}, u32[]{:S(2)}, u32[]{:S(2)}) collective-permute-start(bf16[8,128,128]{2,1,0:T(8,128)(2,1)S(1)} %all_to_all.21.refs_0_), channel_id=1, source_target_pairs={{0,512},{1,65},{2,514},{3,67},{4,516},{5,69},{6,518},{7,71},{8,520... | collective-permute-start | bytes 786440 | tf_op jit(solution)/shard_map/ppermute | solution.py:267
  116.4 23.6 %collective-permute-start.11 = (bf16[8,128,128]{2,1,0:T(8,128)(2,1)S(1)}, bf16[8,128,128]{2,1,0:T(8,128)(2,1)S(1)}, u32[]{:S(2)}, u32[]{:S(2)}) collective-permute-start(bf16[8,128,128]{2,1,0:T(8,128)(2,1)S(1)} %all_to_all.21.refs_0_), channel_id=1, source_target_pairs={{0,384},{1,49},{2,386},{3,51},{4,388},{5,53},{6,390},{7,55},{8,392... | collective-permute-start | bytes 786440 | tf_op jit(solution)/shard_map/ppermute | solution.py:267
  119.9 12.8 %collective-permute-start.4 = (bf16[1,128,256]{2,1,0:T(8,128)(2,1)S(1)}, bf16[1,128,256]{2,1,0:T(8,128)(2,1)S(1)}, u32[]{:S(2)}, u32[]{:S(2)}) collective-permute-start(bf16[1,128,256]{2,1,0:T(8,128)(2,1)S(1)} %slice.23), channel_id=1, source_target_pairs={{0,8},{2,10},{4,12},{6,14},{8,0},{10,2},{12,4},{14,6},{1,9},{3,11}... | collective-permute-start | bytes 196616 | tf_op jit(solution)/shard_map/ppermute | solution.py:242
  123.8 21.3 %collective-permute-start.5 = (bf16[8,128,128]{2,1,0:T(8,128)(2,1)S(1)}, bf16[8,128,128]{2,1,0:T(8,128)(2,1)S(1)}, u32[]{:S(2)}, u32[]{:S(2)}) collective-permute-start(bf16[8,128,128]{2,1,0:T(8,128)(2,1)S(1)} %all_to_all.21.refs_0_), channel_id=1, source_target_pairs={{0,640},{1,81},{2,642},{3,83},{4,644},{5,85},{6,646},{7,87},{8,648... | collective-permute-start | bytes 786440 | tf_op jit(solution)/shard_map/ppermute | solution.py:267
  128.7 16.4 %collective-permute-start.6 = (bf16[8,128,128]{2,1,0:T(8,128)(2,1)S(1)}, bf16[8,128,128]{2,1,0:T(8,128)(2,1)S(1)}, u32[]{:S(2)}, u32[]{:S(2)}) collective-permute-start(bf16[8,128,128]{2,1,0:T(8,128)(2,1)S(1)} %all_to_all.21.refs_0_), channel_id=1, source_target_pairs={{0,256},{1,33},{2,258},{3,35},{4,260},{5,37},{6,262},{7,39},{8,264... | collective-permute-start | bytes 786440 | tf_op jit(solution)/shard_map/ppermute | solution.py:267
  132.7 14.7 %collective-permute-start.7 = (bf16[8,128,128]{2,1,0:T(8,128)(2,1)S(1)}, bf16[8,128,128]{2,1,0:T(8,128)(2,1)S(1)}, u32[]{:S(2)}, u32[]{:S(2)}) collective-permute-start(bf16[8,128,128]{2,1,0:T(8,128)(2,1)S(1)} %all_to_all.21.refs_0_), channel_id=1, source_target_pairs={{0,768},{1,97},{2,770},{3,99},{4,772},{5,101},{6,774},{7,103},{8,7... | collective-permute-start | bytes 786440 | tf_op jit(solution)/shard_map/ppermute | solution.py:267
  136.7 10.7 %collective-permute-start.8 = (bf16[8,128,128]{2,1,0:T(8,128)(2,1)S(1)}, bf16[8,128,128]{2,1,0:T(8,128)(2,1)S(1)}, u32[]{:S(2)}, u32[]{:S(2)}) collective-permute-start(bf16[8,128,128]{2,1,0:T(8,128)(2,1)S(1)} %all_to_all.21.refs_0_), channel_id=1, source_target_pairs={{0,128},{1,17},{2,130},{3,19},{4,132},{5,21},{6,134},{7,23},{8,136... | collective-permute-start | bytes 786440 | tf_op jit(solution)/shard_map/ppermute | solution.py:267
  140.0 10.0 %collective-permute-start.9 = (bf16[8,128,128]{2,1,0:T(8,128)(2,1)S(1)}, bf16[8,128,128]{2,1,0:T(8,128)(2,1)S(1)}, u32[]{:S(2)}, u32[]{:S(2)}) collective-permute-start(bf16[8,128,128]{2,1,0:T(8,128)(2,1)S(1)} %all_to_all.21.refs_0_), channel_id=1, source_target_pairs={{0,896},{1,113},{2,898},{3,115},{4,900},{5,117},{6,902},{7,119},{8... | collective-permute-start | bytes 786440 | tf_op jit(solution)/shard_map/ppermute | solution.py:267

commit v6 on v5

--- a/solution.py
+++ b/solution.py
@@ -207,8 +207,10 @@
         [pltpu.VMEM((rows, width), BF)],
         flops=2 * tokens * rows * width,
         nbytes=4 * 2**20,
+        limit=60,
     )(place, block_pos, owner_rank, hidden, blocks)
-    own, keep, send = lax.optimization_barrier((own, keep, send))
+    swapped = lax.ppermute(send, "core", swap)
+    own, keep, swapped = lax.optimization_barrier((own, keep, swapped))
     other = lax.ppermute(own, "core", swap)
     grads = call(
         functools.partial(grads_kernel, n0, factor),
@@ -225,7 +227,7 @@
         nbytes=4 * 2**20,
         limit=12,
     )(place, block_pos, owner_rank, hid_t, own, other)
-    grads, keep, send = lax.optimization_barrier((grads, keep, send))
+    grads, keep, swapped = lax.optimization_barrier((grads, keep, swapped))
     hidden_grad = call(
         back_kernel,
         jax.ShapeDtypeStruct((tokens, rows), BF),
@@ -244,7 +246,7 @@
         return (value[:half].astype(F32) + theirs.astype(F32)).astype(BF), beside
 
     got = exchange(grads.reshape(n0, slots // n0, bs, bs), first)
-    total = (keep.astype(F32) + lax.ppermute(send, "core", swap).astype(F32)).astype(BF)
+    total = (keep.astype(F32) + swapped.astype(F32)).astype(BF)
     total, hidden_grad = halved(total, 1, hidden_grad)
     if total.shape[0] > 1:
         total, _ = halved(total, 2)

time: 153 us -> 154 us (level)
  local copies, waits for them, and re-layouts: 7.15 us -> 2.7 us
  waiting for transfers between devices: 26.4 us -> 29 us
  Pallas kernels: 15.1 us -> 17.3 us
    unnamed x22 -> x16, local copies, waits for them, and re-layouts: 5.42 us -> 0.96 us
    all_to_all x1, waiting for transfers between devices: 6.85 us -> 11.2 us  [exchange(): lax.all_to_all(value, axes, 0, 0, axis_index_groups=groups, tiled=True)]
    pallas_call x1, Pallas kernels: 3.55 us -> 5.69 us  [shards(): call(partial_kernel, (*(jax.ShapeDtypeStruct((nx, tokens, feats), BF),) *...]
  transfers between devices with their start and end apart: 14 -> 14, of which waited for: 8 -> 8; matrix products, arithmetic and copies ran while one was open for 2% -> 2% of each run, Pallas kernels for 6% -> 7%
where the time goes in v6:
time: 154 us; the launch traced here: 153 us
  starting transfers between devices  67.3 us (44%)
  blocking collectives  30.9 us (20%)
  waiting for transfers between devices  29 us (19%)
  Pallas kernels  17.3 us (11%)
  other arithmetic  5.47 us (4%)
  local copies, waits for them, and re-layouts  2.7 us (2%)
    all_to_all x2, blocking collectives, exchange(): lax.all_to_all(value, axes, 0, 0, axis_index_groups=groups, tiled=True)  30.9 us
    ppermute x7, starting transfers between devices, shards(): lax.ppermute(row, axes, ring_shift(sizes, k))  26.2 us
    all_to_all x1, starting transfers between devices, shards(): lax.all_to_all(jnp.broadcast_to(cotangent, (nx, tokens, feats)), 'x', 0,...  17.9 us
    all_to_all x1, waiting for transfers between devices, exchange(): lax.all_to_all(value, axes, 0, 0, axis_index_groups=groups, tiled=True)  11.2 us
    all_to_all x1, starting transfers between devices, exchange(): lax.all_to_all(value, axes, 0, 0, axis_index_groups=groups, tiled=True)  10.6 us
    ppermute x3, starting transfers between devices, halved(): theirs = lax.ppermute(value[half:], 'x', [(i, i ^ step) for i in range(nx)])  8.79 us
    ppermute x3, waiting for transfers between devices, halved(): theirs = lax.ppermute(value[half:], 'x', [(i, i ^ step) for i in range(nx)])  7.32 us
    pallas_call x1, Pallas kernels, shards(): call(partial_kernel, (*(jax.ShapeDtypeStruct((nx, tokens, feats), BF),) *...  5.69 us
  transfers between devices with their start and end apart: 14, of which 8 were waited for; matrix products, arithmetic and copies ran while one was open for 2% of the time, Pallas kernels for 7%

profile of v6, /device:TPU:2, one launch (start us, length us, event | category | flops | bytes accessed | tf_op | source)
XLA Modules:
  0.0 153.5 jit_solution(13388413324732256890)
XLA Ops:
  0.6 1.7 %broadcast_in_dim.4 = bf16[8,128,256]{2,1,0:T(8,128)(2,1)} broadcast(bf16[128,256]{1,0:T(8,128)(2,1)} %param.8), dimensions={1,2} | broadcast | bytes 589824 | tf_op jit(solution)/shard_map/broadcast_in_dim | solution.py:201
  2.3 17.9 %all-to-all-start = ((bf16[8,128,256]{2,1,0:T(8,128)(2,1)}), bf16[8,128,256]{2,1,0:T(8,128)(2,1)S(1)}, u32[]{:S(2)}, u32[]{:S(2)}) async-start(bf16[8,128,256]{2,1,0:T(8,128)(2,1)} %broadcast_in_dim.4), calls=%async_computation | async-start | bytes 1048576 | tf_op jit(solution)/shard_map/all_to_all | solution.py:201
  20.2 0.6 pad_add_fusion.place_ref
  20.8 5.7 %shard_map.118 = (bf16[8,128,256]{2,1,0:T(8,128)(2,1)}, bf16[8,128,256]{2,1,0:T(8,128)(2,1)}, bf16[128,128]{1,0:T(8,128)(2,1)}, bf16[768,128]{1,0:T(8,128)(2,1)}) custom-call(s32[4]{0:T(128)} %pad_add_fusion.place_ref, s32[1,64]{1,0:T(1,128)} %pos_ref.5, s32[1,64]{1,0:T(1,128)} %rank_ref.5, bf16[128,768]{1,0:T(8,128)(2,1)} %hid_ref.1, ...), custom_call_target="tpu_custom_call" | custom-call | flops 805306368 | bytes 4194304 | tf_op jit(solution)/shard_map/pallas_call | solution.py:202
  26.5 1.9 %collective-permute-start = (bf16[8,128,256]{2,1,0:T(8,128)(2,1)}, bf16[8,128,256]{2,1,0:T(8,128)(2,1)}, u32[]{:S(2)}, u32[]{:S(2)}) collective-permute-start(bf16[8,128,256]{2,1,0:T(8,128)(2,1)} %get-tuple-element.25), channel_id=1, source_target_pairs={{0,1},{1,0},{2,3},{3,2},{4,5},{5,4},{6,7},{7,6},{8,9},{9,8},{10,11... | collective-permute-start | bytes 1572872 | tf_op jit(solution)/shard_map/ppermute | solution.py:212
  28.4 2.2 %collective-permute-done = bf16[8,128,256]{2,1,0:T(8,128)(2,1)} collective-permute-done((bf16[8,128,256]{2,1,0:T(8,128)(2,1)}, bf16[8,128,256]{2,1,0:T(8,128)(2,1)}, u32[]{:S(2)}, u32[]{:S(2)}) %collective-permute-start) | collective-permute-done | bytes 524320 | tf_op jit(solution)/shard_map/ppermute | solution.py:212
  30.6 1.4 all-to-all-done.own_ref
  32.0 1.9 %collective-permute-start.1 = (bf16[8,128,256]{2,1,0:T(8,128)(2,1)S(1)}, bf16[8,128,256]{2,1,0:T(8,128)(2,1)S(1)}, u32[]{:S(2)}, u32[]{:S(2)}) collective-permute-start(bf16[8,128,256]{2,1,0:T(8,128)(2,1)S(1)} %all-to-all-done.own_ref), channel_id=1, source_target_pairs={{0,1},{1,0},{2,3},{3,2},{4,5},{5,4},{6,7},{7,6},{8,9},{9,8},{10,11... | collective-permute-start | bytes 1572872 | tf_op jit(solution)/shard_map/ppermute | solution.py:214
  33.9 1.9 %collective-permute-done.1.other_ref = bf16[8,128,256]{2,1,0:T(8,128)(2,1)S(1)} collective-permute-done((bf16[8,128,256]{2,1,0:T(8,128)(2,1)S(1)}, bf16[8,128,256]{2,1,0:T(8,128)(2,1)S(1)}, u32[]{:S(2)}, u32[]{:S(2)}) %collective-permute-start.1) | collective-permute-done | bytes 524320 | tf_op jit(solution)/shard_map/ppermute | solution.py:214
  35.8 0.0 copy-start.1
  35.8 0.9 copy-done.1
  36.7 4.2 %shard_map.119 = bf16[64,128,128]{2,1,0:T(8,128)(2,1)} custom-call(s32[4]{0:T(128)S(1)} %copy-done.2, s32[1,64]{1,0:T(1,128)S(1)} %copy-done.3, s32[1,64]{1,0:T(1,128)S(1)} %copy-done.4, bf16[768,128]{1,0:T(8,128)(2,1)S(1)} %copy-done.1, bf16[8,128,256]{2,1,0:T(8,128)(2,1)S(1)} %all-to-all-done.own_ref, bf16[8,128,256]{2,1,0:T(8,128)(2,1)S(1)} %collective-permute-done.1.other_ref), custom_call_target="tpu_custom_call" | custom-call | flops 268435456 | bytes 4194304 | tf_op jit(solution)/shard_map/pallas_call | solution.py:215
  41.0 0.0 copy-start
  41.0 10.6 %all-to-all-start.1 = ((bf16[8,8,128,128]{3,2,1,0:T(8,128)(2,1)}), bf16[8,8,128,128]{3,2,1,0:T(8,128)(2,1)}, u32[]{:S(2)}, u32[]{:S(2)}) async-start(bf16[8,8,128,128]{3,2,1,0:T(8,128)(2,1)} %bitcast.5), calls=%async_computation.1 | async-start | bytes 4194304 | tf_op jit(solution)/shard_map/all_to_all | solution.py:199
  51.6 1.3 add_convert_fusion
  52.9 3.4 %collective-permute-start.2 = (bf16[4,128,256]{2,1,0:T(8,128)(2,1)S(1)}, bf16[4,128,256]{2,1,0:T(8,128)(2,1)S(1)}, u32[]{:S(2)}, u32[]{:S(2)}) collective-permute-start(bf16[4,128,256]{2,1,0:T(8,128)(2,1)S(1)} %slice.25), channel_id=1, source_target_pairs={{0,2},{2,0},{4,6},{6,4},{8,10},{10,8},{12,14},{14,12},{1,3},{3,1},... | collective-permute-start | bytes 786440 | tf_op jit(solution)/shard_map/ppermute | solution.py:244
  56.3 4.9 %shard_map.120 = bf16[128,768]{1,0:T(8,128)(2,1)} custom-call(s32[4]{0:T(128)S(1)} %copy-done.2, s32[1,64]{1,0:T(1,128)S(1)} %copy-done.3, bf16[64,128,128]{2,1,0:T(8,128)(2,1)S(1)} %copy-done, bf16[8,128,256]{2,1,0:T(8,128)(2,1)S(1)} %all-to-all-done.own_ref, bf16[8,128,256]{2,1,0:T(8,128)(2,1)S(1)} %collective-permute-done.1.other_ref), custom_call_target="tpu_custom_call" | custom-call | flops 805306368 | bytes 4194304 | tf_op jit(solution)/shard_map/pallas_call | solution.py:231
  61.2 1.4 collective-permute-done.2
  62.6 0.1 add_convert_fusion.1
  62.7 0.0 copy-start.5
  62.7 0.0 copy-start.6
  62.7 0.0 copy-start.7
  62.7 2.1 %collective-permute-start.3 = (bf16[2,128,256]{2,1,0:T(8,128)(2,1)S(1)}, bf16[2,128,256]{2,1,0:T(8,128)(2,1)S(1)}, u32[]{:S(2)}, u32[]{:S(2)}) collective-permute-start(bf16[2,128,256]{2,1,0:T(8,128)(2,1)S(1)} %slice.27), channel_id=1, source_target_pairs={{0,4},{2,6},{4,0},{6,2},{8,12},{10,14},{12,8},{14,10},{1,5},{3,7},... | collective-permute-start | bytes 393224 | tf_op jit(solution)/shard_map/ppermute | solution.py:244
  64.8 5.9 %collective-permute-done.3 = bf16[2,128,256]{2,1,0:T(8,128)(2,1)S(1)} collective-permute-done((bf16[2,128,256]{2,1,0:T(8,128)(2,1)S(1)}, bf16[2,128,256]{2,1,0:T(8,128)(2,1)S(1)}, u32[]{:S(2)}, u32[]{:S(2)}) %collective-permute-start.3) | collective-permute-done | bytes 131104 | tf_op jit(solution)/shard_map/ppermute | solution.py:244
  70.8 11.2 %all-to-all-done.1 = bf16[8,8,128,128]{3,2,1,0:T(8,128)(2,1)} async-done(((bf16[8,8,128,128]{3,2,1,0:T(8,128)(2,1)}), bf16[8,8,128,128]{3,2,1,0:T(8,128)(2,1)}, u32[]{:S(2)}, u32[]{:S(2)}) %all-to-all-start.1) | async-done | bytes 2097184 | tf_op jit(solution)/shard_map/all_to_all | solution.py:199
  82.0 2.0 %reduce_sum.23 = bf16[8,128,128]{2,1,0:T(8,128)(2,1)S(1)} reduce(bf16[8,8,128,128]{3,2,1,0:T(8,128)(2,1)} %all-to-all-done.1, bf16[]{:T(256)} %constant.28.clone.1), dimensions={0}, to_apply=%region_0.1 | reduce | flops 917504 | bytes 2359298 | tf_op jit(solution)/shard_map/reduce_sum | solution.py:253
  83.9 18.0 %all_to_all.20 = bf16[8,128,128]{2,1,0:T(8,128)(2,1)S(1)} all-to-all(bf16[8,128,128]{2,1,0:T(8,128)(2,1)S(1)} %reduce_sum.23), channel_id=1, replica_groups={{0,16,32,48,64,80,96,112},{2,18,34,50,66,82,98,114},{4,20,36,52,68,84,1..., dimensions={0} | all-to-all | bytes 524288 | tf_op jit(solution)/shard_map/all_to_all | solution.py:199
  102.0 0.1 fusion.2
  102.1 12.9 %all_to_all.21.refs_0_ = bf16[8,128,128]{2,1,0:T(8,128)(2,1)S(1)} all-to-all(bf16[8,128,128]{2,1,0:T(8,128)(2,1)S(1)} %broadcast_in_dim.10), channel_id=1, replica_groups={{0,16,32,48,64,80,96,112},{2,18,34,50,66,82,98,114},{4,20,36,52,68,84,1..., dimensions={0} | all-to-all | bytes 524288 | tf_op jit(solution)/shard_map/all_to_all | solution.py:199
  115.0 2.3 %collective-permute-start.10 = (bf16[8,128,128]{2,1,0:T(8,128)(2,1)S(1)}, bf16[8,128,128]{2,1,0:T(8,128)(2,1)S(1)}, u32[]{:S(2)}, u32[]{:S(2)}) collective-permute-start(bf16[8,128,128]{2,1,0:T(8,128)(2,1)S(1)} %all_to_all.21.refs_0_), channel_id=1, source_target_pairs={{0,512},{1,65},{2,514},{3,67},{4,516},{5,69},{6,518},{7,71},{8,520... | collective-permute-start | bytes 786440 | tf_op jit(solution)/shard_map/ppermute | solution.py:269
  117.4 2.7 %collective-permute-start.11 = (bf16[8,128,128]{2,1,0:T(8,128)(2,1)S(1)}, bf16[8,128,128]{2,1,0:T(8,128)(2,1)S(1)}, u32[]{:S(2)}, u32[]{:S(2)}) collective-permute-start(bf16[8,128,128]{2,1,0:T(8,128)(2,1)S(1)} %all_to_all.21.refs_0_), channel_id=1, source_target_pairs={{0,384},{1,49},{2,386},{3,51},{4,388},{5,53},{6,390},{7,55},{8,392... | collective-permute-start | bytes 786440 | tf_op jit(solution)/shard_map/ppermute | solution.py:269
  120.1 3.4 %collective-permute-start.4 = (bf16[1,128,256]{2,1,0:T(8,128)(2,1)S(1)}, bf16[1,128,256]{2,1,0:T(8,128)(2,1)S(1)}, u32[]{:S(2)}, u32[]{:S(2)}) collective-permute-start(bf16[1,128,256]{2,1,0:T(8,128)(2,1)S(1)} %slice.23), channel_id=1, source_target_pairs={{0,8},{2,10},{4,12},{6,14},{8,0},{10,2},{12,4},{14,6},{1,9},{3,11}... | collective-permute-start | bytes 196616 | tf_op jit(solution)/shard_map/ppermute | solution.py:244
  123.5 6.2 %collective-permute-start.5 = (bf16[8,128,128]{2,1,0:T(8,128)(2,1)S(1)}, bf16[8,128,128]{2,1,0:T(8,128)(2,1)S(1)}, u32[]{:S(2)}, u32[]{:S(2)}) collective-permute-start(bf16[8,128,128]{2,1,0:T(8,128)(2,1)S(1)} %all_to_all.21.refs_0_), channel_id=1, source_target_pairs={{0,640},{1,81},{2,642},{3,83},{4,644},{5,85},{6,646},{7,87},{8,648... | collective-permute-start | bytes 786440 | tf_op jit(solution)/shard_map/ppermute | solution.py:269
  129.6 4.0 %collective-permute-start.6 = (bf16[8,128,128]{2,1,0:T(8,128)(2,1)S(1)}, bf16[8,128,128]{2,1,0:T(8,128)(2,1)S(1)}, u32[]{:S(2)}, u32[]{:S(2)}) collective-permute-start(bf16[8,128,128]{2,1,0:T(8,128)(2,1)S(1)} %all_to_all.21.refs_0_), channel_id=1, source_target_pairs={{0,256},{1,33},{2,258},{3,35},{4,260},{5,37},{6,262},{7,39},{8,264... | collective-permute-start | bytes 786440 | tf_op jit(solution)/shard_map/ppermute | solution.py:269
  133.6 0.0 collective-permute-done.4
  133.6 3.9 %collective-permute-start.7 = (bf16[8,128,128]{2,1,0:T(8,128)(2,1)S(1)}, bf16[8,128,128]{2,1,0:T(8,128)(2,1)S(1)}, u32[]{:S(2)}, u32[]{:S(2)}) collective-permute-start(bf16[8,128,128]{2,1,0:T(8,128)(2,1)S(1)} %all_to_all.21.refs_0_), channel_id=1, source_target_pairs={{0,768},{1,97},{2,770},{3,99},{4,772},{5,101},{6,774},{7,103},{8,7... | collective-permute-start | bytes 786440 | tf_op jit(solution)/shard_map/ppermute | solution.py:269
  137.6 0.0 collective-permute-done.10.refs_6_
  137.6 3.4 %collective-permute-start.8 = (bf16[8,128,128]{2,1,0:T(8,128)(2,1)S(1)}, bf16[8,128,128]{2,1,0:T(8,128)(2,1)S(1)}, u32[]{:S(2)}, u32[]{:S(2)}) collective-permute-start(bf16[8,128,128]{2,1,0:T(8,128)(2,1)S(1)} %all_to_all.21.refs_0_), channel_id=1, source_target_pairs={{0,128},{1,17},{2,130},{3,19},{4,132},{5,21},{6,134},{7,23},{8,136... | collective-permute-start | bytes 786440 | tf_op jit(solution)/shard_map/ppermute | solution.py:269
  141.0 0.0 collective-permute-done.11.refs_7_
  141.0 3.7 %collective-permute-start.9 = (bf16[8,128,128]{2,1,0:T(8,128)(2,1)S(1)}, bf16[8,128,128]{2,1,0:T(8,128)(2,1)S(1)}, u32[]{:S(2)}, u32[]{:S(2)}) collective-permute-start(bf16[8,128,128]{2,1,0:T(8,128)(2,1)S(1)} %all_to_all.21.refs_0_), channel_id=1, source_target_pairs={{0,896},{1,113},{2,898},{3,115},{4,900},{5,117},{6,902},{7,119},{8... | collective-permute-start | bytes 786440 | tf_op jit(solution)/shard_map/ppermute | solution.py:269
  144.7 0.7 add_divide_fusion
  145.4 0.6 fusion.8
  146.0 0.0 collective-permute-done.5.refs_1_
  146.0 0.0 collective-permute-done.6.refs_2_
  146.0 2.3 %collective-permute-done.7.refs_3_ = bf16[8,128,128]{2,1,0:T(8,128)(2,1)S(1)} collective-permute-done((bf16[8,128,128]{2,1,0:T(8,128)(2,1)S(1)}, bf16[8,128,128]{2,1,0:T(8,128)(2,1)S(1)}, u32[]{:S(2)}, u32[]{:S(2)}) %collective-permute-start.7) | collective-permute-done | bytes 262176 | tf_op jit(solution)/shard_map/ppermute | solution.py:269
  148.3 0.0 collective-permute-done.8.refs_4_
  148.3 2.7 %collective-permute-done.9.refs_5_ = bf16[8,128,128]{2,1,0:T(8,128)(2,1)S(1)} collective-permute-done((bf16[8,128,128]{2,1,0:T(8,128)(2,1)S(1)}, bf16[8,128,128]{2,1,0:T(8,128)(2,1)S(1)}, u32[]{:S(2)}, u32[]{:S(2)}) %collective-permute-start.9) | collective-permute-done | bytes 262176 | tf_op jit(solution)/shard_map/ppermute | solution.py:269
  151.0 2.5 %shard_map.121 = bf16[64,128,128]{2,1,0:T(8,128)(2,1)} custom-call(s32[4]{0:T(128)S(1)} %copy-done.2, s32[1,64]{1,0:T(1,128)S(1)} %copy-done.4, bf16[8,128,128]{2,1,0:T(8,128)(2,1)S(1)} %all_to_all.21.refs_0_, bf16[8,128,128]{2,1,0:T(8,128)(2,1)S(1)} %collective-permute-done.5.refs_1_, bf16[8,128,128]{2,1,0:T(8,128)(2,1)S(1)} %collective-permute-done.6.refs_2_, ...), custom_call_target="tpu_custom_call" | custom-call | bytes 4194304 | tf_op jit(solution)/shard_map/pallas_call | solution.py:270
  (16 shorter events, 0.2 us)
Async XLA Ops:
  2.3 33.5 %copy-start.3 = (s32[1,64]{1,0:T(1,128)S(1)}, s32[1,64]{1,0:T(1,128)}, u32[]{:S(2)}) copy-start(s32[1,64]{1,0:T(1,128)} %pos_ref.5) | copy-start | bytes 772
  2.3 33.5 %copy-start.4 = (s32[1,64]{1,0:T(1,128)S(1)}, s32[1,64]{1,0:T(1,128)}, u32[]{:S(2)}) copy-start(s32[1,64]{1,0:T(1,128)} %rank_ref.5) | copy-start | bytes 772
  2.3 29.7 %all-to-all-start = ((bf16[8,128,256]{2,1,0:T(8,128)(2,1)}), bf16[8,128,256]{2,1,0:T(8,128)(2,1)S(1)}, u32[]{:S(2)}, u32[]{:S(2)}) async-start(bf16[8,128,256]{2,1,0:T(8,128)(2,1)} %broadcast_in_dim.4), calls=%async_computation | async-start | bytes 1048576 | tf_op jit(solution)/shard_map/all_to_all | solution.py:201
  20.8 15.0 %copy-start.2 = (s32[4]{0:T(128)S(1)}, s32[4]{0:T(128)}, u32[]{:S(2)}) copy-start(s32[4]{0:T(128)} %pad_add_fusion.place_ref) | copy-start | bytes 52
  26.5 4.1 %collective-permute-start = (bf16[8,128,256]{2,1,0:T(8,128)(2,1)}, bf16[8,128,256]{2,1,0:T(8,128)(2,1)}, u32[]{:S(2)}, u32[]{:S(2)}) collective-permute-start(bf16[8,128,256]{2,1,0:T(8,128)(2,1)} %get-tuple-element.25), channel_id=1, source_target_pairs={{0,1},{1,0},{2,3},{3,2},{4,5},{5,4},{6,7},{7,6},{8,9},{9,8},{10,11... | collective-permute-start | bytes 1572872 | tf_op jit(solution)/shard_map/ppermute | solution.py:212
  32.0 3.8 %collective-permute-start.1 = (bf16[8,128,256]{2,1,0:T(8,128)(2,1)S(1)}, bf16[8,128,256]{2,1,0:T(8,128)(2,1)S(1)}, u32[]{:S(2)}, u32[]{:S(2)}) collective-permute-start(bf16[8,128,256]{2,1,0:T(8,128)(2,1)S(1)} %all-to-all-done.own_ref), channel_id=1, source_target_pairs={{0,1},{1,0},{2,3},{3,2},{4,5},{5,4},{6,7},{7,6},{8,9},{9,8},{10,11... | collective-permute-start | bytes 1572872 | tf_op jit(solution)/shard_map/ppermute | solution.py:214
  35.8 0.9 copy-start.1
  41.0 15.4 %copy-start = (bf16[64,128,128]{2,1,0:T(8,128)(2,1)S(1)}, bf16[64,128,128]{2,1,0:T(8,128)(2,1)}, u32[]{:S(2)}) copy-start(bf16[64,128,128]{2,1,0:T(8,128)(2,1)} %blocks_ref.3) | copy-start | bytes 6291460
  41.0 41.0 %all-to-all-start.1 = ((bf16[8,8,128,128]{3,2,1,0:T(8,128)(2,1)}), bf16[8,8,128,128]{3,2,1,0:T(8,128)(2,1)}, u32[]{:S(2)}, u32[]{:S(2)}) async-start(bf16[8,8,128,128]{3,2,1,0:T(8,128)(2,1)} %bitcast.5), calls=%async_computation.1 | async-start | bytes 4194304 | tf_op jit(solution)/shard_map/all_to_all | solution.py:199
  52.9 9.7 %collective-permute-start.2 = (bf16[4,128,256]{2,1,0:T(8,128)(2,1)S(1)}, bf16[4,128,256]{2,1,0:T(8,128)(2,1)S(1)}, u32[]{:S(2)}, u32[]{:S(2)}) collective-permute-start(bf16[4,128,256]{2,1,0:T(8,128)(2,1)S(1)} %slice.25), channel_id=1, source_target_pairs={{0,2},{2,0},{4,6},{6,4},{8,10},{10,8},{12,14},{14,12},{1,3},{3,1},... | collective-permute-start | bytes 786440 | tf_op jit(solution)/shard_map/ppermute | solution.py:244
  62.7 39.3 %copy-start.5 = (f32[1,1,128,128]{3,2,1,0:T(8,128)S(1)}, f32[1,1,128,128]{3,2,1,0:T(8,128)}, u32[]{:S(2)}) copy-start(f32[1,1,128,128]{3,2,1,0:T(8,128)} %param.13) | copy-start | bytes 196612
  62.7 39.3 %copy-start.6 = (f32[1,1,128,128]{3,2,1,0:T(8,128)S(1)}, f32[1,1,128,128]{3,2,1,0:T(8,128)}, u32[]{:S(2)}) copy-start(f32[1,1,128,128]{3,2,1,0:T(8,128)} %param.12) | copy-start | bytes 196612
  62.7 39.3 %copy-start.7 = (bf16[128,128]{1,0:T(8,128)(2,1)S(1)}, bf16[128,128]{1,0:T(8,128)(2,1)}, u32[]{:S(2)}) copy-start(bf16[128,128]{1,0:T(8,128)(2,1)} %get-tuple-element.22) | copy-start | bytes 98308
  62.7 8.0 %collective-permute-start.3 = (bf16[2,128,256]{2,1,0:T(8,128)(2,1)S(1)}, bf16[2,128,256]{2,1,0:T(8,128)(2,1)S(1)}, u32[]{:S(2)}, u32[]{:S(2)}) collective-permute-start(bf16[2,128,256]{2,1,0:T(8,128)(2,1)S(1)} %slice.27), channel_id=1, source_target_pairs={{0,4},{2,6},{4,0},{6,2},{8,12},{10,14},{12,8},{14,10},{1,5},{3,7},... | collective-permute-start | bytes 393224 | tf_op jit(solution)/shard_map/ppermute | solution.py:244
  115.0 22.6 %collective-permute-start.10 = (bf16[8,128,128]{2,1,0:T(8,128)(2,1)S(1)}, bf16[8,128,128]{2,1,0:T(8,128)(2,1)S(1)}, u32[]{:S(2)}, u32[]{:S(2)}) collective-permute-start(bf16[8,128,128]{2,1,0:T(8,128)(2,1)S(1)} %all_to_all.21.refs_0_), channel_id=1, source_target_pairs={{0,512},{1,65},{2,514},{3,67},{4,516},{5,69},{6,518},{7,71},{8,520... | collective-permute-start | bytes 786440 | tf_op jit(solution)/shard_map/ppermute | solution.py:269
  117.4 23.6 %collective-permute-start.11 = (bf16[8,128,128]{2,1,0:T(8,128)(2,1)S(1)}, bf16[8,128,128]{2,1,0:T(8,128)(2,1)S(1)}, u32[]{:S(2)}, u32[]{:S(2)}) collective-permute-start(bf16[8,128,128]{2,1,0:T(8,128)(2,1)S(1)} %all_to_all.21.refs_0_), channel_id=1, source_target_pairs={{0,384},{1,49},{2,386},{3,51},{4,388},{5,53},{6,390},{7,55},{8,392... | collective-permute-start | bytes 786440 | tf_op jit(solution)/shard_map/ppermute | solution.py:269
  120.1 13.6 %collective-permute-start.4 = (bf16[1,128,256]{2,1,0:T(8,128)(2,1)S(1)}, bf16[1,128,256]{2,1,0:T(8,128)(2,1)S(1)}, u32[]{:S(2)}, u32[]{:S(2)}) collective-permute-start(bf16[1,128,256]{2,1,0:T(8,128)(2,1)S(1)} %slice.23), channel_id=1, source_target_pairs={{0,8},{2,10},{4,12},{6,14},{8,0},{10,2},{12,4},{14,6},{1,9},{3,11}... | collective-permute-start | bytes 196616 | tf_op jit(solution)/shard_map/ppermute | solution.py:244
  123.5 22.6 %collective-permute-start.5 = (bf16[8,128,128]{2,1,0:T(8,128)(2,1)S(1)}, bf16[8,128,128]{2,1,0:T(8,128)(2,1)S(1)}, u32[]{:S(2)}, u32[]{:S(2)}) collective-permute-start(bf16[8,128,128]{2,1,0:T(8,128)(2,1)S(1)} %all_to_all.21.refs_0_), channel_id=1, source_target_pairs={{0,640},{1,81},{2,642},{3,83},{4,644},{5,85},{6,646},{7,87},{8,648... | collective-permute-start | bytes 786440 | tf_op jit(solution)/shard_map/ppermute | solution.py:269
  129.6 16.4 %collective-permute-start.6 = (bf16[8,128,128]{2,1,0:T(8,128)(2,1)S(1)}, bf16[8,128,128]{2,1,0:T(8,128)(2,1)S(1)}, u32[]{:S(2)}, u32[]{:S(2)}) collective-permute-start(bf16[8,128,128]{2,1,0:T(8,128)(2,1)S(1)} %all_to_all.21.refs_0_), channel_id=1, source_target_pairs={{0,256},{1,33},{2,258},{3,35},{4,260},{5,37},{6,262},{7,39},{8,264... | collective-permute-start | bytes 786440 | tf_op jit(solution)/shard_map/ppermute | solution.py:269
  133.6 14.7 %collective-permute-start.7 = (bf16[8,128,128]{2,1,0:T(8,128)(2,1)S(1)}, bf16[8,128,128]{2,1,0:T(8,128)(2,1)S(1)}, u32[]{:S(2)}, u32[]{:S(2)}) collective-permute-start(bf16[8,128,128]{2,1,0:T(8,128)(2,1)S(1)} %all_to_all.21.refs_0_), channel_id=1, source_target_pairs={{0,768},{1,97},{2,770},{3,99},{4,772},{5,101},{6,774},{7,103},{8,7... | collective-permute-start | bytes 786440 | tf_op jit(solution)/shard_map/ppermute | solution.py:269
  137.6 10.7 %collective-permute-start.8 = (bf16[8,128,128]{2,1,0:T(8,128)(2,1)S(1)}, bf16[8,128,128]{2,1,0:T(8,128)(2,1)S(1)}, u32[]{:S(2)}, u32[]{:S(2)}) collective-permute-start(bf16[8,128,128]{2,1,0:T(8,128)(2,1)S(1)} %all_to_all.21.refs_0_), channel_id=1, source_target_pairs={{0,128},{1,17},{2,130},{3,19},{4,132},{5,21},{6,134},{7,23},{8,136... | collective-permute-start | bytes 786440 | tf_op jit(solution)/shard_map/ppermute | solution.py:269
  141.0 10.0 %collective-permute-start.9 = (bf16[8,128,128]{2,1,0:T(8,128)(2,1)S(1)}, bf16[8,128,128]{2,1,0:T(8,128)(2,1)S(1)}, u32[]{:S(2)}, u32[]{:S(2)}) collective-permute-start(bf16[8,128,128]{2,1,0:T(8,128)(2,1)S(1)} %all_to_all.21.refs_0_), channel_id=1, source_target_pairs={{0,896},{1,113},{2,898},{3,115},{4,900},{5,117},{6,902},{7,119},{8... | collective-permute-start | bytes 786440 | tf_op jit(solution)/shard_map/ppermute | solution.py:269

commit v7 on v4

--- a/solution.py
+++ b/solution.py
@@ -188,8 +188,10 @@
         [pltpu.VMEM((rows, width), BF)],
         flops=2 * tokens * rows * width,
         nbytes=4 * 2**20,
+        limit=60,
     )(place, block_pos, owner_rank, hidden, blocks)
-    own, keep, send = lax.optimization_barrier((own, keep, send))
+    swapped = lax.ppermute(send, "core", swap)
+    own, keep, swapped = lax.optimization_barrier((own, keep, swapped))
     other = lax.ppermute(own, "core", swap)
     grads = call(
         functools.partial(grads_kernel, n0, factor),
@@ -206,7 +208,7 @@
         nbytes=4 * 2**20,
         limit=12,
     )(place, block_pos, owner_rank, hid_t, own, other)
-    grads, keep, send = lax.optimization_barrier((grads, keep, send))
+    grads, keep, swapped = lax.optimization_barrier((grads, keep, swapped))
     hidden_grad = call(
         back_kernel,
         jax.ShapeDtypeStruct((tokens, rows), BF),
@@ -225,7 +227,7 @@
         return (value[:half].astype(F32) + theirs.astype(F32)).astype(BF), beside
 
     got = exchange(grads.reshape(n0, slots // n0, bs, bs), first)
-    total = (keep.astype(F32) + lax.ppermute(send, "core", swap).astype(F32)).astype(BF)
+    total = (keep.astype(F32) + swapped.astype(F32)).astype(BF)
     total, hidden_grad = halved(total, 1, hidden_grad)
     part = got.astype(F32).sum(axis=0).astype(BF)
     part, total = lax.optimization_barrier((part, total))

time: 153 us -> 154 us (level)
  local copies, waits for them, and re-layouts: 9.01 us -> 4.52 us
  waiting for transfers between devices: 47.6 us -> 50.1 us
  Pallas kernels: 15.1 us -> 17.2 us
    all_to_all x2, waiting for transfers between devices: 24.9 us -> 30.6 us  [exchange(): lax.all_to_all(value, axes, 0, 0, axis_index_groups=groups, tiled=True)]
    unnamed x22 -> x16, local copies, waits for them, and re-layouts: 5.45 us -> 0.96 us
    pallas_call x1, Pallas kernels: 3.56 us -> 5.69 us  [shards(): call(partial_kernel, (*(jax.ShapeDtypeStruct((nx, tokens, feats), BF),) *...]
    ppermute x3, waiting for transfers between devices: 15.9 us -> 13.9 us  [halved(): theirs = lax.ppermute(value[half:], 'x', [(i, i ^ step) for i in range(nx)])]
  transfers between devices with their start and end apart: 8 -> 8, of which waited for: 8 -> 7; matrix products, arithmetic and copies ran while one was open for 2% -> 2% of each run, Pallas kernels for 6% -> 7%
where the time goes in v7:
time: 154 us; the launch traced here: 153 us
  waiting for transfers between devices  50.1 us (33%)
  starting transfers between devices  44.1 us (29%)
  blocking collectives  30.9 us (20%)
  Pallas kernels  17.2 us (11%)
  other arithmetic  5.41 us (4%)
  local copies, waits for them, and re-layouts  4.52 us (3%)
    all_to_all x2, blocking collectives, exchange(): lax.all_to_all(value, axes, 0, 0, axis_index_groups=groups, tiled=True)  30.9 us
    all_to_all x2, waiting for transfers between devices, exchange(): lax.all_to_all(value, axes, 0, 0, axis_index_groups=groups, tiled=True)  30.6 us
    all_to_all x1, starting transfers between devices, shards(): lax.all_to_all(jnp.broadcast_to(cotangent, (nx, tokens, feats)), 'x', 0,...  17.8 us
    all_to_all x2, starting transfers between devices, exchange(): lax.all_to_all(value, axes, 0, 0, axis_index_groups=groups, tiled=True)  14.2 us
    ppermute x3, waiting for transfers between devices, halved(): theirs = lax.ppermute(value[half:], 'x', [(i, i ^ step) for i in range(nx)])  13.9 us
    ppermute x3, starting transfers between devices, halved(): theirs = lax.ppermute(value[half:], 'x', [(i, i ^ step) for i in range(nx)])  8.17 us
    pallas_call x1, Pallas kernels, shards(): call(partial_kernel, (*(jax.ShapeDtypeStruct((nx, tokens, feats), BF),) *...  5.69 us
    pallas_call x1, Pallas kernels, shards(): call(back_kernel, jax.ShapeDtypeStruct((tokens, rows), BF), [SMEM, SMEM,...  4.9 us
  transfers between devices with their start and end apart: 8, of which 7 were waited for; matrix products, arithmetic and copies ran while one was open for 2% of the time, Pallas kernels for 7%

profile of v7, /device:TPU:2, one launch (start us, length us, event | category | flops | bytes accessed | tf_op | source)
XLA Modules:
  0.0 153.1 jit_solution(17854082172827201409)
XLA Ops:
  0.6 1.7 %broadcast_in_dim.12 = bf16[8,128,256]{2,1,0:T(8,128)(2,1)} broadcast(bf16[128,256]{1,0:T(8,128)(2,1)} %param.8), dimensions={1,2} | broadcast | bytes 589824 | tf_op jit(solution)/shard_map/broadcast_in_dim | solution.py:182
  2.3 0.0 copy-start.3
  2.3 0.0 copy-start.4
  2.3 17.8 %all-to-all-start = ((bf16[8,128,256]{2,1,0:T(8,128)(2,1)}), bf16[8,128,256]{2,1,0:T(8,128)(2,1)S(1)}, u32[]{:S(2)}, u32[]{:S(2)}) async-start(bf16[8,128,256]{2,1,0:T(8,128)(2,1)} %broadcast_in_dim.12), calls=%async_computation | async-start | bytes 1048576 | tf_op jit(solution)/shard_map/all_to_all | solution.py:182
  20.1 0.6 pad_add_fusion.place_ref
  20.7 0.0 copy-start.2
  20.7 5.7 %shard_map.118 = (bf16[8,128,256]{2,1,0:T(8,128)(2,1)}, bf16[8,128,256]{2,1,0:T(8,128)(2,1)}, bf16[128,128]{1,0:T(8,128)(2,1)}, bf16[768,128]{1,0:T(8,128)(2,1)}) custom-call(s32[3]{0:T(128)} %pad_add_fusion.place_ref, s32[1,64]{1,0:T(1,128)} %pos_ref.5, s32[1,64]{1,0:T(1,128)} %rank_ref.5, bf16[128,768]{1,0:T(8,128)(2,1)} %hid_ref.1, ...), custom_call_target="tpu_custom_call" | custom-call | flops 805306368 | bytes 4194304 | tf_op jit(solution)/shard_map/pallas_call | solution.py:183
  26.4 1.9 %collective-permute-start = (bf16[8,128,256]{2,1,0:T(8,128)(2,1)}, bf16[8,128,256]{2,1,0:T(8,128)(2,1)}, u32[]{:S(2)}, u32[]{:S(2)}) collective-permute-start(bf16[8,128,256]{2,1,0:T(8,128)(2,1)} %get-tuple-element.22), channel_id=1, source_target_pairs={{0,1},{1,0},{2,3},{3,2},{4,5},{5,4},{6,7},{7,6},{8,9},{9,8},{10,11... | collective-permute-start | bytes 1572872 | tf_op jit(solution)/shard_map/ppermute | solution.py:193
  28.3 2.2 %collective-permute-done = bf16[8,128,256]{2,1,0:T(8,128)(2,1)} collective-permute-done((bf16[8,128,256]{2,1,0:T(8,128)(2,1)}, bf16[8,128,256]{2,1,0:T(8,128)(2,1)}, u32[]{:S(2)}, u32[]{:S(2)}) %collective-permute-start) | collective-permute-done | bytes 524320 | tf_op jit(solution)/shard_map/ppermute | solution.py:193
  30.6 1.4 all-to-all-done.own_ref
  32.0 1.9 %collective-permute-start.1 = (bf16[8,128,256]{2,1,0:T(8,128)(2,1)S(1)}, bf16[8,128,256]{2,1,0:T(8,128)(2,1)S(1)}, u32[]{:S(2)}, u32[]{:S(2)}) collective-permute-start(bf16[8,128,256]{2,1,0:T(8,128)(2,1)S(1)} %all-to-all-done.own_ref), channel_id=1, source_target_pairs={{0,1},{1,0},{2,3},{3,2},{4,5},{5,4},{6,7},{7,6},{8,9},{9,8},{10,11... | collective-permute-start | bytes 1572872 | tf_op jit(solution)/shard_map/ppermute | solution.py:195
  33.9 1.9 %collective-permute-done.1.other_ref = bf16[8,128,256]{2,1,0:T(8,128)(2,1)S(1)} collective-permute-done((bf16[8,128,256]{2,1,0:T(8,128)(2,1)S(1)}, bf16[8,128,256]{2,1,0:T(8,128)(2,1)S(1)}, u32[]{:S(2)}, u32[]{:S(2)}) %collective-permute-start.1) | collective-permute-done | bytes 524320 | tf_op jit(solution)/shard_map/ppermute | solution.py:195
  35.8 0.0 copy-done.3
  35.8 0.0 copy-done.4
  35.8 0.0 copy-done.2
  35.8 0.0 copy-start.1
  35.8 0.9 copy-done.1
  36.7 4.2 %shard_map.119 = bf16[64,128,128]{2,1,0:T(8,128)(2,1)} custom-call(s32[3]{0:T(128)S(1)} %copy-done.2, s32[1,64]{1,0:T(1,128)S(1)} %copy-done.3, s32[1,64]{1,0:T(1,128)S(1)} %copy-done.4, bf16[768,128]{1,0:T(8,128)(2,1)S(1)} %copy-done.1, bf16[8,128,256]{2,1,0:T(8,128)(2,1)S(1)} %all-to-all-done.own_ref, bf16[8,128,256]{2,1,0:T(8,128)(2,1)S(1)} %collective-permute-done.1.other_ref), custom_call_target="tpu_custom_call" | custom-call | flops 268435456 | bytes 4194304 | tf_op jit(solution)/shard_map/pallas_call | solution.py:196
  40.9 0.0 copy-start
  41.0 10.6 %all-to-all-start.1 = ((bf16[8,8,128,128]{3,2,1,0:T(8,128)(2,1)}), bf16[8,8,128,128]{3,2,1,0:T(8,128)(2,1)}, u32[]{:S(2)}, u32[]{:S(2)}) async-start(bf16[8,8,128,128]{3,2,1,0:T(8,128)(2,1)} %bitcast.3), calls=%async_computation.1 | async-start | bytes 4194304 | tf_op jit(solution)/shard_map/all_to_all | solution.py:180
  51.6 1.3 add_convert_fusion
  52.9 3.4 %collective-permute-start.2 = (bf16[4,128,256]{2,1,0:T(8,128)(2,1)S(1)}, bf16[4,128,256]{2,1,0:T(8,128)(2,1)S(1)}, u32[]{:S(2)}, u32[]{:S(2)}) collective-permute-start(bf16[4,128,256]{2,1,0:T(8,128)(2,1)S(1)} %slice.25), channel_id=1, source_target_pairs={{0,2},{2,0},{4,6},{6,4},{8,10},{10,8},{12,14},{14,12},{1,3},{3,1},... | collective-permute-start | bytes 786440 | tf_op jit(solution)/shard_map/ppermute | solution.py:225
  56.3 0.0 copy-done
  56.3 4.9 %shard_map.120 = bf16[128,768]{1,0:T(8,128)(2,1)} custom-call(s32[3]{0:T(128)S(1)} %copy-done.2, s32[1,64]{1,0:T(1,128)S(1)} %copy-done.3, bf16[64,128,128]{2,1,0:T(8,128)(2,1)S(1)} %copy-done, bf16[8,128,256]{2,1,0:T(8,128)(2,1)S(1)} %all-to-all-done.own_ref, bf16[8,128,256]{2,1,0:T(8,128)(2,1)S(1)} %collective-permute-done.1.other_ref), custom_call_target="tpu_custom_call" | custom-call | flops 805306368 | bytes 4194304 | tf_op jit(solution)/shard_map/pallas_call | solution.py:212
  61.3 0.0 copy-start.5
  61.3 0.0 copy-start.6
  61.3 0.0 copy-start.7
  61.3 0.0 collective-permute-done.2
  61.3 0.1 add_convert_fusion.1
  61.4 20.6 %all-to-all-done.1 = bf16[8,8,128,128]{3,2,1,0:T(8,128)(2,1)} async-done(((bf16[8,8,128,128]{3,2,1,0:T(8,128)(2,1)}), bf16[8,8,128,128]{3,2,1,0:T(8,128)(2,1)}, u32[]{:S(2)}, u32[]{:S(2)}) %all-to-all-start.1) | async-done | bytes 2097184 | tf_op jit(solution)/shard_map/all_to_all | solution.py:180
  82.0 2.0 %reduce_sum.23 = bf16[8,128,128]{2,1,0:T(8,128)(2,1)S(1)} reduce(bf16[8,8,128,128]{3,2,1,0:T(8,128)(2,1)} %all-to-all-done.1, bf16[]{:T(256)} %constant.11.clone.1), dimensions={0}, to_apply=%region_0.0 | reduce | flops 917504 | bytes 2359298 | tf_op jit(solution)/shard_map/reduce_sum | solution.py:232
  83.9 18.0 %all_to_all.25 = bf16[8,128,128]{2,1,0:T(8,128)(2,1)S(1)} all-to-all(bf16[8,128,128]{2,1,0:T(8,128)(2,1)S(1)} %reduce_sum.23), channel_id=1, replica_groups={{0,16,32,48,64,80,96,112},{2,18,34,50,66,82,98,114},{4,20,36,52,68,84,1..., dimensions={0} | all-to-all | bytes 524288 | tf_op jit(solution)/shard_map/all_to_all | solution.py:180
  102.0 0.0 copy-done.5
  102.0 0.0 copy-done.6
  102.0 0.0 copy-done.7
  102.0 0.1 fusion.2
  102.1 12.9 %all_to_all.26 = bf16[8,128,128]{2,1,0:T(8,128)(2,1)S(1)} all-to-all(bf16[8,128,128]{2,1,0:T(8,128)(2,1)S(1)} %broadcast_in_dim.13), channel_id=1, replica_groups={{0,16,32,48,64,80,96,112},{2,18,34,50,66,82,98,114},{4,20,36,52,68,84,1..., dimensions={0} | all-to-all | bytes 524288 | tf_op jit(solution)/shard_map/all_to_all | solution.py:180
  115.0 1.8 %broadcast_in_dim.14 = bf16[8,8,128,128]{3,2,1,0:T(8,128)(2,1)} broadcast(bf16[8,128,128]{2,1,0:T(8,128)(2,1)S(1)} %all_to_all.26), dimensions={1,2,3} | broadcast | bytes 2359296 | tf_op jit(solution)/shard_map/broadcast_in_dim | solution.py:246
  116.8 3.6 %all-to-all-start.4 = ((bf16[8,8,128,128]{3,2,1,0:T(8,128)(2,1)}), bf16[8,8,128,128]{3,2,1,0:T(8,128)(2,1)S(1)}, u32[]{:S(2)}, u32[]{:S(2)}) async-start(bf16[8,8,128,128]{3,2,1,0:T(8,128)(2,1)} %broadcast_in_dim.14), calls=%async_computation.4 | async-start | bytes 4194304 | tf_op jit(solution)/shard_map/all_to_all | solution.py:180
  120.5 1.9 %collective-permute-start.3 = (bf16[2,128,256]{2,1,0:T(8,128)(2,1)S(1)}, bf16[2,128,256]{2,1,0:T(8,128)(2,1)S(1)}, u32[]{:S(2)}, u32[]{:S(2)}) collective-permute-start(bf16[2,128,256]{2,1,0:T(8,128)(2,1)S(1)} %slice.21), channel_id=1, source_target_pairs={{0,4},{2,6},{4,0},{6,2},{8,12},{10,14},{12,8},{14,10},{1,5},{3,7},... | collective-permute-start | bytes 393224 | tf_op jit(solution)/shard_map/ppermute | solution.py:225
  122.4 6.4 %collective-permute-done.3 = bf16[2,128,256]{2,1,0:T(8,128)(2,1)S(1)} collective-permute-done((bf16[2,128,256]{2,1,0:T(8,128)(2,1)S(1)}, bf16[2,128,256]{2,1,0:T(8,128)(2,1)S(1)}, u32[]{:S(2)}, u32[]{:S(2)}) %collective-permute-start.3) | collective-permute-done | bytes 131104 | tf_op jit(solution)/shard_map/ppermute | solution.py:225
  128.9 2.9 %collective-permute-start.4 = (bf16[1,128,256]{2,1,0:T(8,128)(2,1)S(1)}, bf16[1,128,256]{2,1,0:T(8,128)(2,1)S(1)}, u32[]{:S(2)}, u32[]{:S(2)}) collective-permute-start(bf16[1,128,256]{2,1,0:T(8,128)(2,1)S(1)} %slice.27), channel_id=1, source_target_pairs={{0,8},{2,10},{4,12},{6,14},{8,0},{10,2},{12,4},{14,6},{1,9},{3,11}... | collective-permute-start | bytes 196616 | tf_op jit(solution)/shard_map/ppermute | solution.py:225
  131.8 7.5 %collective-permute-done.4 = bf16[1,128,256]{2,1,0:T(8,128)(2,1)S(1)} collective-permute-done((bf16[1,128,256]{2,1,0:T(8,128)(2,1)S(1)}, bf16[1,128,256]{2,1,0:T(8,128)(2,1)S(1)}, u32[]{:S(2)}, u32[]{:S(2)}) %collective-permute-start.4) | collective-permute-done | bytes 65568 | tf_op jit(solution)/shard_map/ppermute | solution.py:225
  139.3 0.6 fusion.8
  139.9 0.7 add_divide_fusion
  140.6 10.0 %all-to-all-done.4 = bf16[8,8,128,128]{3,2,1,0:T(8,128)(2,1)S(1)} async-done(((bf16[8,8,128,128]{3,2,1,0:T(8,128)(2,1)}), bf16[8,8,128,128]{3,2,1,0:T(8,128)(2,1)S(1)}, u32[]{:S(2)}, u32[]{:S(2)}) %all-to-all-start.4) | async-done | bytes 2097184 | tf_op jit(solution)/shard_map/all_to_all | solution.py:180
  150.6 2.4 %shard_map.121 = bf16[64,128,128]{2,1,0:T(8,128)(2,1)} custom-call(s32[3]{0:T(128)S(1)} %copy-done.2, s32[1,64]{1,0:T(1,128)S(1)} %copy-done.4, bf16[64,128,128]{2,1,0:T(8,128)(2,1)S(1)} %bitcast.20), custom_call_target="tpu_custom_call" | custom-call | bytes 4194304 | tf_op jit(solution)/shard_map/pallas_call | solution.py:247
  (6 shorter events, 0.1 us)
Async XLA Ops:
  2.3 33.5 %copy-start.3 = (s32[1,64]{1,0:T(1,128)S(1)}, s32[1,64]{1,0:T(1,128)}, u32[]{:S(2)}) copy-start(s32[1,64]{1,0:T(1,128)} %pos_ref.5) | copy-start | bytes 772
  2.3 33.5 %copy-start.4 = (s32[1,64]{1,0:T(1,128)S(1)}, s32[1,64]{1,0:T(1,128)}, u32[]{:S(2)}) copy-start(s32[1,64]{1,0:T(1,128)} %rank_ref.5) | copy-start | bytes 772
  2.3 29.7 %all-to-all-start = ((bf16[8,128,256]{2,1,0:T(8,128)(2,1)}), bf16[8,128,256]{2,1,0:T(8,128)(2,1)S(1)}, u32[]{:S(2)}, u32[]{:S(2)}) async-start(bf16[8,128,256]{2,1,0:T(8,128)(2,1)} %broadcast_in_dim.12), calls=%async_computation | async-start | bytes 1048576 | tf_op jit(solution)/shard_map/all_to_all | solution.py:182
  20.7 15.1 %copy-start.2 = (s32[3]{0:T(128)S(1)}, s32[3]{0:T(128)}, u32[]{:S(2)}) copy-start(s32[3]{0:T(128)} %pad_add_fusion.place_ref) | copy-start | bytes 40
  26.4 4.1 %collective-permute-start = (bf16[8,128,256]{2,1,0:T(8,128)(2,1)}, bf16[8,128,256]{2,1,0:T(8,128)(2,1)}, u32[]{:S(2)}, u32[]{:S(2)}) collective-permute-start(bf16[8,128,256]{2,1,0:T(8,128)(2,1)} %get-tuple-element.22), channel_id=1, source_target_pairs={{0,1},{1,0},{2,3},{3,2},{4,5},{5,4},{6,7},{7,6},{8,9},{9,8},{10,11... | collective-permute-start | bytes 1572872 | tf_op jit(solution)/shard_map/ppermute | solution.py:193
  32.0 3.8 %collective-permute-start.1 = (bf16[8,128,256]{2,1,0:T(8,128)(2,1)S(1)}, bf16[8,128,256]{2,1,0:T(8,128)(2,1)S(1)}, u32[]{:S(2)}, u32[]{:S(2)}) collective-permute-start(bf16[8,128,256]{2,1,0:T(8,128)(2,1)S(1)} %all-to-all-done.own_ref), channel_id=1, source_target_pairs={{0,1},{1,0},{2,3},{3,2},{4,5},{5,4},{6,7},{7,6},{8,9},{9,8},{10,11... | collective-permute-start | bytes 1572872 | tf_op jit(solution)/shard_map/ppermute | solution.py:195
  35.8 0.9 copy-start.1
  40.9 15.4 %copy-start = (bf16[64,128,128]{2,1,0:T(8,128)(2,1)S(1)}, bf16[64,128,128]{2,1,0:T(8,128)(2,1)}, u32[]{:S(2)}) copy-start(bf16[64,128,128]{2,1,0:T(8,128)(2,1)} %blocks_ref.3) | copy-start | bytes 6291460
  41.0 41.0 %all-to-all-start.1 = ((bf16[8,8,128,128]{3,2,1,0:T(8,128)(2,1)}), bf16[8,8,128,128]{3,2,1,0:T(8,128)(2,1)}, u32[]{:S(2)}, u32[]{:S(2)}) async-start(bf16[8,8,128,128]{3,2,1,0:T(8,128)(2,1)} %bitcast.3), calls=%async_computation.1 | async-start | bytes 4194304 | tf_op jit(solution)/shard_map/all_to_all | solution.py:180
  52.9 8.4 %collective-permute-start.2 = (bf16[4,128,256]{2,1,0:T(8,128)(2,1)S(1)}, bf16[4,128,256]{2,1,0:T(8,128)(2,1)S(1)}, u32[]{:S(2)}, u32[]{:S(2)}) collective-permute-start(bf16[4,128,256]{2,1,0:T(8,128)(2,1)S(1)} %slice.25), channel_id=1, source_target_pairs={{0,2},{2,0},{4,6},{6,4},{8,10},{10,8},{12,14},{14,12},{1,3},{3,1},... | collective-permute-start | bytes 786440 | tf_op jit(solution)/shard_map/ppermute | solution.py:225
  61.3 40.7 %copy-start.5 = (f32[1,1,128,128]{3,2,1,0:T(8,128)S(1)}, f32[1,1,128,128]{3,2,1,0:T(8,128)}, u32[]{:S(2)}) copy-start(f32[1,1,128,128]{3,2,1,0:T(8,128)} %param.13) | copy-start | bytes 196612
  61.3 40.7 %copy-start.6 = (f32[1,1,128,128]{3,2,1,0:T(8,128)S(1)}, f32[1,1,128,128]{3,2,1,0:T(8,128)}, u32[]{:S(2)}) copy-start(f32[1,1,128,128]{3,2,1,0:T(8,128)} %param.12) | copy-start | bytes 196612
  61.3 40.7 %copy-start.7 = (bf16[128,128]{1,0:T(8,128)(2,1)S(1)}, bf16[128,128]{1,0:T(8,128)(2,1)}, u32[]{:S(2)}) copy-start(bf16[128,128]{1,0:T(8,128)(2,1)} %get-tuple-element.33) | copy-start | bytes 98308
  116.8 33.8 %all-to-all-start.4 = ((bf16[8,8,128,128]{3,2,1,0:T(8,128)(2,1)}), bf16[8,8,128,128]{3,2,1,0:T(8,128)(2,1)S(1)}, u32[]{:S(2)}, u32[]{:S(2)}) async-start(bf16[8,8,128,128]{3,2,1,0:T(8,128)(2,1)} %broadcast_in_dim.14), calls=%async_computation.4 | async-start | bytes 4194304 | tf_op jit(solution)/shard_map/all_to_all | solution.py:180
  120.5 8.4 %collective-permute-start.3 = (bf16[2,128,256]{2,1,0:T(8,128)(2,1)S(1)}, bf16[2,128,256]{2,1,0:T(8,128)(2,1)S(1)}, u32[]{:S(2)}, u32[]{:S(2)}) collective-permute-start(bf16[2,128,256]{2,1,0:T(8,128)(2,1)S(1)} %slice.21), channel_id=1, source_target_pairs={{0,4},{2,6},{4,0},{6,2},{8,12},{10,14},{12,8},{14,10},{1,5},{3,7},... | collective-permute-start | bytes 393224 | tf_op jit(solution)/shard_map/ppermute | solution.py:225
  128.9 10.4 %collective-permute-start.4 = (bf16[1,128,256]{2,1,0:T(8,128)(2,1)S(1)}, bf16[1,128,256]{2,1,0:T(8,128)(2,1)S(1)}, u32[]{:S(2)}, u32[]{:S(2)}) collective-permute-start(bf16[1,128,256]{2,1,0:T(8,128)(2,1)S(1)} %slice.27), channel_id=1, source_target_pairs={{0,8},{2,10},{4,12},{6,14},{8,0},{10,2},{12,4},{14,6},{1,9},{3,11}... | collective-permute-start | bytes 196616 | tf_op jit(solution)/shard_map/ppermute | solution.py:225
